TPU v7x, 32 devices: a whole 2x2x4 slice. The times are simulated.
32 devices in a mesh: dp: 8 (over y, x, core), mp: 4 (over z).
Axes of the slice: x: 2, y: 2, z: 4, core: 2. Of those that a mesh axis runs over, the one named last changes fastest.
Arguments:
- tokens: bfloat16 [8192, 2048], P(('dp', 'mp')), may hold values from -6 to 6
- cotangent: bfloat16 [8192, 2048], P(('dp', 'mp')), may hold values from -6 to 6
- valid_counts: int32 [8], P('dp'), may hold values from 1 to 1024, 7168 in all
- w_qkv: float32 [2048, 3, 2048], P('dp', None, 'mp'), may hold values from -0.1875 to 0.1875
- w_out: float32 [2048, 2048], P('mp', 'dp'), may hold values from -0.1875 to 0.1875
- w_gu: float32 [2048, 2, 8192], P('dp', None, 'mp'), may hold values from -0.125 to 0.125
- w_down: float32 [8192, 2048], P('mp', 'dp'), may hold values from -0.0625 to 0.0625
- gains: float32 [2, 2048], P(None, ('dp', 'mp')), may hold values from 0.5 to 1.5
- mom_qkv: float32 [2048, 3, 2048], P('dp', None, 'mp'), may hold values from -28 to 28
- mom_out: float32 [2048, 2048], P('mp', 'dp'), may hold values from -28 to 28
- mom_gu: float32 [2048, 2, 8192], P('dp', None, 'mp'), may hold values from -16 to 16
- mom_down: float32 [8192, 2048], P('mp', 'dp'), may hold values from -28 to 28
- mom_gains: float32 [2, 2048], P(None, ('dp', 'mp')), may hold values from -28 to 28
- avg_qkv: float32 [2048, 3, 2048], P('dp', None, 'mp'), may hold values from -0.1875 to 0.1875
- avg_out: float32 [2048, 2048], P('mp', 'dp'), may hold values from -0.1875 to 0.1875
- avg_gu: float32 [2048, 2, 8192], P('dp', None, 'mp'), may hold values from -0.125 to 0.125
- avg_down: float32 [8192, 2048], P('mp', 'dp'), may hold values from -0.0625 to 0.0625
- avg_gains: float32 [2, 2048], P(None, ('dp', 'mp')), may hold values from 0.5 to 1.5
Outputs:
- block_out: bfloat16 [8192, 2048], P(('dp', 'mp'))
- input_grad: float32 [8192, 2048], P(('dp', 'mp'))
- new_qkv: float32 [2048, 3, 2048], P('dp', None, 'mp')
- new_out: float32 [2048, 2048], P('mp', 'dp')
- new_gu: float32 [2048, 2, 8192], P('dp', None, 'mp')
- new_down: float32 [8192, 2048], P('mp', 'dp')
- new_gains: float32 [2, 2048], P(None, ('dp', 'mp'))
- next_mom_qkv: float32 [2048, 3, 2048], P('dp', None, 'mp')
- next_mom_out: float32 [2048, 2048], P('mp', 'dp')
- next_mom_gu: float32 [2048, 2, 8192], P('dp', None, 'mp')
- next_mom_down: float32 [8192, 2048], P('mp', 'dp')
- next_mom_gains: float32 [2, 2048], P(None, ('dp', 'mp'))
- next_avg_qkv: float32 [2048, 3, 2048], P('dp', None, 'mp')
- next_avg_out: float32 [2048, 2048], P('mp', 'dp')
- next_avg_gu: float32 [2048, 2, 8192], P('dp', None, 'mp')
- next_avg_down: float32 [8192, 2048], P('mp', 'dp')
- next_avg_gains: float32 [2, 2048], P(None, ('dp', 'mp'))
- copy_qkv: bfloat16 [2048, 3, 2048], P('dp', None, 'mp')
- copy_out: bfloat16 [2048, 2048], P('mp', 'dp')
- copy_gu: bfloat16 [2048, 2, 8192], P('dp', None, 'mp')
- copy_down: bfloat16 [8192, 2048], P('mp', 'dp')
Inputs may be any that keep to these rules, and one draw needn't show every extreme that they name: `valid_counts`: each slot's valid tokens are its first rows; the counts sum to 7168 and the largest equals 1024.
All inputs are finite; a program needn't handle non-finite values. No bound on the sum of `valid_counts` on one device may be relied on, other than what follows from the above.
Results may differ from a plain program's by a relative error of at most 0.017.
Values may be sent and summed in bfloat16 or wider, within the bound.
A program may use at most 256 MiB of HBM per device.

v0:
```python
import math

import jax
import jax.numpy as jnp
from jax import lax
from jax.sharding import PartitionSpec as P

HDIM = 128
SEQ = 1024


norm_eps = 1e-05
rope_base = 10000.0
momentum_decay = 0.9
average_decay = 0.9
step_rate = 0.05
gain_rate = 0.5


def rope_tables(length, half_dim):
    positions = jnp.arange(length, dtype=jnp.float32)[:, None]
    inverse_freq = rope_base ** (-jnp.arange(half_dim, dtype=jnp.float32) / half_dim)
    angles = positions * inverse_freq[None, :]
    return (jnp.cos(angles)[:, None, :], jnp.sin(angles)[:, None, :])


def rotate(values, cosine, sine_tab):
    half_dim = values.shape[-1] // 2
    first, second = (values[..., :half_dim], values[..., half_dim:])
    return jnp.concatenate(
        [first * cosine - second * sine_tab, second * cosine + first * sine_tab], axis=-1
    )


def unrotate(gradient, cosine, sine_tab):
    half_dim = gradient.shape[-1] // 2
    first, second = (gradient[..., :half_dim], gradient[..., half_dim:])
    return jnp.concatenate(
        [first * cosine + second * sine_tab, second * cosine - first * sine_tab], axis=-1
    )


def norm_forward(row_vals, gain_row):
    inverse = lax.rsqrt(jnp.mean(row_vals * row_vals, axis=1, keepdims=True) + norm_eps)
    unit_rows = row_vals * inverse
    return (unit_rows, inverse, unit_rows * gain_row[None, :])


def norm_backward(gradient, unit_rows, inverse, gain_row):
    scaled = gradient * gain_row[None, :]
    inner = jnp.mean(scaled * unit_rows, axis=1, keepdims=True)
    return (inverse * (scaled - unit_rows * inner), jnp.sum(gradient * unit_rows, axis=0))


def update(weight, moment, average, gradient, step_size):
    moment_new = momentum_decay * moment + (1.0 - momentum_decay) * gradient
    weight_new = weight - step_size * (
        (1.0 - momentum_decay) * gradient + momentum_decay * moment_new
    )
    average_new = average_decay * average + (1.0 - average_decay) * weight_new
    return (weight_new, moment_new, average_new)


def per_device(
    tokens,
    cotangent,
    valid_counts,
    w_qkv,
    w_out,
    w_gu,
    w_down,
    gains,
    mom_qkv,
    mom_out,
    mom_gu,
    mom_down,
    mom_gains,
    avg_qkv,
    avg_out,
    avg_gu,
    avg_down,
    avg_gains,
):
    row_count = tokens.shape[0]
    local_width = w_qkv.shape[2]
    heads_here = local_width // HDIM
    block_len = min(512, SEQ)
    block_total = SEQ // block_len
    score_scale = 1.0 / math.sqrt(HDIM)
    score_shift = -math.log(SEQ)
    valid_len = valid_counts[0]
    qkv_w, out_w, gu_w, down_w = (
        lax.all_gather(w_qkv.astype(jnp.bfloat16), "dp", axis=0, tiled=True),
        lax.all_gather(w_out.astype(jnp.bfloat16), "dp", axis=1, tiled=True),
        lax.all_gather(w_gu.astype(jnp.bfloat16), "dp", axis=0, tiled=True),
        lax.all_gather(w_down.astype(jnp.bfloat16), "dp", axis=1, tiled=True),
    )
    gain_all = lax.all_gather(gains, ("dp", "mp"), axis=1, tiled=True)
    row_ids = lax.axis_index("mp") * row_count + jnp.arange(row_count, dtype=jnp.int32)
    live_rows = (row_ids < valid_len).astype(jnp.float32)[:, None]
    xin = tokens.astype(jnp.float32)
    unit_first, inv_first, normed_first = norm_forward(xin, gain_all[0])
    h_first = lax.all_gather(normed_first.astype(jnp.bfloat16), "mp", axis=0, tiled=True)
    joined = jnp.einsum("td,dcn->tcn", h_first, qkv_w, preferred_element_type=jnp.float32)
    cosine, sine_tab = rope_tables(SEQ, HDIM // 2)
    queries = rotate(joined[:, 0].reshape(SEQ, heads_here, HDIM), cosine, sine_tab).astype(
        jnp.bfloat16
    )
    keys = rotate(joined[:, 1].reshape(SEQ, heads_here, HDIM), cosine, sine_tab).astype(
        jnp.bfloat16
    )
    values = joined[:, 2].reshape(SEQ, heads_here, HDIM).astype(jnp.bfloat16)
    key_pos = jnp.arange(SEQ, dtype=jnp.int32)

    def probabilities(query_blk, offset):
        raw = jnp.einsum("qhd,khd->hqk", query_blk, keys, preferred_element_type=jnp.float32)
        query_pos = offset + jnp.arange(block_len, dtype=jnp.int32)
        allowed = (key_pos[None, :] <= query_pos[:, None]) & (key_pos[None, :] < valid_len)
        return jax.nn.sigmoid(raw * score_scale + score_shift) * allowed.astype(jnp.float32)[None]

    def attend(block_idx):
        offset = block_idx * block_len
        query_blk = lax.dynamic_slice_in_dim(queries, offset, block_len, 0)
        attn_prob = probabilities(query_blk, offset).astype(jnp.bfloat16)
        return jnp.einsum(
            "hqk,khd->qhd", attn_prob, values, preferred_element_type=jnp.float32
        ).astype(jnp.bfloat16)

    mixed = lax.map(attend, jnp.arange(block_total, dtype=jnp.int32)).reshape(SEQ, local_width)
    picked = mixed
    second = xin + lax.psum_scatter(
        jnp.dot(picked, out_w, preferred_element_type=jnp.float32),
        "mp",
        scatter_dimension=0,
        tiled=True,
    )
    unit_second, inv_second, normed_second = norm_forward(second, gain_all[1])
    h_second = lax.all_gather(normed_second.astype(jnp.bfloat16), "mp", axis=0, tiled=True)
    gate_up = jnp.einsum("td,dcf->tcf", h_second, gu_w, preferred_element_type=jnp.float32)
    gate_val = gate_up[:, 0]
    up_val = gate_up[:, 1]
    act = (jax.nn.silu(gate_val) * up_val).astype(jnp.bfloat16)
    picked = act
    block_out = (
        second
        + lax.psum_scatter(
            jnp.dot(picked, down_w, preferred_element_type=jnp.float32).astype(jnp.bfloat16),
            "mp",
            scatter_dimension=0,
            tiled=True,
        ).astype(jnp.float32)
    ).astype(jnp.bfloat16)
    out_grad = cotangent.astype(jnp.float32) * live_rows
    branch_grad = lax.all_gather(out_grad.astype(jnp.bfloat16), "mp", axis=0, tiled=True)
    grad_down = jnp.einsum("tf,td->fd", act, branch_grad, preferred_element_type=jnp.float32)
    act_grad = jnp.einsum("td,fd->tf", branch_grad, down_w, preferred_element_type=jnp.float32)
    sigma = jax.nn.sigmoid(gate_val)
    gate_grad = act_grad * up_val * sigma * (1.0 + gate_val * (1.0 - sigma))
    up_grad = act_grad * gate_val * sigma
    gu_grad = jnp.stack([gate_grad, up_grad], axis=1).astype(jnp.bfloat16)
    grad_gu = jnp.einsum("td,tcf->dcf", h_second, gu_grad, preferred_element_type=jnp.float32)
    picked = gu_grad
    h_second_grad = lax.psum_scatter(
        jnp.einsum("tcf,dcf->td", picked, gu_w, preferred_element_type=jnp.float32),
        "mp",
        scatter_dimension=0,
        tiled=True,
    )
    norm_grad_second, gain_grad_second = norm_backward(
        h_second_grad, unit_second, inv_second, gain_all[1]
    )
    second_grad = out_grad + norm_grad_second
    attn_grad = lax.all_gather(second_grad.astype(jnp.bfloat16), "mp", axis=0, tiled=True)
    grad_out = jnp.einsum("tn,td->nd", mixed, attn_grad, preferred_element_type=jnp.float32)
    mixed_grad = jnp.einsum("td,nd->tn", attn_grad, out_w, preferred_element_type=jnp.float32)
    mixed_grad = mixed_grad.astype(jnp.bfloat16).reshape(SEQ, heads_here, HDIM)

    def back_block(carried, block_idx):
        key_grad, value_grad = carried
        offset = block_idx * block_len
        query_blk = lax.dynamic_slice_in_dim(queries, offset, block_len, 0)
        mixed_blk = lax.dynamic_slice_in_dim(mixed_grad, offset, block_len, 0)
        attn_prob = probabilities(query_blk, offset)
        prob_grad = jnp.einsum(
            "qhd,khd->hqk", mixed_blk, values, preferred_element_type=jnp.float32
        )
        value_grad = value_grad + jnp.einsum(
            "hqk,qhd->khd",
            attn_prob.astype(jnp.bfloat16),
            mixed_blk,
            preferred_element_type=jnp.float32,
        )
        score_grad = (prob_grad * attn_prob * (1.0 - attn_prob) * score_scale).astype(jnp.bfloat16)
        query_grad = jnp.einsum(
            "hqk,khd->qhd", score_grad, keys, preferred_element_type=jnp.float32
        )
        key_grad = key_grad + jnp.einsum(
            "hqk,qhd->khd", score_grad, query_blk, preferred_element_type=jnp.float32
        )
        return ((key_grad, value_grad), query_grad)

    zeros_kv = jnp.zeros((SEQ, heads_here, HDIM), jnp.float32)
    (key_total, value_total), query_blocks = lax.scan(
        back_block, (zeros_kv, zeros_kv), jnp.arange(block_total, dtype=jnp.int32)
    )
    query_total = query_blocks.reshape(SEQ, heads_here, HDIM)
    joined_grad = jnp.stack(
        [
            unrotate(query_total, cosine, sine_tab).reshape(SEQ, local_width),
            unrotate(key_total, cosine, sine_tab).reshape(SEQ, local_width),
            value_total.reshape(SEQ, local_width),
        ],
        axis=1,
    ).astype(jnp.bfloat16)
    grad_qkv = jnp.einsum("td,tcn->dcn", h_first, joined_grad, preferred_element_type=jnp.float32)
    picked = joined_grad
    h_first_grad = lax.psum_scatter(
        jnp.einsum("tcn,dcn->td", picked, qkv_w, preferred_element_type=jnp.float32).astype(
            jnp.bfloat16
        ),
        "mp",
        scatter_dimension=0,
        tiled=True,
    ).astype(jnp.float32)
    norm_grad_first, gain_grad_first = norm_backward(
        h_first_grad, unit_first, inv_first, gain_all[0]
    )
    input_grad = second_grad + norm_grad_first
    gain_partial = jnp.stack([gain_grad_first, gain_grad_second], axis=0)
    sum_gains = lax.psum_scatter(gain_partial, ("dp", "mp"), scatter_dimension=1, tiled=True)
    full_qkv, full_out, full_gu, full_down = (
        lax.psum(grad_qkv.astype(jnp.bfloat16), "dp").astype(jnp.float32),
        lax.psum(grad_out.astype(jnp.bfloat16), "dp").astype(jnp.float32),
        lax.psum(grad_gu.astype(jnp.bfloat16), "dp").astype(jnp.float32),
        lax.psum(grad_down.astype(jnp.bfloat16), "dp").astype(jnp.float32),
    )
    owner = lax.axis_index("dp")
    sum_qkv = lax.dynamic_slice_in_dim(full_qkv, owner * w_qkv.shape[0], w_qkv.shape[0], 0)
    sum_out = lax.dynamic_slice_in_dim(full_out, owner * w_out.shape[1], w_out.shape[1], 1)
    sum_gu = lax.dynamic_slice_in_dim(full_gu, owner * w_gu.shape[0], w_gu.shape[0], 0)
    sum_down = lax.dynamic_slice_in_dim(full_down, owner * w_down.shape[1], w_down.shape[1], 1)
    total_rows = SEQ * lax.axis_size("dp")
    matrix_rate = step_rate / math.sqrt(total_rows)
    scale_rate = gain_rate / math.sqrt(total_rows)
    new_qkv, next_mom_qkv, next_avg_qkv = update(w_qkv, mom_qkv, avg_qkv, sum_qkv, matrix_rate)
    new_out, next_mom_out, next_avg_out = update(w_out, mom_out, avg_out, sum_out, matrix_rate)
    new_gu, next_mom_gu, next_avg_gu = update(w_gu, mom_gu, avg_gu, sum_gu, matrix_rate)
    new_down, next_mom_down, next_avg_down = update(
        w_down, mom_down, avg_down, sum_down, matrix_rate
    )
    new_gains, next_mom_gains, next_avg_gains = update(
        gains, mom_gains, avg_gains, sum_gains, scale_rate
    )
    return (
        block_out,
        input_grad,
        new_qkv,
        new_out,
        new_gu,
        new_down,
        new_gains,
        next_mom_qkv,
        next_mom_out,
        next_mom_gu,
        next_mom_down,
        next_mom_gains,
        next_avg_qkv,
        next_avg_out,
        next_avg_gu,
        next_avg_down,
        next_avg_gains,
        new_qkv.astype(jnp.bfloat16),
        new_out.astype(jnp.bfloat16),
        new_gu.astype(jnp.bfloat16),
        new_down.astype(jnp.bfloat16),
    )


def solution(mesh):
    return jax.shard_map(
        per_device,
        mesh=mesh,
        in_specs=(
            P(("dp", "mp"), None),
            P(("dp", "mp"), None),
            P("dp"),
            P("dp", None, "mp"),
            P("mp", "dp"),
            P("dp", None, "mp"),
            P("mp", "dp"),
            P(None, ("dp", "mp")),
            P("dp", None, "mp"),
            P("mp", "dp"),
            P("dp", None, "mp"),
            P("mp", "dp"),
            P(None, ("dp", "mp")),
            P("dp", None, "mp"),
            P("mp", "dp"),
            P("dp", None, "mp"),
            P("mp", "dp"),
            P(None, ("dp", "mp")),
        ),
        out_specs=(
            P(("dp", "mp"), None),
            P(("dp", "mp"), None),
            P("dp", None, "mp"),
            P("mp", "dp"),
            P("dp", None, "mp"),
            P("mp", "dp"),
            P(None, ("dp", "mp")),
            P("dp", None, "mp"),
            P("mp", "dp"),
            P("dp", None, "mp"),
            P("mp", "dp"),
            P(None, ("dp", "mp")),
            P("dp", None, "mp"),
            P("mp", "dp"),
            P("dp", None, "mp"),
            P("mp", "dp"),
            P(None, ("dp", "mp")),
            P("dp", None, "mp"),
            P("mp", "dp"),
            P("dp", None, "mp"),
            P("mp", "dp"),
        ),
        check_vma=False,
    )
```

profile of v0, /device:TPU:0, one launch (start us, length us, event | category | flops | bytes accessed | tf_op | source)
XLA Modules:
  0.0 1838.9 jit_solution(5286131066196238677)
XLA Ops:
  7.2 70.0 %all-gather = f32[32,64,2]{1,2,0:T(2,128)S(1)} all-gather(f32[1,64,2]{1,2,0:T(2,128)} %bitcast.149), channel_id=1, replica_groups=mesh['dp'=8,'mp'=4] {'dp','mp'}, dimensions={0}, use_global_device_ids=true | all-gather | bytes 16896 | tf_op jit(solution)/shard_map/all_gather | solution.py:98
  86.5 72.2 %all-gather.10.cloned.1.call-done = bf16[1024,2048]{1,0:T(8,128)(2,1)} async-done(((bf16[256,2048]{1,0:T(8,128)(2,1)}), bf16[1024,2048]{1,0:T(8,128)(2,1)}) %all-gather.10.cloned.1.call-update) | async-done | bytes 4194320 | tf_op jit(solution)/shard_map/all_gather | solution.py:103
  158.8 47.7 %all-gather.12.cloned.1.call-done = bf16[2048,3,512]{0,2,1:T(8,128)(2,1)} async-done(((bf16[256,3,512]{0,2,1:T(8,128)(2,1)}), bf16[2048,3,512]{0,2,1:T(8,128)(2,1)}) %all-gather.12.cloned.1.call-update) | async-done | bytes 6291472 | tf_op jit(solution)/shard_map/all_gather | solution.py:93
  240.7 21.0 %while.28 = (s32[]{:T(128)}, bf16[2,512,4,128]{3,2,1,0:T(4,128)(2,1)}, s32[2]{0:T(128)S(1)}, bf16[1024,4,128]{2,0,1:T(8,128)(2,1)}, bf16[1024,4,128]{2,0,1:T(8,1...) while((s32[]{:T(128)}, ...), condition=%wide.region_2.3_spmd.clone.clone, body=%wide.region_1.2_spmd.clone.clone.sunk | while | flops 1090258432 | bytes 8395443 | solution.py:129
  275.2 139.0 %reduce-scatter.8.cloned.1.call-done = f32[256,2048]{1,0:T(8,128)} async-done(((f32[1024,2048]{1,0:T(8,128)}), f32[256,2048]{1,0:T(8,128)}) %reduce-scatter.8.cloned.1.call-update) | async-done | bytes 2097168 | tf_op jit(solution)/shard_map/reduce_scatter | solution.py:131
  423.6 83.5 %all-gather.18.cloned.1.call-done = bf16[2048,2,2048]{2,0,1:T(8,128)(2,1)} async-done(((bf16[256,2,2048]{2,0,1:T(8,128)(2,1)}), bf16[2048,2,2048]{2,0,1:T(8,128)(2,1)}) %all-gather.18.cloned.1.call-update) | async-done | bytes 16777232 | tf_op jit(solution)/shard_map/all_gather | solution.py:95
  507.1 82.8 %all-gather.16.cloned.1.call-done = bf16[1024,2048]{1,0:T(8,128)(2,1)} async-done(((bf16[256,2048]{1,0:T(8,128)(2,1)}), bf16[1024,2048]{1,0:T(8,128)(2,1)}) %all-gather.16.cloned.1.call-update) | async-done | bytes 4194320 | tf_op jit(solution)/shard_map/all_gather | solution.py:138
  589.9 23.9 %fusion.36 = f32[1024,2,2048]{2,0,1:T(8,128)} fusion(bf16[2048,2,2048]{2,0,1:T(8,128)(2,1)} %all-gather.18.cloned.1.call-done, bf16[1024,2048]{1,0:T(8,128)(2,1)} %all-gather.16.cloned.1.call-done), kind=kOutput, calls=%fused_computation.53 | convolution fusion | flops 17179869184 | bytes 37748736 | tf_op jit(solution)/shard_map/td,dcf->tcf/dot_general | solution.py:139
  613.8 57.6 %all-gather.22.cloned.1.call-done = bf16[1024,2048]{1,0:T(8,128)(2,1)} async-done(((bf16[256,2048]{1,0:T(8,128)(2,1)}), bf16[1024,2048]{1,0:T(8,128)(2,1)}) %all-gather.22.cloned.1.call-update) | async-done | bytes 4194320 | tf_op jit(solution)/shard_map/all_gather | solution.py:154
  671.3 57.0 %all-gather.20.cloned.1.call-done = bf16[2048,2048]{1,0:T(8,128)(2,1)} async-done(((bf16[2048,256]{1,0:T(8,128)(2,1)}), bf16[2048,2048]{1,0:T(8,128)(2,1)}) %all-gather.20.cloned.1.call-update) | async-done | bytes 8388624 | tf_op jit(solution)/shard_map/all_gather | solution.py:96
  728.3 21.8 %fusion.44 = (bf16[1024,1,2048]{2,0,1:T(8,128)(2,1)}, bf16[1024,1,2048]{2,0,1:T(8,128)(2,1)}, bf16[1024,2048]{1,0:T(8,128)(2,1)}) fusion(f32[1024,2,2048]{2,0,1:T(8,128)} %fusion.36, bf16[1024,2048]{1,0:T(8,128)(2,1)} %all-gather.22.cloned.1.call-done, bf16[2048,2048]{1,0:T(8,128)(2,1)} %all-gather.20.cloned.1.call-done), kind=kOutput, calls=%fused_computation.65 | convolution fusion | flops 8623489024 | bytes 41943040 | tf_op jit(solution)/shard_map/td,fd->tf/dot_general | solution.py:156
  750.2 24.2 %fusion.34 = f32[1024,2048]{1,0:T(8,128)} fusion(bf16[2048,2,2048]{2,0,1:T(8,128)(2,1)} %all-gather.18.cloned.1.call-done, bf16[1024,1,2048]{2,0,1:T(8,128)(2,1)} %get-tuple-element.405, bf16[1024,1,2048]{2,0,1:T(8,128)(2,1)} %get-tuple-element.404), kind=kOutput, calls=%fused_computation.51 | convolution fusion | flops 17184063488 | bytes 33554432 | tf_op jit(solution)/shard_map/tcf,dcf->td/dot_general | solution.py:164
  774.5 14.0 convolution_convert_fusion.3
  788.6 130.5 %reduce-scatter.12.cloned.1.call-done = f32[256,2048]{1,0:T(8,128)} async-done(((f32[1024,2048]{1,0:T(8,128)}), f32[256,2048]{1,0:T(8,128)}) %reduce-scatter.12.cloned.1.call-update) | async-done | bytes 2097168 | tf_op jit(solution)/shard_map/reduce_scatter | solution.py:163
  921.8 76.9 %reduce-scatter.10.cloned.1.call-done = bf16[256,2048]{1,0:T(8,128)(2,1)} async-done(((bf16[1024,2048]{1,0:T(8,128)(2,1)}), bf16[256,2048]{1,0:T(8,128)(2,1)}) %reduce-scatter.10.cloned.1.call-update) | async-done | bytes 1048592 | tf_op jit(solution)/shard_map/reduce_scatter | solution.py:146
  1003.8 81.3 %all-gather.24.cloned.1.call-done = bf16[1024,2048]{1,0:T(8,128)(2,1)} async-done(((bf16[256,2048]{1,0:T(8,128)(2,1)}), bf16[1024,2048]{1,0:T(8,128)(2,1)}) %all-gather.24.cloned.1.call-update) | async-done | bytes 4194320 | tf_op jit(solution)/shard_map/all_gather | solution.py:173
  1091.4 47.3 %while.29 = (s32[]{:T(128)}, f32[1024,4,128]{0,2,1:T(8,128)S(1)}, f32[1024,4,128]{0,2,1:T(8,128)}, f32[2,512,4,128]{3,1,0,2:T(8,128)}, s32[2]{0:T(128)S(1)}, /*i...) while((s32[]{:T(128)}, f32[1024,4,128]{0,2,1:T(8,128)S(1)}, ...), condition=%wide.region_9.10_spmd.clone.clone, body=%wide.region_8.9_spmd.clone.clone.sunk | while | flops 2713191936 | bytes 157293472 | solution.py:203
  1155.2 11.4 bitcast_convert_fusion
  1166.7 14.1 convolution_convert_fusion.1
  1180.8 25.1 %convolution_convert_fusion = bf16[2048,2,2048]{2,0,1:T(8,128)(2,1)} fusion(bf16[1024,1,2048]{2,0,1:T(8,128)(2,1)} %get-tuple-element.405, bf16[1024,1,2048]{2,0,1:T(8,128)(2,1)} %get-tuple-element.404, bf16[1024,2048]{1,0:T(8,128)(2,1)} %all-gather.16.cloned.1.call-done), kind=kOutput, calls=%fused_computation.39 | convolution fusion | flops 17205035008 | bytes 29360128 | tf_op jit(solution)/shard_map/td,tcf->dcf/dot_general | solution.py:161
  1206.0 11.3 convolution_convert_fusion.2
  1217.3 24.8 %reduce-scatter.14.cloned.1.call-done = bf16[256,2048]{1,0:T(8,128)(2,1)} async-done(((bf16[1024,2048]{1,0:T(8,128)(2,1)}), bf16[256,2048]{1,0:T(8,128)(2,1)}) %reduce-scatter.14.cloned.1.call-update) | async-done | bytes 1048592 | tf_op jit(solution)/shard_map/reduce_scatter | solution.py:217
  1256.3 125.4 %reduce-scatter.16.cloned.1.call-done = f32[64,2]{1,0:T(8,128)} async-done(((f32[2048,2]{1,0:T(8,128)}), f32[64,2]{1,0:T(8,128)}) %reduce-scatter.16.cloned.1.call-update) | async-done | bytes 528
  1383.2 401.2 %all-reduce.3.cloned.1.call-done = (bf16[2048,3,512]{2,0,1:T(8,128)(2,1)}, bf16[512,2048]{1,0:T(8,128)(2,1)}, bf16[2048,2,2048]{2,0,1:T(8,128)(2,1)}, bf16[2048,2048]{1,0:T(8,128)(2,1)}) async-done(((bf16[2048,3,512]{2,0,1:T(8,128)(2,1)}, bf16[512,2048]{1,0:T(8,128)(2,1)}, bf16[2048,2,2048]{2,0,1:T(8,128)(2,1)}, bf16[2048,2048]{1,0:T(8,128)(2,1)}), (bf16[2048,3,512]{2,0,1:T(8,128)(2,1)}, ...) | async-done | bytes 33554448 | tf_op jit(solution)/shard_map/psum | solution.py:232
  (217 shorter events, 224.4 us)
Async XLA Ops:
  7.2 151.6 %all-gather.10.cloned.1.call-start = ((), (), s32[]{:S(2)}) async-start(), calls=%async_computation.5 | async-start | bytes 5242880 | tf_op jit(solution)/shard_map/all_gather | solution.py:103
  81.6 124.9 %all-gather.12.cloned.1.call-start = ((), (), s32[]{:S(2)}) async-start(), calls=%async_computation.6 | async-start | bytes 7077888 | tf_op jit(solution)/shard_map/all_gather | solution.py:93
  82.8 178.9 %all-gather.14.cloned.1.call-start = ((), (), s32[]{:S(2)}) async-start(), calls=%async_computation.7 | async-start | bytes 2359296 | tf_op jit(solution)/shard_map/all_gather | solution.py:94
  83.7 330.5 %reduce-scatter.8.cloned.1.call-start = ((), (), s32[]{:S(2)}) async-start(), calls=%async_computation.8 | async-start | bytes 10485760 | tf_op jit(solution)/shard_map/reduce_scatter | solution.py:131
  269.3 237.8 %all-gather.18.cloned.1.call-start = ((), (), s32[]{:S(2)}) async-start(), calls=%async_computation.10 | async-start | bytes 18874368 | tf_op jit(solution)/shard_map/all_gather | solution.py:95
  275.1 314.7 %all-gather.16.cloned.1.call-start = ((), (), s32[]{:S(2)}) async-start(), calls=%async_computation.9 | async-start | bytes 5242880 | tf_op jit(solution)/shard_map/all_gather | solution.py:138
  417.6 253.7 %all-gather.22.cloned.1.call-start = ((), (), s32[]{:S(2)}) async-start(), calls=%async_computation.13 | async-start | bytes 5242880 | tf_op jit(solution)/shard_map/all_gather | solution.py:154
  420.8 307.5 %all-gather.20.cloned.1.call-start = ((), (), s32[]{:S(2)}) async-start(), calls=%async_computation.11 | async-start | bytes 9437184 | tf_op jit(solution)/shard_map/all_gather | solution.py:96
  423.5 495.5 %reduce-scatter.12.cloned.1.call-start = ((), (), s32[]{:S(2)}) async-start(), calls=%async_computation.14 | async-start | bytes 10485760 | tf_op jit(solution)/shard_map/reduce_scatter | solution.py:163
  774.4 224.3 %reduce-scatter.10.cloned.1.call-start = ((), (), s32[]{:S(2)}) async-start(), calls=%async_computation.12 | async-start | bytes 5242880 | tf_op jit(solution)/shard_map/reduce_scatter | solution.py:146
  788.5 296.7 %all-gather.24.cloned.1.call-start = ((), (), s32[]{:S(2)}) async-start(), calls=%async_computation.15 | async-start | bytes 5242880 | tf_op jit(solution)/shard_map/all_gather | solution.py:173
  1003.8 238.4 %reduce-scatter.14.cloned.1.call-start = ((), (), s32[]{:S(2)}) async-start(), calls=%async_computation.16 | async-start | bytes 5242880 | tf_op jit(solution)/shard_map/reduce_scatter | solution.py:217
  1127.0 8.0 copy-start.1
  1166.7 215.1 %reduce-scatter.16.cloned.1.call-start = ((), (), s32[]{:S(2)}) async-start(), calls=%async_computation.17 | async-start | bytes 1081344
  1180.8 25.1 %copy-start.24 = (bf16[1024,1,512]{2,0,1:T(8,128)(2,1)S(1)}, bf16[1024,1,512]{2,0,1:T(8,128)(2,1)}, u32[]{:S(2)}) copy-start(bf16[1024,1,512]{2,0,1:T(8,128)(2,1)} %copy.128) | copy-start | bytes 3145732
  1205.9 36.2 %copy-start.3 = (bf16[256,2048]{1,0:T(8,128)(2,1)S(1)}, bf16[256,2048]{1,0:T(8,128)(2,1)}, u32[]{:S(2)}) copy-start(bf16[256,2048]{1,0:T(8,128)(2,1)} %param.22) | copy-start | bytes 3145732
  1205.9 36.2 %copy-start.29 = (f32[1,2048]{1,0:T(1,128)S(1)}, f32[1,2048]{1,0:T(1,128)}, u32[]{:S(2)}) copy-start(f32[1,2048]{1,0:T(1,128)} %copy-done.28) | copy-start | bytes 24580
  1205.9 36.2 %copy-start.32 = (f32[256]{0:T(256)S(1)}, f32[256]{0:T(256)}, u32[]{:S(2)}) copy-start(f32[256]{0:T(256)} %copy-done.31) | copy-start | bytes 3076
  1217.3 26.9 %copy-start.30 = (f32[2048]{0:T(1024)S(1)}, f32[2048]{0:T(1024)}, u32[]{:S(2)}) copy-start(f32[2048]{0:T(1024)} %get-tuple-element.343) | copy-start | bytes 24580
  1217.3 28.4 %copy-start.36 = (bf16[2,512,4,128]{3,2,1,0:T(4,128)(2,1)S(1)}, bf16[2,512,4,128]{3,2,1,0:T(4,128)(2,1)}, u32[]{:S(2)}) copy-start(bf16[2,512,4,128]{3,2,1,0:T(4,128)(2,1)} %get-tuple-element.128) | copy-start | bytes 3145732
  1245.6 538.8 %all-reduce.3.cloned.1.call-start = ((), (), s32[]{:S(2)}) async-start(), calls=%async_computation.18 | async-start | bytes 67108864 | tf_op jit(solution)/shard_map/psum | solution.py:232
  1253.1 129.5 %copy-start.33 = (f32[2,64]{1,0:T(2,128)S(1)}, f32[2,64]{1,0:T(2,128)}, u32[]{:S(2)}) copy-start(f32[2,64]{1,0:T(2,128)} %param.29) | copy-start | bytes 1540
  1253.1 129.5 %copy-start.34 = (f32[2,64]{1,0:T(2,128)S(1)}, f32[2,64]{1,0:T(2,128)}, u32[]{:S(2)}) copy-start(f32[2,64]{1,0:T(2,128)} %param.39) | copy-start | bytes 1540
  1253.1 129.5 %copy-start.35 = (f32[2,64]{1,0:T(2,128)S(1)}, f32[2,64]{1,0:T(2,128)}, u32[]{:S(2)}) copy-start(f32[2,64]{1,0:T(2,128)} %param.34) | copy-start | bytes 1540
  (34 other events, 105.9 us)
Sparse Core Ops, SparseCore 0:
  81.7 77.0 all-gather.9
  161.2 45.1 all-gather.11
  208.9 28.1 all-gather.13
  269.4 144.6 reduce-scatter.7
  416.5 90.5 all-gather.17
  509.1 80.7 all-gather.15
  592.0 79.2 all-gather.21
  673.8 54.4 all-gather.19
  774.6 144.4 reduce-scatter.11
  921.2 77.4 reduce-scatter.9
  1003.9 81.2 all-gather.23
  1166.8 75.2 reduce-scatter.13
  1245.7 136.0 reduce-scatter.15
  1387.1 397.2 all-reduce.2
where the time goes:
time: 1850 us; the launch traced here: 1840 us
  waiting for transfers between devices  1380 us (75%)
  matrix products  222 us (12%)
  other arithmetic  77 us (4%)
  local copies, waits for them, and re-layouts  70.2 us (4%)
  blocking collectives  70 us (4%)
    psum x1, waiting for transfers between devices, per_device(): lax.psum(grad_qkv.astype(jnp.bfloat16), 'dp').astype(jnp.float32)  401 us
    reduce_scatter x1, waiting for transfers between devices, per_device(): lax.psum_scatter(jnp.dot(picked, out_w, preferred_element_type=jnp.float3...  139 us
    reduce_scatter x1, waiting for transfers between devices, per_device(): lax.psum_scatter(jnp.einsum('tcf,dcf->td', picked, gu_w, preferred_elemen...  130 us
    unnamed x15, waiting for transfers between devices  126 us
    all_gather x1, waiting for transfers between devices, per_device(): lax.all_gather(w_gu.astype(jnp.bfloat16), 'dp', axis=0, tiled=True)  83.5 us
    all_gather x1, waiting for transfers between devices, per_device(): lax.all_gather(normed_second.astype(jnp.bfloat16), 'mp', axis=0, tiled=True)  82.8 us
    all_gather x1, waiting for transfers between devices, per_device(): lax.all_gather(second_grad.astype(jnp.bfloat16), 'mp', axis=0, tiled=True)  81.3 us
    reduce_scatter x1, waiting for transfers between devices, per_device(): lax.psum_scatter(jnp.dot(picked, down_w, preferred_element_type=jnp.float...  76.9 us
  transfers between devices with their start and end apart: 14, of which 13 were waited for; matrix products, arithmetic and copies ran while one was open for 9% of the time, Pallas kernels for 0%

commit v1 on v0

v1 whole, which is shorter than its diff:
```python
import functools
import math

import jax
import jax.numpy as jnp
from jax import lax
from jax.experimental import pallas as pl
from jax.experimental.pallas import tpu as pltpu
from jax.sharding import PartitionSpec as P

HDIM = 128
SEQ = 1024
MESH = pl.DeviceIdType.MESH
ANY = pl.BlockSpec(memory_space=pl.ANY)
VMEM = pl.BlockSpec(memory_space=pltpu.VMEM)
VMEM_LIMIT = 60 * 1024 * 1024

norm_eps = 1e-05
rope_base = 10000.0
momentum_decay = 0.9
average_decay = 0.9
step_rate = 0.05
gain_rate = 0.5


def rows_at(start, size):
    return pl.ds(pl.multiple_of(start, size), size)


def remote(src, dst, send_sem, recv_sem, peer):
    return pltpu.make_async_remote_copy(
        src_ref=src,
        dst_ref=dst,
        send_sem=send_sem,
        recv_sem=recv_sem,
        device_id={"mp": peer},
        device_id_type=MESH,
    )


def neighbour_barrier(n):
    me = lax.axis_index("mp")
    barrier = pltpu.get_barrier_semaphore()

    @pl.when(me > 0)
    def _():
        pl.semaphore_signal(barrier, inc=1, device_id={"mp": me - 1}, device_id_type=MESH)

    @pl.when(me < n - 1)
    def _():
        pl.semaphore_signal(barrier, inc=1, device_id={"mp": me + 1}, device_id_type=MESH)

    pl.semaphore_wait(barrier, jnp.where(me > 0, 1, 0) + jnp.where(me < n - 1, 1, 0))


class LineGather:
    def __init__(self, n, rows, chunks, own, whole, sems):
        self.n, self.rows, self.chunks = n, rows, chunks
        self.size = rows // chunks
        self.own, self.whole, self.sems = own, whole, sems
        self.me = lax.axis_index("mp")

    def at(self, block, chunk):
        return self.whole.at[rows_at(block * self.rows + chunk * self.size, self.size)]

    def copies(self, step, chunk, first):
        me, n = self.me, self.n
        send_r, recv_r, send_l, recv_l = self.sems
        out = []
        for block, peer, has, send, recv in (
            (me - step, me + 1, (me - step >= 0) & (me < n - 1), send_r, recv_r),
            (me + step, me - 1, (me + step <= n - 1) & (me > 0), send_l, recv_l),
        ):
            src = (
                self.own.at[pl.ds(chunk * self.size, self.size)]
                if first
                else self.at(block, chunk)
            )
            index = step * self.chunks + chunk
            out.append(
                (has, remote(src, self.at(block, chunk), send.at[index], recv.at[index], peer))
            )
        return out

    def arrivals(self, step, chunk):
        me, n = self.me, self.n
        send_r, recv_r, send_l, recv_l = self.sems
        index = step * self.chunks + chunk
        out = []
        for block, has, send, recv in (
            (me - 1 - step, me - 1 - step >= 0, send_r, recv_r),
            (me + 1 + step, me + 1 + step <= n - 1, send_l, recv_l),
        ):
            ref = self.at(block, chunk)
            out.append((has, remote(ref, ref, send.at[index], recv.at[index], me)))
        return out

    def send_own(self, chunk):
        for has, copy in self.copies(0, chunk, True):
            pl.when(has)(copy.start)

    def forward(self, step):
        for chunk in range(self.chunks):
            for (got, arrival), (has, copy) in zip(
                self.arrivals(step - 1, chunk), self.copies(step, chunk, False)
            ):
                pl.when(got)(arrival.wait_recv)
                pl.when(has)(copy.start)

    def finish(self):
        for chunk in range(self.chunks):
            for got, arrival in self.arrivals(self.n - 2, chunk):
                pl.when(got)(arrival.wait_recv)
        for chunk in range(self.chunks):
            for has, copy in self.copies(0, chunk, True):
                pl.when(has)(copy.wait_send)

        def waits(step, carry):
            for chunk in range(self.chunks):
                for has, copy in self.copies(step, chunk, False):
                    pl.when(has)(copy.wait_send)
            return carry

        lax.fori_loop(1, self.n - 1, waits, 0)

    def forward_all(self):
        def step_of(step, carry):
            self.forward(step)
            return carry

        lax.fori_loop(1, self.n - 1, step_of, 0)


def gather_sems(n, chunks):
    return [pltpu.SemaphoreType.DMA(((n - 1) * chunks,))] * 4


def gather_rows(n, own, collective_id):
    rows, width = own.shape

    def kernel(own_ref, whole_ref, local_sem, *sems):
        me = lax.axis_index("mp")
        stream = LineGather(n, rows, 1, own_ref, whole_ref, sems)
        local = pltpu.make_async_copy(own_ref, stream.at(me, 0), local_sem)
        local.start()
        neighbour_barrier(n)
        stream.send_own(0)
        stream.forward_all()
        stream.finish()
        local.wait()

    return pl.pallas_call(
        kernel,
        out_shape=jax.ShapeDtypeStruct((n * rows, width), own.dtype),
        in_specs=[ANY],
        out_specs=ANY,
        scratch_shapes=[pltpu.SemaphoreType.DMA] + gather_sems(n, 1),
        compiler_params=pltpu.CompilerParams(collective_id=collective_id, has_side_effects=True),
        cost_estimate=pl.CostEstimate(
            flops=0, bytes_accessed=200 * own.size * own.dtype.itemsize, transcendentals=0
        ),
        name="gather_rows",
    )(own)


def scatter_rows(n, pairs, own_rows, epilogue, gains_row, collective_id, extra=None, chunks=2):
    total_rows = pairs[0][0].shape[0]
    rows = total_rows // n
    width = gains_row.shape[1]
    size = rows // chunks
    tile = 512
    gathers = epilogue != "last"
    lhs_args = [p[0] for p in pairs]
    rhs_args = [p[1] for p in pairs]
    flips = [p[2] for p in pairs]
    count = len(pairs)
    block = 32

    def kernel(*refs):
        refs = list(refs)
        take = lambda k: [refs.pop(0) for _ in range(k)]
        lhs, rhs = take(count), take(count)
        (gain_ref,) = take(1)
        own = take(len(own_rows))
        extra_ref = take(1)[0] if extra is not None else None
        outs = take(2 if epilogue != "forward" else 1)
        whole = take(1)[0] if gathers else None
        extra_whole = take(1)[0] if extra is not None else None
        held, sent, part = take(3)
        normed = take(1)[0] if gathers else None
        send_sems, recv_sems = take(2)
        gather = extra_gather = None
        me = lax.axis_index("mp")
        if gathers:
            (local_sem,) = take(1)
            gather = LineGather(n, rows, chunks, normed, whole, take(4))
        if extra is not None:
            (extra_sem,) = take(1)
            extra_gather = LineGather(n, rows, 1, extra_ref, extra_whole, take(4))
            extra_local = pltpu.make_async_copy(extra_ref, extra_gather.at(me, 0), extra_sem)
            extra_local.start()
        neighbour_barrier(n)
        if extra is not None:
            extra_gather.send_own(0)

        def product(block_id):
            def column(ct, carry):
                cols = rows_at(ct * tile, tile)
                total = None
                for a, b, flip in zip(lhs, rhs, flips):
                    left = a[rows_at(block_id * rows, rows), :]
                    if flip:
                        term = lax.dot_general(
                            left,
                            b[cols, :],
                            (((1,), (1,)), ((), ())),
                            preferred_element_type=jnp.float32,
                        )
                    else:
                        term = jnp.dot(left, b[:, cols], preferred_element_type=jnp.float32)
                    total = term if total is None else total + term
                part[:, cols] = total
                return carry

            lax.fori_loop(0, width // tile, column, 0)

        def hop(block_id, chunk, rightward):
            peer = me + 1 if rightward else me - 1
            slot = block_id if rightward else jnp.where(block_id == peer, n, block_id)
            return remote(
                sent.at[block_id, pl.ds(chunk * size, size)],
                held.at[slot, pl.ds(chunk * size, size)],
                send_sems.at[block_id * chunks + chunk],
                recv_sems.at[slot * chunks + chunk],
                peer,
            )

        def arrival(slot, chunk):
            ref = held.at[slot, pl.ds(chunk * size, size)]
            return remote(
                ref, ref, send_sems.at[chunk], recv_sems.at[slot * chunks + chunk], me
            )

        def add_rows(block_id, chunk, slots):
            def body(i, carry):
                span = rows_at(chunk * size + i * block, block)
                value = part[span, :]
                for slot in slots:
                    value = value + held[slot, span, :].astype(jnp.float32)
                sent[block_id, span, :] = value.astype(jnp.bfloat16)
                return carry

            lax.fori_loop(0, size // block, body, 0)

        def relay(block_id, rightward, inner):
            product(block_id)
            for chunk in range(chunks):

                @pl.when(inner)
                def _():
                    arrival(block_id, chunk).wait_recv()
                    add_rows(block_id, chunk, [block_id])

                @pl.when(jnp.logical_not(inner))
                def _():
                    add_rows(block_id, chunk, [])

                hop(block_id, chunk, rightward).start()

        def step_of(step, carry):
            @pl.when((step >= me + 1) & (me < n - 1))
            def _():
                relay(me + n - step, True, me > 0)

            @pl.when((step >= n - me) & (me > 0))
            def _():
                relay(me - n + step, False, me < n - 1)

            if extra is not None:

                @pl.when(step < n - 1)
                def _():
                    extra_gather.forward(step)

            return carry

        lax.fori_loop(1, n, step_of, 0)
        product(me)
        if epilogue != "forward":
            outs[1][...] = jnp.zeros_like(outs[1])
        for chunk in range(chunks):

            @pl.when(me > 0)
            def _():
                arrival(me, chunk).wait_recv()

            @pl.when(me < n - 1)
            def _():
                arrival(n, chunk).wait_recv()

            def body(i, carry):
                span = rows_at(chunk * size + i * block, block)
                total = part[span, :]
                zero = jnp.zeros_like(total)
                total = total + jnp.where(me > 0, held[me, span, :].astype(jnp.float32), zero)
                total = total + jnp.where(
                    me < n - 1, held[n, span, :].astype(jnp.float32), zero
                )
                gain = gain_ref[...]
                if epilogue == "forward":
                    value = own[0][span, :] + total
                    outs[0][span, :] = value
                    inverse = lax.rsqrt(
                        jnp.mean(value * value, axis=1, keepdims=True) + norm_eps
                    )
                    normed[span, :] = (value * inverse * gain).astype(jnp.bfloat16)
                else:
                    value = own[0][span, :]
                    inverse = lax.rsqrt(
                        jnp.mean(value * value, axis=1, keepdims=True) + norm_eps
                    )
                    unit = value * inverse
                    scaled = total * gain
                    inner = jnp.mean(scaled * unit, axis=1, keepdims=True)
                    result = own[1][span, :] + inverse * (scaled - unit * inner)
                    outs[0][span, :] = result
                    outs[1][...] += jnp.sum(
                        (total * unit).reshape(block // 8, 8, width), axis=0
                    )
                    if gathers:
                        normed[span, :] = result.astype(jnp.bfloat16)
                return carry

            lax.fori_loop(0, size // block, body, 0)
            if gathers:
                gather.send_own(chunk)
        if gathers:
            local = pltpu.make_async_copy(
                normed, whole.at[rows_at(me * rows, rows)], local_sem
            )
            local.start()
        if extra is not None:
            extra_gather.finish()
            extra_local.wait()
        if gathers:
            gather.forward_all()
            gather.finish()
            local.wait()

        def sends(step, carry):
            for chunk in range(chunks):

                @pl.when((step >= me + 1) & (me < n - 1))
                def _():
                    hop(me + n - step, chunk, True).wait_send()

                @pl.when((step >= n - me) & (me > 0))
                def _():
                    hop(me - n + step, chunk, False).wait_send()

            return carry

        lax.fori_loop(1, n, sends, 0)

    out_shape = [jax.ShapeDtypeStruct((rows, width), jnp.float32)]
    out_specs = [VMEM]
    if epilogue != "forward":
        out_shape.append(jax.ShapeDtypeStruct((8, width), jnp.float32))
        out_specs.append(VMEM)
    scratch = [
        pltpu.VMEM((n + 1, rows, width), jnp.bfloat16),
        pltpu.VMEM((n, rows, width), jnp.bfloat16),
        pltpu.VMEM((rows, width), jnp.float32),
    ]
    if gathers:
        out_shape.append(jax.ShapeDtypeStruct((total_rows, width), jnp.bfloat16))
        out_specs.append(ANY)
        scratch.append(pltpu.VMEM((rows, width), jnp.bfloat16))
    scratch += [
        pltpu.SemaphoreType.DMA((n * chunks,)),
        pltpu.SemaphoreType.DMA(((n + 1) * chunks,)),
    ]
    if gathers:
        scratch += [pltpu.SemaphoreType.DMA] + gather_sems(n, chunks)
    extra_args = []
    if extra is not None:
        out_shape.append(jax.ShapeDtypeStruct((total_rows, width), jnp.bfloat16))
        out_specs.append(ANY)
        scratch += [pltpu.SemaphoreType.DMA] + gather_sems(n, 1)
        extra_args = [extra]
    flops = sum(2 * a.size * width for a in lhs_args)
    return pl.pallas_call(
        kernel,
        out_shape=out_shape,
        in_specs=[VMEM] * (2 * count + 1 + len(own_rows)) + [ANY] * len(extra_args),
        out_specs=out_specs,
        scratch_shapes=scratch,
        compiler_params=pltpu.CompilerParams(
            collective_id=collective_id, has_side_effects=True, vmem_limit_bytes=VMEM_LIMIT
        ),
        cost_estimate=pl.CostEstimate(
            flops=flops, bytes_accessed=300_000_000, transcendentals=0
        ),
        name="scatter_" + epilogue,
    )(*lhs_args, *rhs_args, gains_row, *own_rows, *extra_args)


def small_exchange(n_dp, n_mp, table, reduces, collective_id):
    peers_mp, peers_dp = n_mp - 1, n_dp - 1

    def kernel(in_ref, out_ref, first, second, mid, s_mp, r_mp, s_dp, r_dp):
        dp, mp = lax.axis_index("dp"), lax.axis_index("mp")
        barrier = pltpu.get_barrier_semaphore()
        for k in range(1, n_mp):
            pl.semaphore_signal(
                barrier, inc=1, device_id={"mp": lax.rem(mp + k, n_mp)}, device_id_type=MESH
            )
        for k in range(1, n_dp):
            pl.semaphore_signal(
                barrier, inc=1, device_id={"dp": lax.rem(dp + k, n_dp)}, device_id_type=MESH
            )
        pl.semaphore_wait(barrier, peers_mp + peers_dp)
        if reduces:
            first[mp] = in_ref[mp]
        else:
            first[mp] = in_ref[...]
        copies = []
        for k in range(1, n_mp):
            peer = lax.rem(mp + k, n_mp)
            copies.append(
                pltpu.make_async_remote_copy(
                    src_ref=in_ref.at[peer] if reduces else in_ref,
                    dst_ref=first.at[mp],
                    send_sem=s_mp.at[k - 1],
                    recv_sem=r_mp.at[k - 1],
                    device_id={"mp": peer},
                    device_id_type=MESH,
                )
            )
        for copy in copies:
            copy.start()
        for copy in copies:
            copy.wait()
        if reduces:
            total = first[0]
            for k in range(1, n_mp):
                total = total + first[k]
            mid[...] = total
        else:
            mid[...] = first[...]
        second[dp] = mid[dp] if reduces else mid[...]
        copies = []
        for k in range(1, n_dp):
            peer = lax.rem(dp + k, n_dp)
            copies.append(
                pltpu.make_async_remote_copy(
                    src_ref=mid.at[peer] if reduces else mid,
                    dst_ref=second.at[dp],
                    send_sem=s_dp.at[k - 1],
                    recv_sem=r_dp.at[k - 1],
                    device_id={"dp": peer},
                    device_id_type=MESH,
                )
            )
        for copy in copies:
            copy.start()
        for copy in copies:
            copy.wait()
        if reduces:
            total = second[0]
            for k in range(1, n_dp):
                total = total + second[k]
            out_ref[...] = total
        else:
            out_ref[...] = second[...]

    if reduces:
        out = (8, 128)
        first, mid, second = (n_mp, n_dp, 8, 128), (n_dp, 8, 128), (n_dp, 8, 128)
    else:
        out = (n_dp, n_mp, 8, 128)
        first, mid, second = (n_mp, 8, 128), (n_mp, 8, 128), (n_dp, n_mp, 8, 128)
    return pl.pallas_call(
        kernel,
        out_shape=jax.ShapeDtypeStruct(out, jnp.float32),
        in_specs=[VMEM],
        out_specs=VMEM,
        scratch_shapes=[
            pltpu.VMEM(first, jnp.float32),
            pltpu.VMEM(second, jnp.float32),
            pltpu.VMEM(mid, jnp.float32),
            pltpu.SemaphoreType.DMA((peers_mp,)),
            pltpu.SemaphoreType.DMA((peers_mp,)),
            pltpu.SemaphoreType.DMA((peers_dp,)),
            pltpu.SemaphoreType.DMA((peers_dp,)),
        ],
        compiler_params=pltpu.CompilerParams(collective_id=collective_id, has_side_effects=True),
        name="sum_small" if reduces else "gather_small",
    )(table)


def gather_gains(n_dp, n_mp, gains, collective_id):
    local = gains.shape[1]
    flat = jnp.pad(gains.reshape(1, 2 * local), ((0, 7), (0, 128 - 2 * local)))
    whole = small_exchange(n_dp, n_mp, flat, False, collective_id)
    rows = whole[:, :, 0, : 2 * local].reshape(n_dp * n_mp, 2, local)
    return rows.transpose(1, 0, 2).reshape(2, n_dp * n_mp * local)


def scatter_gains(n_dp, n_mp, partial, collective_id):
    local = partial.shape[1] // (n_dp * n_mp)
    table = partial.reshape(2, n_dp, n_mp, local).transpose(2, 1, 0, 3)
    table = table.reshape(n_mp, n_dp, 1, 2 * local)
    table = jnp.pad(table, ((0, 0), (0, 0), (0, 7), (0, 128 - 2 * local)))
    out = small_exchange(n_dp, n_mp, table, True, collective_id)
    return out[0, : 2 * local].reshape(2, local)


def rope_tables(length, half_dim):
    positions = jnp.arange(length, dtype=jnp.float32)[:, None]
    inverse_freq = rope_base ** (-jnp.arange(half_dim, dtype=jnp.float32) / half_dim)
    angles = positions * inverse_freq[None, :]
    return (jnp.cos(angles)[:, None, :], jnp.sin(angles)[:, None, :])


def rotate(values, cosine, sine_tab):
    half_dim = values.shape[-1] // 2
    first, second = (values[..., :half_dim], values[..., half_dim:])
    return jnp.concatenate(
        [first * cosine - second * sine_tab, second * cosine + first * sine_tab], axis=-1
    )


def unrotate(gradient, cosine, sine_tab):
    half_dim = gradient.shape[-1] // 2
    first, second = (gradient[..., :half_dim], gradient[..., half_dim:])
    return jnp.concatenate(
        [first * cosine + second * sine_tab, second * cosine - first * sine_tab], axis=-1
    )


def update(weight, moment, average, gradient, step_size):
    moment_new = momentum_decay * moment + (1.0 - momentum_decay) * gradient
    weight_new = weight - step_size * (
        (1.0 - momentum_decay) * gradient + momentum_decay * moment_new
    )
    average_new = average_decay * average + (1.0 - average_decay) * weight_new
    return (weight_new, moment_new, average_new)


def dot_t(left, right):
    return lax.dot_general(
        left, right, (((1,), (1,)), ((), ())), preferred_element_type=jnp.float32
    )


def t_dot(left, right):
    return lax.dot_general(
        left, right, (((0,), (0,)), ((), ())), preferred_element_type=jnp.float32
    )


def dot(left, right):
    return jnp.dot(left, right, preferred_element_type=jnp.float32)


def per_device(
    n_dp,
    n_mp,
    tokens,
    cotangent,
    valid_counts,
    w_qkv,
    w_out,
    w_gu,
    w_down,
    gains,
    mom_qkv,
    mom_out,
    mom_gu,
    mom_down,
    mom_gains,
    avg_qkv,
    avg_out,
    avg_gu,
    avg_down,
    avg_gains,
):
    half = jnp.bfloat16
    row_count, width = tokens.shape
    owned, _, local_width = w_qkv.shape
    hidden = w_gu.shape[2]
    heads_here = local_width // HDIM
    block_len = min(512, SEQ)
    block_total = SEQ // block_len
    score_scale = 1.0 / math.sqrt(HDIM)
    score_shift = -math.log(SEQ)
    valid_len = valid_counts[0]

    attn_part = jnp.concatenate(
        [w_qkv.reshape(owned, 3 * local_width), w_out.T], axis=1
    ).astype(half)
    attn_w = lax.all_gather(attn_part, "dp", axis=0, tiled=True)
    ffn_part = jnp.concatenate([w_gu.reshape(owned, 2 * hidden), w_down.T], axis=1).astype(half)
    ffn_w = lax.all_gather(ffn_part, "dp", axis=0, tiled=True)
    qkv_w, out_wt = attn_w[:, : 3 * local_width], attn_w[:, 3 * local_width :]
    gu_w, down_wt = ffn_w[:, : 2 * hidden], ffn_w[:, 2 * hidden :]

    gain_all = gather_gains(n_dp, n_mp, gains, 0)
    row_ids = lax.axis_index("mp") * row_count + jnp.arange(row_count, dtype=jnp.int32)
    live_rows = (row_ids < valid_len).astype(jnp.float32)[:, None]
    xin = tokens.astype(jnp.float32)
    inverse = lax.rsqrt(jnp.mean(xin * xin, axis=1, keepdims=True) + norm_eps)
    normed_first = (xin * inverse * gain_all[0][None, :]).astype(half)
    h_first = gather_rows(n_mp, normed_first, 1)
    out_grad = cotangent.astype(jnp.float32) * live_rows
    branch_grad = lax.all_gather(out_grad.astype(half), "mp", axis=0, tiled=True)

    joined = dot(h_first, qkv_w)
    cosine, sine_tab = rope_tables(SEQ, HDIM // 2)
    parts = [
        joined[:, k * local_width : (k + 1) * local_width].reshape(SEQ, heads_here, HDIM)
        for k in range(3)
    ]
    queries = rotate(parts[0], cosine, sine_tab).astype(half)
    keys = rotate(parts[1], cosine, sine_tab).astype(half)
    values = parts[2].astype(half)
    key_pos = jnp.arange(SEQ, dtype=jnp.int32)

    def probabilities(query_blk, offset):
        raw = jnp.einsum("qhd,khd->hqk", query_blk, keys, preferred_element_type=jnp.float32)
        query_pos = offset + jnp.arange(block_len, dtype=jnp.int32)
        allowed = (key_pos[None, :] <= query_pos[:, None]) & (key_pos[None, :] < valid_len)
        return jax.nn.sigmoid(raw * score_scale + score_shift) * allowed.astype(jnp.float32)[None]

    def attend(block_idx):
        offset = block_idx * block_len
        query_blk = lax.dynamic_slice_in_dim(queries, offset, block_len, 0)
        attn_prob = probabilities(query_blk, offset).astype(half)
        return jnp.einsum(
            "hqk,khd->qhd", attn_prob, values, preferred_element_type=jnp.float32
        ).astype(half)

    mixed = lax.map(attend, jnp.arange(block_total, dtype=jnp.int32)).reshape(SEQ, local_width)
    second, h_second = scatter_rows(
        n_mp, [(mixed, out_wt, True)], [xin], "forward", gain_all[1:2], 2
    )

    gate_up = dot(h_second, gu_w)
    gate_val, up_val = gate_up[:, :hidden], gate_up[:, hidden:]
    act = (jax.nn.silu(gate_val) * up_val).astype(half)
    ffn_out = lax.psum_scatter(
        dot_t(act, down_wt).astype(half), "mp", scatter_dimension=0, tiled=True
    )
    block_out = (second + ffn_out.astype(jnp.float32)).astype(half)
    act_grad = dot(branch_grad, down_wt)
    sigma = jax.nn.sigmoid(gate_val)
    gate_grad = act_grad * up_val * sigma * (1.0 + gate_val * (1.0 - sigma))
    up_grad = act_grad * gate_val * sigma
    gu_grad = jnp.concatenate([gate_grad, up_grad], axis=1).astype(half)
    grad_ffn = jnp.concatenate(
        [t_dot(h_second, gu_grad).astype(half), t_dot(branch_grad, act).astype(half)], axis=1
    )
    sum_ffn = lax.psum_scatter(grad_ffn, "dp", scatter_dimension=0, tiled=True)
    second_grad, gain_two, attn_grad = scatter_rows(
        n_mp, [(gu_grad, gu_w, True)], [second, out_grad], "backward", gain_all[1:2], 3
    )

    mixed_grad = dot(attn_grad, out_wt).astype(half).reshape(SEQ, heads_here, HDIM)
    grad_out = t_dot(attn_grad, mixed).astype(half)

    def back_block(carried, block_idx):
        key_grad, value_grad = carried
        offset = block_idx * block_len
        query_blk = lax.dynamic_slice_in_dim(queries, offset, block_len, 0)
        mixed_blk = lax.dynamic_slice_in_dim(mixed_grad, offset, block_len, 0)
        attn_prob = probabilities(query_blk, offset)
        prob_grad = jnp.einsum(
            "qhd,khd->hqk", mixed_blk, values, preferred_element_type=jnp.float32
        )
        value_grad = value_grad + jnp.einsum(
            "hqk,qhd->khd",
            attn_prob.astype(half),
            mixed_blk,
            preferred_element_type=jnp.float32,
        )
        score_grad = (prob_grad * attn_prob * (1.0 - attn_prob) * score_scale).astype(half)
        query_grad = jnp.einsum(
            "hqk,khd->qhd", score_grad, keys, preferred_element_type=jnp.float32
        )
        key_grad = key_grad + jnp.einsum(
            "hqk,qhd->khd", score_grad, query_blk, preferred_element_type=jnp.float32
        )
        return ((key_grad, value_grad), query_grad)

    zeros_kv = jnp.zeros((SEQ, heads_here, HDIM), jnp.float32)
    (key_total, value_total), query_blocks = lax.scan(
        back_block, (zeros_kv, zeros_kv), jnp.arange(block_total, dtype=jnp.int32)
    )
    query_total = query_blocks.reshape(SEQ, heads_here, HDIM)
    joined_grad = jnp.concatenate(
        [
            unrotate(query_total, cosine, sine_tab).reshape(SEQ, local_width),
            unrotate(key_total, cosine, sine_tab).reshape(SEQ, local_width),
            value_total.reshape(SEQ, local_width),
        ],
        axis=1,
    ).astype(half)
    grad_attn = jnp.concatenate([t_dot(h_first, joined_grad).astype(half), grad_out], axis=1)
    sum_attn = lax.psum_scatter(grad_attn, "dp", scatter_dimension=0, tiled=True)
    input_grad, gain_one = scatter_rows(
        n_mp, [(joined_grad, qkv_w, True)], [xin, second_grad], "last", gain_all[0:1], 4
    )
    gain_partial = jnp.stack([gain_one.sum(axis=0), gain_two.sum(axis=0)], axis=0)
    sum_gains = scatter_gains(n_dp, n_mp, gain_partial, 5)

    total_rows = SEQ * n_dp
    matrix_rate = step_rate / math.sqrt(total_rows)
    scale_rate = gain_rate / math.sqrt(total_rows)
    sum_attn = sum_attn.astype(jnp.float32)
    sum_ffn = sum_ffn.astype(jnp.float32)
    sum_qkv = sum_attn[:, : 3 * local_width].reshape(owned, 3, local_width)
    sum_out = sum_attn[:, 3 * local_width :].T
    sum_gu = sum_ffn[:, : 2 * hidden].reshape(owned, 2, hidden)
    sum_down = sum_ffn[:, 2 * hidden :].T
    new_qkv, next_mom_qkv, next_avg_qkv = update(w_qkv, mom_qkv, avg_qkv, sum_qkv, matrix_rate)
    new_out, next_mom_out, next_avg_out = update(w_out, mom_out, avg_out, sum_out, matrix_rate)
    new_gu, next_mom_gu, next_avg_gu = update(w_gu, mom_gu, avg_gu, sum_gu, matrix_rate)
    new_down, next_mom_down, next_avg_down = update(
        w_down, mom_down, avg_down, sum_down, matrix_rate
    )
    new_gains, next_mom_gains, next_avg_gains = update(
        gains, mom_gains, avg_gains, sum_gains, scale_rate
    )
    return (
        block_out,
        input_grad,
        new_qkv,
        new_out,
        new_gu,
        new_down,
        new_gains,
        next_mom_qkv,
        next_mom_out,
        next_mom_gu,
        next_mom_down,
        next_mom_gains,
        next_avg_qkv,
        next_avg_out,
        next_avg_gu,
        next_avg_down,
        next_avg_gains,
        new_qkv.astype(half),
        new_out.astype(half),
        new_gu.astype(half),
        new_down.astype(half),
    )


def solution(mesh):
    rows, one = P(("dp", "mp"), None), P("dp")
    tall, wide, spread = P("dp", None, "mp"), P("mp", "dp"), P(None, ("dp", "mp"))
    weights = (tall, wide, tall, wide)
    return jax.shard_map(
        functools.partial(per_device, mesh.shape["dp"], mesh.shape["mp"]),
        mesh=mesh,
        in_specs=(rows, rows, one, *((*weights, spread) * 3)),
        out_specs=(rows, rows, *((*weights, spread) * 3), *weights),
        check_vma=False,
    )
```

time: 1850 us -> 1030 us (0.56)
  waiting for transfers between devices: 1380 us -> 45.2 us
  Pallas kernels: 0 us -> 567 us
  blocking collectives: 70 us -> 0 us
  matrix products: 222 us -> 178 us
  other arithmetic: 77 us -> 114 us
  local copies, waits for them, and re-layouts: 70.2 us -> 98.5 us
    pallas_call x0 -> x6, Pallas kernels: none -> 567 us  [the longest x3 468 us: scatter_rows(): pl.pallas_call(kernel, out_shape=out_shape, in_specs=[VMEM] * (2 * count...]
    all_gather x8 -> x3, waiting for transfers between devices: 482 us -> 0.02 us  [the longest x1 0.02 us: per_device(): ffn_w = lax.all_gather(ffn_part, 'dp', axis=0, tiled=True)]
    psum x1 -> x0, waiting for transfers between devices: 401 us -> none  [per_device(): lax.psum(grad_qkv.astype(jnp.bfloat16), 'dp').astype(jnp.float32)]
    reduce_scatter x4 -> x3, waiting for transfers between devices: 371 us -> 45.1 us  [the longest x1 45.1 us: per_device(): sum_ffn = lax.psum_scatter(grad_ffn, 'dp', scatter_dimension=0, tiled=True)]
    unnamed x15 -> x6, waiting for transfers between devices: 126 us -> 0.1 us
    all_gather x1 -> x0, blocking collectives: 70 us -> none  [per_device(): gain_all = lax.all_gather(gains, ('dp', 'mp'), axis=1, tiled=True)]
    dot_general x14 -> x11, matrix products: 181 us -> 134 us  [the longest x4 61.6 us: dot(): return jnp.dot(left, right, preferred_element_type=jnp.float32)]
    concatenate x2 -> x6, other arithmetic: 2.38 us -> 38.8 us  [the longest x1 17.9 us: per_device(): jnp.concatenate([t_dot(h_second, gu_grad).astype(half), t_dot(branch_grad...]
  transfers between devices with their start and end apart: 14 -> 6, of which waited for: 13 -> 1; matrix products, arithmetic and copies ran while one was open for 9% -> 28% of each run, Pallas kernels for 0% -> 56%
where the time goes in v1:
time: 1030 us; the launch traced here: 1020 us
  Pallas kernels  567 us (55%)
  matrix products  178 us (17%)
  other arithmetic  114 us (11%)
  local copies, waits for them, and re-layouts  98.5 us (10%)
  waiting for transfers between devices  45.2 us (4%)
  between operations  15.9 us (2%)
    pallas_call x3, Pallas kernels, scatter_rows(): pl.pallas_call(kernel, out_shape=out_shape, in_specs=[VMEM] * (2 * count...  468 us
    pallas_call x1, Pallas kernels, gather_rows(): pl.pallas_call(kernel, out_shape=jax.ShapeDtypeStruct((n * rows, width),...  74.4 us
    dot_general x4, matrix products, dot(): return jnp.dot(left, right, preferred_element_type=jnp.float32)  61.6 us
    dot_general x4, matrix products, t_dot(): lax.dot_general(left, right, (((0,), (0,)), ((), ())), preferred_element_...  52.5 us
    reduce_scatter x1, waiting for transfers between devices, per_device(): sum_ffn = lax.psum_scatter(grad_ffn, 'dp', scatter_dimension=0, tiled=True)  45.1 us
    unnamed x88, local copies, waits for them, and re-layouts  33.1 us
    pallas_call x2, Pallas kernels, small_exchange(): pl.pallas_call(kernel, out_shape=jax.ShapeDtypeStruct(out, jnp.float32),...  24.8 us
  transfers between devices with their start and end apart: 6, of which 1 were waited for; matrix products, arithmetic and copies ran while one was open for 28% of the time, Pallas kernels for 56%

profile of v1, /device:TPU:0, one launch (start us, length us, event | category | flops | bytes accessed | tf_op | source)
XLA Modules:
  0.0 1021.4 jit_solution(8282086297653928209)
XLA Ops:
  25.9 13.2 %gather_small.1 = f32[8,4,8,128]{3,2,1,0:T(8,128)} custom-call(f32[8,128]{1,0:T(8,128)} %pad.8.in_ref), custom_call_target="tpu_custom_call" | custom-call | tf_op jit(solution)/shard_map/gather_small/pallas_call | solution.py:483
  41.6 74.4 %gather_rows.1 = bf16[1024,2048]{1,0:T(8,128)(2,1)} custom-call(bf16[256,2048]{1,0:T(8,128)(2,1)} %multiply_convert_fusion.10.own_ref), custom_call_target="tpu_custom_call" | custom-call | bytes 209715200 | tf_op jit(solution)/shard_map/gather_rows/pallas_call | solution.py:152
  119.4 10.0 fusion.49
  147.6 21.1 %while.28 = (s32[]{:T(128)}, bf16[2,512,4,128]{3,2,1,0:T(4,128)(2,1)}, s32[2]{0:T(128)S(1)}, bf16[1024,4,128]{2,0,1:T(8,128)(2,1)}, bf16[1024,4,128]{2,1,0:T(4,1...) while((s32[]{:T(128)}, ...), condition=%wide.region_2.3_spmd.clone.clone, body=%wide.region_1.2_spmd.clone.clone.sunk | while | flops 1090258432 | bytes 8395443 | solution.py:644
  174.2 194.4 %scatter_forward.1 = (f32[256,2048]{1,0:T(8,128)}, bf16[1024,2048]{1,0:T(8,128)(2,1)}) custom-call(bf16[1024,512]{1,0:T(8,128)(2,1)} %bitcast.125, bf16[2048,512]{1,0:T(8,128)(2,1)} %slice.120.refs_1_, f32[1,2048]{1,0:T(1,128)} %slice.96.refs_2_, f32[256,2048]{1,0:T(8,128)} %convert_element_type.107.refs_3_), custom_call_target="tpu_custom_call" | custom-call | flops 2147483648 | bytes 300000000 | tf_op jit(solution)/shard_map/scatter_forward/pallas_call | solution.py:392
  368.6 23.4 %fusion.51 = f32[1024,4096]{1,0:T(8,128)} fusion(bf16[1024,2048]{1,0:T(8,128)(2,1)} %get-tuple-element.137, bf16[2048,6144]{1,0:T(8,128)(2,1)} %all-gather.6.cloned.1.call-done), kind=kOutput, calls=%fused_computation.119 | convolution fusion | flops 17179869184 | bytes 37748736 | tf_op jit(solution)/shard_map/dot_general | solution.py:564
  392.0 21.8 %multiply_convert_fusion.8 = (bf16[1024,2048]{1,0:T(8,128)(2,1)}, bf16[1024,2048]{1,0:T(8,128)(2,1)}, bf16[1024,2048]{1,0:T(8,128)(2,1)}) fusion(f32[1024,4096]{1,0:T(8,128)} %fusion.51, bf16[1024,2048]{1,0:T(8,128)(2,1)} %all-gather.8.cloned.1.call-done, bf16[2048,6144]{1,0:T(8,128)(2,1)} %all-gather.6.cloned.1.call-done), kind=kOutput, calls=%fused_computation.45 | convolution fusion | flops 8623489024 | bytes 41943040 | tf_op jit(solution)/shard_map/dot_general | solution.py:564
  413.8 14.2 %fusion.39 = bf16[1024,2048]{1,0:T(8,128)(2,1)} fusion(bf16[1024,2048]{1,0:T(8,128)(2,1)} %get-tuple-element.370, bf16[2048,6144]{1,0:T(8,128)(2,1)} %all-gather.6.cloned.1.call-done), kind=kOutput, calls=%fused_computation.58 | convolution fusion | flops 8592031744 | bytes 16777216 | tf_op jit(solution)/shard_map/dot_general | solution.py:552
  428.1 7.8 pad_maximum_fusion.1.refs_0_
  435.9 14.0 %slice.122.refs_1_ = bf16[2048,4096]{1,0:T(8,128)(2,1)} slice(bf16[2048,6144]{1,0:T(8,128)(2,1)} %all-gather.6.cloned.1.call-done), slice={[0:2048], [0:4096]} | slice | bytes 33554432 | tf_op jit(solution)/shard_map/slice | solution.py:607
  450.0 193.9 %scatter_backward.1 = (f32[256,2048]{1,0:T(8,128)}, f32[8,2048]{1,0:T(8,128)}, bf16[1024,2048]{1,0:T(8,128)(2,1)}) custom-call(bf16[1024,4096]{1,0:T(8,128)(2,1)} %pad_maximum_fusion.1.refs_0_, bf16[2048,4096]{1,0:T(8,128)(2,1)} %slice.122.refs_1_, f32[1,2048]{1,0:T(1,128)} %slice.96.refs_2_, f32[256,2048]{1,0:T(8,128)} %get-tuple-element.136.refs_3_, ...), custom_call_target="tpu_custom_call" | custom-call | flops 17179869184 | bytes 300000000 | tf_op jit(solution)/shard_map/scatter_backward/pallas_call | solution.py:392
  643.9 6.3 convolution_convert_fusion.4
  650.2 49.2 %while.29 = (s32[]{:T(128)}, f32[1024,4,128]{0,2,1:T(8,128)S(1)}, f32[1024,4,128]{0,2,1:T(8,128)}, f32[2,512,4,128]{3,1,0,2:T(8,128)}, s32[2]{0:T(128)S(1)}, /*i...) while((s32[]{:T(128)}, f32[1024,4,128]{0,2,1:T(8,128)S(1)}, ...), condition=%wide.region_5.6_spmd.clone.clone, body=%wide.region_4.5_spmd.clone.clone.sunk | while | flops 2713191936 | bytes 140516224 | solution.py:697
  716.4 9.0 convolution_convert_fusion.2
  725.4 8.3 pad_maximum_fusion.2
  733.8 14.1 %convolution_convert_fusion.1 = bf16[2048,2048]{1,0:T(8,128)(2,1)} fusion(bf16[1024,2048]{1,0:T(8,128)(2,1)} %all-gather.8.cloned.1.call-done, bf16[1024,2048]{1,0:T(8,128)(2,1)} %get-tuple-element.370), kind=kOutput, calls=%fused_computation.48 | convolution fusion | flops 8594128896 | bytes 16777216 | tf_op jit(solution)/shard_map/dot_general | solution.py:558
  747.9 25.6 %convolution_convert_fusion = bf16[2048,4096]{1,0:T(8,128)(2,1)} fusion(bf16[1024,2048]{1,0:T(8,128)(2,1)} %get-tuple-element.137, bf16[1024,2048]{1,0:T(8,128)(2,1)} %get-tuple-element.369, bf16[1024,2048]{1,0:T(8,128)(2,1)} %get-tuple-element.368), kind=kOutput, calls=%fused_computation.41 | convolution fusion | flops 17205035008 | bytes 29360128 | tf_op jit(solution)/shard_map/dot_general | solution.py:558
  773.5 17.9 %pad_maximum_fusion = bf16[2048,6144]{1,0:T(8,128)(2,1)} fusion(bf16[2048,2048]{1,0:T(8,128)(2,1)} %convolution_convert_fusion.1, bf16[2048,4096]{1,0:T(8,128)(2,1)} %convolution_convert_fusion), kind=kLoop, calls=%fused_computation.40 | loop fusion | flops 50331648 | bytes 50331648 | tf_op jit(solution)/shard_map/concatenate | solution.py:661
  806.3 79.6 %scatter_last.1 = (f32[256,2048]{1,0:T(8,128)}, f32[8,2048]{1,0:T(8,128)}) custom-call(bf16[1024,1536]{1,0:T(8,128)(2,1)} %pad_maximum_fusion.4.refs_0_, bf16[2048,1536]{1,0:T(8,128)(2,1)} %slice.112.refs_1_, f32[1,2048]{1,0:T(1,128)} %slice.105.refs_2_, f32[256,2048]{1,0:T(8,128)} %convert_element_type.107.refs_3_, f32[256,2048]{1,0:T(8,128)} %get-tuple-element.142.refs_4_), custom_call_target="tpu_custom_call" | custom-call | flops 6442450944 | bytes 300000000 | tf_op jit(solution)/shard_map/scatter_last/pallas_call | solution.py:392
  887.8 11.6 %sum_small.1 = f32[8,128]{1,0:T(8,128)} custom-call(f32[4,8,8,128]{3,2,1,0:T(8,128)} %pad.9.in_ref), custom_call_target="tpu_custom_call" | custom-call | tf_op jit(solution)/shard_map/sum_small/pallas_call | solution.py:483
  919.2 45.1 %reduce-scatter.8.cloned.1.call-done = bf16[256,6144]{1,0:T(8,128)(2,1)} async-done(((bf16[2048,6144]{1,0:T(8,128)(2,1)}), bf16[256,6144]{1,0:T(8,128)(2,1)}) %reduce-scatter.8.cloned.1.call-update) | async-done | bytes 3145744 | tf_op jit(solution)/shard_map/reduce_scatter | solution.py:664
  972.2 6.6 mul.514
  995.2 11.1 %fusion.54 = (bf16[256,2,2048]{2,1,0:T(2,128)(2,1)}, f32[256,2,2048]{2,1,0:T(2,128)S(1)}, f32[256,2,2048]{2,1,0:T(2,128)}) fusion(f32[256,2,2048]{2,1,0:T(2,128)} %param.27, f32[256,2,2048]{2,1,0:T(2,128)} %mul.514, f32[256,2,2048]{2,1,0:T(2,128)} %param.32), kind=kLoop, calls=%fused_computation.122 | loop fusion | flops 7340032 | bytes 23068672 | tf_op jit(solution)/shard_map/convert_element_type | solution.py:755
  1006.4 6.4 multiply_add_fusion
  (229 shorter events, 193.2 us)
Async XLA Ops:
  7.2 112.2 %all-gather.4.cloned.1.call-start = ((), (), s32[]{:S(2)}) async-start(), calls=%async_computation.3 | async-start | bytes 9437184 | tf_op jit(solution)/shard_map/all_gather | solution.py:603
  10.5 358.1 %all-gather.6.cloned.1.call-start = ((), (), s32[]{:S(2)}) async-start(), calls=%async_computation.4 | async-start | bytes 28311552 | tf_op jit(solution)/shard_map/all_gather | solution.py:605
  12.5 5.9 copy-start.7
  20.5 371.6 %all-gather.8.cloned.1.call-start = ((), (), s32[]{:S(2)}) async-start(), calls=%async_computation.6 | async-start | bytes 5242880 | tf_op jit(solution)/shard_map/all_gather | solution.py:617
  23.3 877.5 %reduce-scatter.4.cloned.1.call-start = ((), (), s32[]{:S(2)}) async-start(), calls=%async_computation.5 | async-start | bytes 5242880 | tf_op jit(solution)/shard_map/reduce_scatter | solution.py:652
  40.2 78.6 %copy-start.33 = (f32[1,32,64]{2,1,0:T(8,128)}, f32[1,32,64]{2,1,0:T(8,128)S(1)}, u32[]{:S(2)}) copy-start(f32[1,32,64]{2,1,0:T(8,128)S(1)} %get-tuple-element.392) | copy-start | bytes 24580
  428.1 475.2 %reduce-scatter.6.cloned.1.call-start = ((), (), s32[]{:S(2)}) async-start(), calls=%async_computation.7 | async-start | bytes 9437184 | tf_op jit(solution)/shard_map/reduce_scatter | solution.py:710
  643.9 6.4 copy-start.2
  652.9 7.2 copy-start.3
  664.0 8.0 slice-start
  664.0 8.0 slice-start.1
  676.5 7.2 copy-start.3
  687.6 8.0 slice-start
  687.6 8.0 slice-start.1
  733.7 230.6 %reduce-scatter.8.cloned.1.call-start = ((), (), s32[]{:S(2)}) async-start(), calls=%async_computation.8 | async-start | bytes 28311552 | tf_op jit(solution)/shard_map/reduce_scatter | solution.py:664
  806.3 80.6 %copy-start.35 = (f32[8,2048]{1,0:T(8,128)S(1)}, f32[8,2048]{1,0:T(8,128)}, u32[]{:S(2)}) copy-start(f32[8,2048]{1,0:T(8,128)} %get-tuple-element.145) | copy-start | bytes 196612
  806.3 93.9 %copy-start.37 = (f32[2,64]{1,0:T(2,128)S(1)}, f32[2,64]{1,0:T(2,128)}, u32[]{:S(2)}) copy-start(f32[2,64]{1,0:T(2,128)} %param.29) | copy-start | bytes 1540
  806.3 93.9 %copy-start.38 = (f32[2,64]{1,0:T(2,128)S(1)}, f32[2,64]{1,0:T(2,128)}, u32[]{:S(2)}) copy-start(f32[2,64]{1,0:T(2,128)} %param.39) | copy-start | bytes 1540
  806.3 93.9 %copy-start.39 = (f32[2,64]{1,0:T(2,128)S(1)}, f32[2,64]{1,0:T(2,128)}, u32[]{:S(2)}) copy-start(f32[2,64]{1,0:T(2,128)} %param.34) | copy-start | bytes 1540
  806.3 94.5 %copy-start.24 = (f32[256,2048]{1,0:T(8,128)S(1)}, f32[256,2048]{1,0:T(8,128)}, u32[]{:S(2)}) copy-start(f32[256,2048]{1,0:T(8,128)} %get-tuple-element.136.refs_3_) | copy-start | bytes 6291460
  904.7 7.4 copy-start.32
  995.2 11.2 %copy-start.20 = (f32[256,2,2048]{2,1,0:T(2,128)S(1)}, f32[256,2,2048]{2,1,0:T(2,128)}, u32[]{:S(2)}) copy-start(f32[256,2,2048]{2,1,0:T(2,128)} %param.37) | copy-start | bytes 12582916
  1006.3 6.4 copy-start.8
  1006.3 6.4 copy-start.25
  (31 other events, 97.4 us)
Sparse Core Ops, SparseCore 0:
  10.7 57.7 all-gather.3
  70.9 125.3 all-gather.5
  198.5 135.6 all-gather.7
  428.2 116.2 reduce-scatter.3
  733.8 69.7 reduce-scatter.5
  807.1 157.1 reduce-scatter.7

commit v2 on v1

--- a/solution.py
+++ b/solution.py
@@ -163,37 +163,75 @@
     )(own)
 
 
-def scatter_rows(n, pairs, own_rows, epilogue, gains_row, collective_id, extra=None, chunks=2):
-    total_rows = pairs[0][0].shape[0]
+def dot_t(left, right):
+    return lax.dot_general(
+        left, right, (((1,), (1,)), ((), ())), preferred_element_type=jnp.float32
+    )
+
+
+def t_dot(left, right):
+    return lax.dot_general(
+        left, right, (((0,), (0,)), ((), ())), preferred_element_type=jnp.float32
+    )
+
+
+def dot(left, right):
+    return jnp.dot(left, right, preferred_element_type=jnp.float32)
+
+
+def probability(raw):
+    return 1.0 / (1.0 + jnp.exp(math.log(SEQ) - raw * (1.0 / math.sqrt(HDIM))))
+
+
+def rotated(values, cosine, sine, backward=False):
+    turned = pltpu.roll(values, HDIM // 2, 1) * sine
+    return values * cosine - turned if backward else values * cosine + turned
+
+
+def scatter_rows(
+    n, lhs, rhs, rhs_start, own_rows, epilogue, gains_row, collective_id, heads=None, extra=None, chunks=2
+):
+    total_rows = lhs[0].shape[0]
     rows = total_rows // n
     width = gains_row.shape[1]
     size = rows // chunks
     tile = 512
-    gathers = epilogue != "last"
-    lhs_args = [p[0] for p in pairs]
-    rhs_args = [p[1] for p in pairs]
-    flips = [p[2] for p in pairs]
-    count = len(pairs)
+    has_norm, has_gain = epilogue in ("forward", "backward"), epilogue in ("backward", "last")
+    count = len(lhs)
     block = 32
+    if heads is not None:
+        inner_width = lhs[0].shape[1] // 3
+        head_count = inner_width // HDIM
+        pieces = [inner_width]
+    else:
+        pieces = [a.shape[1] for a in lhs]
+    depth = sum(pieces)
 
     def kernel(*refs):
         refs = list(refs)
-        take = lambda k: [refs.pop(0) for _ in range(k)]
-        lhs, rhs = take(count), take(count)
+
+        def take(k):
+            return [refs.pop(0) for _ in range(k)]
+
+        left_refs = take(count)
+        (right_hbm,) = take(1)
         (gain_ref,) = take(1)
         own = take(len(own_rows))
+        if heads is not None:
+            cosine_ref, sine_ref, mask_ref = take(3)
         extra_ref = take(1)[0] if extra is not None else None
-        outs = take(2 if epilogue != "forward" else 1)
-        whole = take(1)[0] if gathers else None
+        outs = take(1 + has_gain)
+        normed = take(1)[0] if has_norm else None
+        if heads is not None:
+            query_ref, key_ref, value_ref, mixed_ref = take(4)
         extra_whole = take(1)[0] if extra is not None else None
-        held, sent, part = take(3)
-        normed = take(1)[0] if gathers else None
-        send_sems, recv_sems = take(2)
-        gather = extra_gather = None
+        right, held, sent, part = take(4)
+        right_sem, send_sems, recv_sems = take(3)
         me = lax.axis_index("mp")
-        if gathers:
-            (local_sem,) = take(1)
-            gather = LineGather(n, rows, chunks, normed, whole, take(4))
+        fetch = pltpu.make_async_copy(
+            right_hbm.at[:, pl.ds(rhs_start, depth)], right, right_sem
+        )
+        fetch.start()
         if extra is not None:
             (extra_sem,) = take(1)
             extra_gather = LineGather(n, rows, 1, extra_ref, extra_whole, take(4))
@@ -202,22 +240,67 @@
         neighbour_barrier(n)
         if extra is not None:
             extra_gather.send_own(0)
+        if heads is not None:
+            turn = 128
+
+            def enter(i, carry):
+                span = rows_at(i * turn, turn)
+                cosine, sine = cosine_ref[span, :], sine_ref[span, :]
+                for h in range(head_count):
+                    cols = pl.ds(h * HDIM, HDIM)
+                    for k, target in ((0, query_ref), (1, key_ref)):
+                        piece = left_refs[0][span, pl.ds(k * inner_width + h * HDIM, HDIM)]
+                        target[span, cols] = rotated(piece, cosine, sine).astype(jnp.bfloat16)
+                value_ref[span, :] = left_refs[0][
+                    span, pl.ds(2 * inner_width, inner_width)
+                ].astype(jnp.bfloat16)
+                return carry
+
+            lax.fori_loop(0, total_rows // turn, enter, 0)
+        fetch.wait()
+
+        def attend(block_id):
+            span = rows_at(block_id * rows, rows)
+            row_pos = block_id * rows + lax.broadcasted_iota(jnp.int32, (rows, rows), 0)
+
+            def against(kb, totals):
+                other = rows_at(kb * rows, rows)
+                col_pos = kb * rows + lax.broadcasted_iota(jnp.int32, (rows, rows), 1)
+                allowed = jnp.where(col_pos <= row_pos, mask_ref[:, other], 0.0)
+                out = []
+                for h in range(head_count):
+                    cols = pl.ds(h * HDIM, HDIM)
+                    raw = dot_t(query_ref[span, cols], key_ref[other, cols])
+                    prob = probability(raw) * allowed
+                    out.append(
+                        totals[h]
+                        + jnp.dot(
+                            prob.astype(jnp.bfloat16),
+                            value_ref[other, cols],
+                            preferred_element_type=jnp.float32,
+                        )
+                    )
+                return tuple(out)
+
+            start = tuple(jnp.zeros((rows, HDIM), jnp.float32) for _ in range(head_count))
+            totals = lax.fori_loop(0, block_id + 1, against, start)
+            for h in range(head_count):
+                mixed_ref[span, pl.ds(h * HDIM, HDIM)] = totals[h].astype(jnp.bfloat16)
 
         def product(block_id):
+            if heads is not None:
+                attend(block_id)
+            sources = [mixed_ref] if heads is not None else left_refs
+
             def column(ct, carry):
                 cols = rows_at(ct * tile, tile)
-                total = None
-                for a, b, flip in zip(lhs, rhs, flips):
-                    left = a[rows_at(block_id * rows, rows), :]
-                    if flip:
-                        term = lax.dot_general(
-                            left,
-                            b[cols, :],
-                            (((1,), (1,)), ((), ())),
-                            preferred_element_type=jnp.float32,
-                        )
-                    else:
-                        term = jnp.dot(left, b[:, cols], preferred_element_type=jnp.float32)
+                total, start = None, 0
+                for source, piece in zip(sources, pieces):
+                    term = dot_t(
+                        source[rows_at(block_id * rows, rows), :],
+                        right[cols, pl.ds(start, piece)],
+                    )
+                    start += piece
                     total = term if total is None else total + term
                 part[:, cols] = total
                 return carry
@@ -286,7 +369,7 @@
 
         lax.fori_loop(1, n, step_of, 0)
         product(me)
-        if epilogue != "forward":
+        if has_gain:
             outs[1][...] = jnp.zeros_like(outs[1])
         for chunk in range(chunks):
 
@@ -307,7 +390,9 @@
                     me < n - 1, held[n, span, :].astype(jnp.float32), zero
                 )
                 gain = gain_ref[...]
-                if epilogue == "forward":
+                if epilogue == "residual":
+                    outs[0][span, :] = (own[0][span, :] + total).astype(jnp.bfloat16)
+                elif epilogue == "forward":
                     value = own[0][span, :] + total
                     outs[0][span, :] = value
                     inverse = lax.rsqrt(
@@ -327,25 +412,14 @@
                     outs[1][...] += jnp.sum(
                         (total * unit).reshape(block // 8, 8, width), axis=0
                     )
-                    if gathers:
+                    if has_norm:
                         normed[span, :] = result.astype(jnp.bfloat16)
                 return carry
 
             lax.fori_loop(0, size // block, body, 0)
-            if gathers:
-                gather.send_own(chunk)
-        if gathers:
-            local = pltpu.make_async_copy(
-                normed, whole.at[rows_at(me * rows, rows)], local_sem
-            )
-            local.start()
         if extra is not None:
             extra_gather.finish()
             extra_local.wait()
-        if gathers:
-            gather.forward_all()
-            gather.finish()
-            local.wait()
 
         def sends(step, carry):
             for chunk in range(chunks):
@@ -362,37 +436,45 @@
 
         lax.fori_loop(1, n, sends, 0)
 
-    out_shape = [jax.ShapeDtypeStruct((rows, width), jnp.float32)]
+    out_type = jnp.bfloat16 if epilogue == "residual" else jnp.float32
+    out_shape = [jax.ShapeDtypeStruct((rows, width), out_type)]
     out_specs = [VMEM]
-    if epilogue != "forward":
+    if has_gain:
         out_shape.append(jax.ShapeDtypeStruct((8, width), jnp.float32))
         out_specs.append(VMEM)
     scratch = [
+        pltpu.VMEM((width, depth), jnp.bfloat16),
         pltpu.VMEM((n + 1, rows, width), jnp.bfloat16),
         pltpu.VMEM((n, rows, width), jnp.bfloat16),
         pltpu.VMEM((rows, width), jnp.float32),
     ]
-    if gathers:
-        out_shape.append(jax.ShapeDtypeStruct((total_rows, width), jnp.bfloat16))
-        out_specs.append(ANY)
-        scratch.append(pltpu.VMEM((rows, width), jnp.bfloat16))
+    if has_norm:
+        out_shape.append(jax.ShapeDtypeStruct((rows, width), jnp.bfloat16))
+        out_specs.append(VMEM)
     scratch += [
+        pltpu.SemaphoreType.DMA,
         pltpu.SemaphoreType.DMA((n * chunks,)),
         pltpu.SemaphoreType.DMA(((n + 1) * chunks,)),
     ]
-    if gathers:
-        scratch += [pltpu.SemaphoreType.DMA] + gather_sems(n, chunks)
+    head_args = []
+    if heads is not None:
+        head_args = list(heads)
+        out_shape += [jax.ShapeDtypeStruct((total_rows, inner_width), jnp.bfloat16)] * 4
+        out_specs += [VMEM] * 4
     extra_args = []
     if extra is not None:
         out_shape.append(jax.ShapeDtypeStruct((total_rows, width), jnp.bfloat16))
         out_specs.append(ANY)
         scratch += [pltpu.SemaphoreType.DMA] + gather_sems(n, 1)
         extra_args = [extra]
-    flops = sum(2 * a.size * width for a in lhs_args)
+    flops = 2 * total_rows * depth * width
     return pl.pallas_call(
         kernel,
         out_shape=out_shape,
-        in_specs=[VMEM] * (2 * count + 1 + len(own_rows)) + [ANY] * len(extra_args),
+        in_specs=[VMEM] * count
+        + [ANY]
+        + [VMEM] * (1 + len(own_rows) + len(head_args))
+        + [ANY] * len(extra_args),
         out_specs=out_specs,
         scratch_shapes=scratch,
         compiler_params=pltpu.CompilerParams(
@@ -402,7 +484,58 @@
             flops=flops, bytes_accessed=300_000_000, transcendentals=0
         ),
         name="scatter_" + epilogue,
-    )(*lhs_args, *rhs_args, gains_row, *own_rows, *extra_args)
+    )(*lhs, rhs, gains_row, *own_rows, *head_args, *extra_args)
+
+
+def attention_backward(queries, keys, values, mixed_grad, cosine, sine, key_mask):
+    total_rows, inner_width = queries.shape
+    block = min(256, total_rows)
+
+    def kernel(q_ref, k_ref, v_ref, do_ref, cos_ref, sin_ref, mask_ref, dq_out, dk_out, dv_out, dk_ref, dv_ref):
+        dk_ref[...] = jnp.zeros_like(dk_ref)
+        dv_ref[...] = jnp.zeros_like(dv_ref)
+        for i in range(total_rows // block):
+            span = pl.ds(i * block, block)
+            upto = (i + 1) * block
+            shape = (upto, block)
+            key_pos = lax.broadcasted_iota(jnp.int32, shape, 0)
+            query_pos = i * block + lax.broadcasted_iota(jnp.int32, shape, 1)
+            allowed = jnp.where(key_pos <= query_pos, mask_ref[:upto, :], 0.0)
+            query, grad = q_ref[span, :], do_ref[span, :]
+            key = k_ref[:upto, :]
+            prob = probability(dot_t(key, query)) * allowed
+            prob_grad = dot_t(v_ref[:upto, :], grad)
+            dv_ref[:upto, :] += jnp.dot(
+                prob.astype(jnp.bfloat16), grad, preferred_element_type=jnp.float32
+            )
+            score_grad = (prob_grad * prob * (1.0 - prob) * (1.0 / math.sqrt(HDIM))).astype(
+                jnp.bfloat16
+            )
+            dk_ref[:upto, :] += jnp.dot(score_grad, query, preferred_element_type=jnp.float32)
+            dq = t_dot(score_grad, key)
+            dq_out[span, :] = rotated(
+                dq, cos_ref[span, :], sin_ref[span, :], True
+            ).astype(jnp.bfloat16)
+        dk_out[...] = rotated(dk_ref[...], cos_ref[...], sin_ref[...], True).astype(jnp.bfloat16)
+        dv_out[...] = dv_ref[...].astype(jnp.bfloat16)
+
+    head = pl.BlockSpec((total_rows, HDIM), lambda h: (0, h))
+    table = pl.BlockSpec((total_rows, HDIM), lambda h: (0, 0))
+    return pl.pallas_call(
+        kernel,
+        grid=(inner_width // HDIM,),
+        out_shape=[jax.ShapeDtypeStruct((total_rows, inner_width), jnp.bfloat16)] * 3,
+        in_specs=[head] * 4 + [table] * 2 + [pl.BlockSpec((total_rows, 1), lambda h: (0, 0))],
+        out_specs=[head] * 3,
+        scratch_shapes=[pltpu.VMEM((total_rows, HDIM), jnp.float32)] * 2,
+        compiler_params=pltpu.CompilerParams(vmem_limit_bytes=VMEM_LIMIT),
+        cost_estimate=pl.CostEstimate(
+            flops=8 * total_rows * total_rows * inner_width,
+            bytes_accessed=14 * total_rows * inner_width,
+            transcendentals=0,
+        ),
+        name="attention_backward",
+    )(queries, keys, values, mixed_grad, cosine, sine, key_mask)
 
 
 def small_exchange(n_dp, n_mp, table, reduces, collective_id):
@@ -520,23 +653,8 @@
     positions = jnp.arange(length, dtype=jnp.float32)[:, None]
     inverse_freq = rope_base ** (-jnp.arange(half_dim, dtype=jnp.float32) / half_dim)
     angles = positions * inverse_freq[None, :]
-    return (jnp.cos(angles)[:, None, :], jnp.sin(angles)[:, None, :])
-
-
-def rotate(values, cosine, sine_tab):
-    half_dim = values.shape[-1] // 2
-    first, second = (values[..., :half_dim], values[..., half_dim:])
-    return jnp.concatenate(
-        [first * cosine - second * sine_tab, second * cosine + first * sine_tab], axis=-1
-    )
-
-
-def unrotate(gradient, cosine, sine_tab):
-    half_dim = gradient.shape[-1] // 2
-    first, second = (gradient[..., :half_dim], gradient[..., half_dim:])
-    return jnp.concatenate(
-        [first * cosine + second * sine_tab, second * cosine - first * sine_tab], axis=-1
-    )
+    cosine, sine = jnp.cos(angles), jnp.sin(angles)
+    return jnp.concatenate([cosine, cosine], axis=1), jnp.concatenate([-sine, sine], axis=1)
 
 
 def update(weight, moment, average, gradient, step_size):
@@ -546,22 +664,6 @@
     )
     average_new = average_decay * average + (1.0 - average_decay) * weight_new
     return (weight_new, moment_new, average_new)
-
-
-def dot_t(left, right):
-    return lax.dot_general(
-        left, right, (((1,), (1,)), ((), ())), preferred_element_type=jnp.float32
-    )
-
-
-def t_dot(left, right):
-    return lax.dot_general(
-        left, right, (((0,), (0,)), ((), ())), preferred_element_type=jnp.float32
-    )
-
-
-def dot(left, right):
-    return jnp.dot(left, right, preferred_element_type=jnp.float32)
 
 
 def per_device(
@@ -590,11 +692,6 @@
     row_count, width = tokens.shape
     owned, _, local_width = w_qkv.shape
     hidden = w_gu.shape[2]
-    heads_here = local_width // HDIM
-    block_len = min(512, SEQ)
-    block_total = SEQ // block_len
-    score_scale = 1.0 / math.sqrt(HDIM)
-    score_shift = -math.log(SEQ)
     valid_len = valid_counts[0]
 
     attn_part = jnp.concatenate(
@@ -604,7 +701,7 @@
     ffn_part = jnp.concatenate([w_gu.reshape(owned, 2 * hidden), w_down.T], axis=1).astype(half)
     ffn_w = lax.all_gather(ffn_part, "dp", axis=0, tiled=True)
     qkv_w, out_wt = attn_w[:, : 3 * local_width], attn_w[:, 3 * local_width :]
-    gu_w, down_wt = ffn_w[:, : 2 * hidden], ffn_w[:, 2 * hidden :]
+    down_wt = ffn_w[:, 2 * hidden :]
 
     gain_all = gather_gains(n_dp, n_mp, gains, 0)
     row_ids = lax.axis_index("mp") * row_count + jnp.arange(row_count, dtype=jnp.int32)
@@ -614,102 +711,81 @@
     normed_first = (xin * inverse * gain_all[0][None, :]).astype(half)
     h_first = gather_rows(n_mp, normed_first, 1)
     out_grad = cotangent.astype(jnp.float32) * live_rows
-    branch_grad = lax.all_gather(out_grad.astype(half), "mp", axis=0, tiled=True)
+    cosine, sine = rope_tables(SEQ, HDIM // 2)
+    key_mask = (jnp.arange(SEQ, dtype=jnp.int32) < valid_len).astype(jnp.float32)
 
     joined = dot(h_first, qkv_w)
-    cosine, sine_tab = rope_tables(SEQ, HDIM // 2)
-    parts = [
-        joined[:, k * local_width : (k + 1) * local_width].reshape(SEQ, heads_here, HDIM)
-        for k in range(3)
-    ]
-    queries = rotate(parts[0], cosine, sine_tab).astype(half)
-    keys = rotate(parts[1], cosine, sine_tab).astype(half)
-    values = parts[2].astype(half)
-    key_pos = jnp.arange(SEQ, dtype=jnp.int32)
-
-    def probabilities(query_blk, offset):
-        raw = jnp.einsum("qhd,khd->hqk", query_blk, keys, preferred_element_type=jnp.float32)
-        query_pos = offset + jnp.arange(block_len, dtype=jnp.int32)
-        allowed = (key_pos[None, :] <= query_pos[:, None]) & (key_pos[None, :] < valid_len)
-        return jax.nn.sigmoid(raw * score_scale + score_shift) * allowed.astype(jnp.float32)[None]
-
-    def attend(block_idx):
-        offset = block_idx * block_len
-        query_blk = lax.dynamic_slice_in_dim(queries, offset, block_len, 0)
-        attn_prob = probabilities(query_blk, offset).astype(half)
-        return jnp.einsum(
-            "hqk,khd->qhd", attn_prob, values, preferred_element_type=jnp.float32
-        ).astype(half)
-
-    mixed = lax.map(attend, jnp.arange(block_total, dtype=jnp.int32)).reshape(SEQ, local_width)
-    second, h_second = scatter_rows(
-        n_mp, [(mixed, out_wt, True)], [xin], "forward", gain_all[1:2], 2
-    )
-
-    gate_up = dot(h_second, gu_w)
-    gate_val, up_val = gate_up[:, :hidden], gate_up[:, hidden:]
+    second, normed_second, queries, keys, values, mixed, branch_grad = scatter_rows(
+        n_mp,
+        [joined],
+        attn_w,
+        3 * local_width,
+        [xin],
+        "forward",
+        gain_all[1:2],
+        2,
+        heads=(cosine, sine, key_mask[None, :]),
+        extra=out_grad.astype(half),
+    )
+
+    h_second = gather_rows(n_mp, normed_second, 6)
+    gate_val = dot(h_second, ffn_w[:, :hidden])
+    up_val = dot(h_second, ffn_w[:, hidden : 2 * hidden])
     act = (jax.nn.silu(gate_val) * up_val).astype(half)
-    ffn_out = lax.psum_scatter(
-        dot_t(act, down_wt).astype(half), "mp", scatter_dimension=0, tiled=True
-    )
-    block_out = (second + ffn_out.astype(jnp.float32)).astype(half)
     act_grad = dot(branch_grad, down_wt)
     sigma = jax.nn.sigmoid(gate_val)
-    gate_grad = act_grad * up_val * sigma * (1.0 + gate_val * (1.0 - sigma))
-    up_grad = act_grad * gate_val * sigma
-    gu_grad = jnp.concatenate([gate_grad, up_grad], axis=1).astype(half)
-    grad_ffn = jnp.concatenate(
-        [t_dot(h_second, gu_grad).astype(half), t_dot(branch_grad, act).astype(half)], axis=1
-    )
+    gate_grad = (act_grad * up_val * sigma * (1.0 + gate_val * (1.0 - sigma))).astype(half)
+    up_grad = (act_grad * gate_val * sigma).astype(half)
+    grad_ffn = jnp.zeros((width, 3 * hidden), half)
+    for k, (a, b) in enumerate(
+        ((h_second, gate_grad), (h_second, up_grad), (branch_grad, act))
+    ):
+        grad_ffn = lax.dynamic_update_slice(grad_ffn, t_dot(a, b).astype(half), (0, k * hidden))
+    grad_ffn, gate_grad = lax.optimization_barrier((grad_ffn, gate_grad))
     sum_ffn = lax.psum_scatter(grad_ffn, "dp", scatter_dimension=0, tiled=True)
-    second_grad, gain_two, attn_grad = scatter_rows(
-        n_mp, [(gu_grad, gu_w, True)], [second, out_grad], "backward", gain_all[1:2], 3
-    )
-
-    mixed_grad = dot(attn_grad, out_wt).astype(half).reshape(SEQ, heads_here, HDIM)
-    grad_out = t_dot(attn_grad, mixed).astype(half)
-
-    def back_block(carried, block_idx):
-        key_grad, value_grad = carried
-        offset = block_idx * block_len
-        query_blk = lax.dynamic_slice_in_dim(queries, offset, block_len, 0)
-        mixed_blk = lax.dynamic_slice_in_dim(mixed_grad, offset, block_len, 0)
-        attn_prob = probabilities(query_blk, offset)
-        prob_grad = jnp.einsum(
-            "qhd,khd->hqk", mixed_blk, values, preferred_element_type=jnp.float32
+    second_grad, gain_two, own_grad = scatter_rows(
+        n_mp, [gate_grad, up_grad], ffn_w, 0, [second, out_grad], "backward", gain_all[1:2], 3
+    )
+    block_out, attn_grad = scatter_rows(
+        n_mp,
+        [act],
+        ffn_w,
+        2 * hidden,
+        [second],
+        "residual",
+        gain_all[1:2],
+        7,
+        extra=own_grad,
+    )
+
+    mixed_grad = dot(attn_grad, out_wt).astype(half)
+    joined_grad = attention_backward(
+        queries, keys, values, mixed_grad, cosine, sine, key_mask[:, None]
+    )
+    grad_attn = jnp.zeros((width, 4 * local_width), half)
+    for k, (a, b) in enumerate(
+        (
+            (h_first, joined_grad[0]),
+            (h_first, joined_grad[1]),
+            (h_first, joined_grad[2]),
+            (attn_grad, mixed),
         )
-        value_grad = value_grad + jnp.einsum(
-            "hqk,qhd->khd",
-            attn_prob.astype(half),
-            mixed_blk,
-            preferred_element_type=jnp.float32,
+    ):
+        grad_attn = lax.dynamic_update_slice(
+            grad_attn, t_dot(a, b).astype(half), (0, k * local_width)
         )
-        score_grad = (prob_grad * attn_prob * (1.0 - attn_prob) * score_scale).astype(half)
-        query_grad = jnp.einsum(
-            "hqk,khd->qhd", score_grad, keys, preferred_element_type=jnp.float32
-        )
-        key_grad = key_grad + jnp.einsum(
-            "hqk,qhd->khd", score_grad, query_blk, preferred_element_type=jnp.float32
-        )
-        return ((key_grad, value_grad), query_grad)
-
-    zeros_kv = jnp.zeros((SEQ, heads_here, HDIM), jnp.float32)
-    (key_total, value_total), query_blocks = lax.scan(
-        back_block, (zeros_kv, zeros_kv), jnp.arange(block_total, dtype=jnp.int32)
-    )
-    query_total = query_blocks.reshape(SEQ, heads_here, HDIM)
-    joined_grad = jnp.concatenate(
-        [
-            unrotate(query_total, cosine, sine_tab).reshape(SEQ, local_width),
-            unrotate(key_total, cosine, sine_tab).reshape(SEQ, local_width),
-            value_total.reshape(SEQ, local_width),
-        ],
-        axis=1,
-    ).astype(half)
-    grad_attn = jnp.concatenate([t_dot(h_first, joined_grad).astype(half), grad_out], axis=1)
+    grad_attn, second_grad = lax.optimization_barrier((grad_attn, second_grad))
+    grad_attn, sum_ffn = lax.optimization_barrier((grad_attn, sum_ffn))
     sum_attn = lax.psum_scatter(grad_attn, "dp", scatter_dimension=0, tiled=True)
     input_grad, gain_one = scatter_rows(
-        n_mp, [(joined_grad, qkv_w, True)], [xin, second_grad], "last", gain_all[0:1], 4
+        n_mp,
+        [joined_grad[0], joined_grad[1], joined_grad[2]],
+        attn_w,
+        0,
+        [xin, second_grad],
+        "last",
+        gain_all[0:1],
+        4,
     )
     gain_partial = jnp.stack([gain_one.sum(axis=0), gain_two.sum(axis=0)], axis=0)
     sum_gains = scatter_gains(n_dp, n_mp, gain_partial, 5)

time: 1030 us -> 830 us (0.81)
  matrix products: 178 us -> 123 us
  other arithmetic: 114 us -> 60.2 us
  waiting for transfers between devices: 45.2 us -> 0.09 us
  Pallas kernels: 567 us -> 538 us
  local copies, waits for them, and re-layouts: 98.5 us -> 83.4 us
    pallas_call x3 -> x5, Pallas kernels: 468 us -> 367 us  [the longest x4 354 us: scatter_rows(): pl.pallas_call(kernel, out_shape=out_shape, in_specs=[VMEM] * count + [AN...]
    pallas_call x1 -> x2, Pallas kernels: 74.4 us -> 141 us  [gather_rows(): pl.pallas_call(kernel, out_shape=jax.ShapeDtypeStruct((n * rows, width),...]
    dot_general x13 -> x0, matrix products: 63.5 us -> none  [the longest x1 14.2 us: dot_t(): lax.dot_general(left, right, (((1,), (1,)), ((), ())), preferred_element_...]
    reduce_scatter x1, waiting for transfers between devices: 45.1 us -> 0.01 us  [per_device(): sum_ffn = lax.psum_scatter(grad_ffn, 'dp', scatter_dimension=0, tiled=True)]
    concatenate x5 -> x1, other arithmetic: 38 us -> 1.31 us  [rope_tables(): jnp.concatenate([cosine, cosine], axis=1)]
    slice x6 -> x0, local copies, waits for them, and re-layouts: 29.9 us -> none  [the longest x1 14 us: per_device(): gu_w, down_wt = (ffn_w[:, :2 * hidden], ffn_w[:, 2 * hidden:])]
    unnamed x88 -> x92, local copies, waits for them, and re-layouts: 33.1 us -> 53.7 us
    dynamic_update_slice x2, local copies, waits for them, and re-layouts: 4.48 us -> 17.1 us  [the longest x1 12.7 us: per_device(): lax.dynamic_update_slice(grad_ffn, t_dot(a, b).astype(half), (0, k * hidd...]
  transfers between devices with their start and end apart: 6 -> 4, of which waited for: 1 -> 0; matrix products, arithmetic and copies ran while one was open for 28% -> 15% of each run, Pallas kernels for 56% -> 66%
where the time goes in v2:
time: 830 us; the launch traced here: 820 us
  Pallas kernels  538 us (65%)
  matrix products  123 us (15%)
  local copies, waits for them, and re-layouts  83.4 us (10%)
  other arithmetic  60.2 us (7%)
  between operations  15.1 us (2%)
    pallas_call x4, Pallas kernels, scatter_rows(): pl.pallas_call(kernel, out_shape=out_shape, in_specs=[VMEM] * count + [AN...  354 us
    pallas_call x2, Pallas kernels, gather_rows(): pl.pallas_call(kernel, out_shape=jax.ShapeDtypeStruct((n * rows, width),...  141 us
    dot_general x5, matrix products, dot(): return jnp.dot(left, right, preferred_element_type=jnp.float32)  67.7 us
    dot_general x7, matrix products, t_dot(): lax.dot_general(left, right, (((0,), (0,)), ((), ())), preferred_element_...  55.3 us
    unnamed x92, local copies, waits for them, and re-layouts  53.7 us
    pallas_call x2, Pallas kernels, small_exchange(): pl.pallas_call(kernel, out_shape=jax.ShapeDtypeStruct(out, jnp.float32),...  29.9 us
  transfers between devices with their start and end apart: 4, of which 0 were waited for; matrix products, arithmetic and copies ran while one was open for 15% of the time, Pallas kernels for 66%

profile of v2, /device:TPU:0, one launch (start us, length us, event | category | flops | bytes accessed | tf_op | source)
XLA Modules:
  0.0 820.1 jit_solution(4053010570848719585)
XLA Ops:
  14.7 5.0 convert.18
  23.4 14.5 %gather_small.1 = f32[8,4,8,128]{3,2,1,0:T(8,128)} custom-call(f32[8,128]{1,0:T(8,128)} %pad.10.in_ref), custom_call_target="tpu_custom_call" | custom-call | tf_op jit(solution)/shard_map/gather_small/pallas_call | solution.py:616
  42.2 74.8 %gather_rows.2 = bf16[1024,2048]{1,0:T(8,128)(2,1)} custom-call(bf16[256,2048]{1,0:T(8,128)(2,1)} %multiply_convert_fusion.3.own_ref), custom_call_target="tpu_custom_call" | custom-call | bytes 209715200 | tf_op jit(solution)/shard_map/gather_rows/pallas_call | solution.py:152
  124.1 12.4 %fusion.6.refs_0_ = f32[1024,1536]{1,0:T(8,128)} fusion(bf16[1024,2048]{1,0:T(8,128)(2,1)} %gather_rows.2, bf16[2048,2048]{1,0:T(8,128)(2,1)} %all-gather.3.cloned.1.call-done.refs_1_.refs_3_), kind=kOutput, calls=%fused_computation.13 | convolution fusion | flops 6442450944 | bytes 16777216 | tf_op jit(solution)/shard_map/dot_general | solution.py:179
  136.5 99.7 %scatter_forward.1 = (f32[256,2048]{1,0:T(8,128)}, bf16[256,2048]{1,0:T(8,128)(2,1)}, bf16[1024,512]{1,0:T(8,128)(2,1)}, bf16[1024,512]{1,0:T(8,128)(2,1)}, bf16...) custom-call(f32[1024,1536]{1,0:T(8,128)} %fusion.6.refs_0_, ...), custom_call_target="tpu_custom_call" | custom-call | flops 2147483648 | bytes 300000000 | tf_op jit(solution)/shard_map/scatter_forward/pallas_call | solution.py:471
  236.3 66.4 %gather_rows.3 = bf16[1024,2048]{1,0:T(8,128)(2,1)} custom-call(bf16[256,2048]{1,0:T(8,128)(2,1)} %get-tuple-element.44.own_ref), custom_call_target="tpu_custom_call" | custom-call | bytes 209715200 | tf_op jit(solution)/shard_map/gather_rows/pallas_call | solution.py:152
  302.7 14.7 %fusion.4 = f32[1024,2048]{1,0:T(8,128)} fusion(bf16[1024,2048]{1,0:T(8,128)(2,1)} %gather_rows.3, bf16[2048,6144]{1,0:T(8,128)(2,1)} %all-gather.5.cloned.1.call-done.refs_2_.refs_1_), kind=kOutput, calls=%fused_computation.4 | convolution fusion | flops 8589934592 | bytes 20971520 | tf_op jit(solution)/shard_map/dot_general | solution.py:179
  317.4 13.3 %fusion.2 = f32[1024,2048]{1,0:T(8,128)} fusion(bf16[1024,2048]{1,0:T(8,128)(2,1)S(1)} %copy-done.12, bf16[2048,6144]{1,0:T(8,128)(2,1)} %all-gather.5.cloned.1.call-done.refs_2_.refs_1_), kind=kOutput, calls=%fused_computation.2 | convolution fusion | flops 8589934592 | bytes 20971520 | tf_op jit(solution)/shard_map/dot_general | solution.py:179
  330.8 21.1 %multiply_convert_fusion = (bf16[1024,2048]{1,0:T(8,128)(2,1)}, bf16[1024,2048]{1,0:T(8,128)(2,1)}, bf16[1024,2048]{1,0:T(8,128)(2,1)S(1)}) fusion(f32[1024,2048]{1,0:T(8,128)} %fusion.4, f32[1024,2048]{1,0:T(8,128)} %fusion.2, bf16[1024,2048]{1,0:T(8,128)(2,1)} %get-tuple-element.46, bf16[2048,6144]{1,0:T(8,128)(2,1)} %all-gather.5.cloned.1.call-done.refs_2_.refs_1_), kind=kOutput, calls=%fused_computation.8 | convolution fusion | flops 8623489024 | bytes 41943040 | tf_op jit(solution)/shard_map/dot_general | solution.py:179
  351.9 13.5 %convolution_convert_fusion = bf16[2048,2048]{1,0:T(8,128)(2,1)S(1)} fusion(bf16[1024,2048]{1,0:T(8,128)(2,1)} %gather_rows.3, bf16[1024,2048]{1,0:T(8,128)(2,1)} %get-tuple-element.47.refs_0_), kind=kOutput, calls=%fused_computation.12 | convolution fusion | flops 8594128896 | bytes 16777216 | tf_op jit(solution)/shard_map/dot_general | solution.py:173
  365.4 12.7 %dynamic_update_slice.21 = bf16[2048,6144]{1,0:T(8,128)(2,1)} pad(bf16[2048,2048]{1,0:T(8,128)(2,1)S(1)} %convolution_convert_fusion, bf16[]{:T(256)} %constant.27.clone.1), padding=0_0x0_4096 | pad | bytes 33554432 | tf_op jit(solution)/shard_map/dynamic_update_slice | solution.py:743
  378.1 13.7 %convert_dynamic-update-slice_fusion.1 = bf16[2048,6144]{1,0:T(8,128)(2,1)} fusion(bf16[2048,6144]{1,0:T(8,128)(2,1)} %dynamic_update_slice.21, bf16[1024,2048]{1,0:T(8,128)(2,1)S(1)} %copy-done.13, bf16[1024,2048]{1,0:T(8,128)(2,1)} %get-tuple-element.123.refs_1_), kind=kOutput, calls=%fused_computation.7 | convolution fusion | flops 8594128896 | bytes 16777216 | tf_op jit(solution)/shard_map/dot_general | solution.py:173
  391.8 11.6 %convert_dynamic-update-slice_fusion = bf16[2048,6144]{1,0:T(8,128)(2,1)} fusion(bf16[2048,6144]{1,0:T(8,128)(2,1)} %convert_dynamic-update-slice_fusion.1, bf16[1024,2048]{1,0:T(8,128)(2,1)S(1)} %copy-done.30, bf16[1024,2048]{1,0:T(8,128)(2,1)S(1)} %get-tuple-element.125.refs_0_), kind=kOutput, calls=%fused_computation.6 | convolution fusion | flops 8594128896 | bytes 16777216 | tf_op jit(solution)/shard_map/dot_general | solution.py:173
  404.3 91.0 %scatter_backward.1 = (f32[256,2048]{1,0:T(8,128)}, f32[8,2048]{1,0:T(8,128)}, bf16[256,2048]{1,0:T(8,128)(2,1)}) custom-call(bf16[1024,2048]{1,0:T(8,128)(2,1)} %get-tuple-element.47.refs_0_, bf16[1024,2048]{1,0:T(8,128)(2,1)} %get-tuple-element.123.refs_1_, bf16[2048,6144]{1,0:T(8,128)(2,1)} %all-gather.5.cloned.1.call-done.refs_2_.refs_1_, ...), custom_call_target="tpu_custom_call" | custom-call | flops 17179869184 | bytes 300000000 | tf_op jit(solution)/shard_map/scatter_backward/pallas_call | solution.py:471
  495.3 91.9 %scatter_residual.1 = (bf16[256,2048]{1,0:T(8,128)(2,1)}, bf16[1024,2048]{1,0:T(8,128)(2,1)}) custom-call(bf16[1024,2048]{1,0:T(8,128)(2,1)} %copy-done.10, bf16[2048,6144]{1,0:T(8,128)(2,1)} %all-gather.5.cloned.1.call-done.refs_2_.refs_1_, f32[1,2048]{1,0:T(1,128)} %slice.52.refs_2_.refs_3_, f32[256,2048]{1,0:T(8,128)} %get-tuple-element.45.refs_4_.refs_3_, ...), custom_call_target="tpu_custom_call" | custom-call | flops 8589934592 | bytes 300000000 | tf_op jit(solution)/shard_map/scatter_residual/pallas_call | solution.py:471
  587.3 6.2 fusion.14.do_ref
  593.4 12.7 %attention_backward.1 = (bf16[1024,512]{1,0:T(8,128)(2,1)}, bf16[1024,512]{1,0:T(8,128)(2,1)}, bf16[1024,512]{1,0:T(8,128)(2,1)}) custom-call(bf16[1024,512]{1,0:T(8,128)(2,1)} %get-tuple-element.50.q_ref, bf16[1024,512]{1,0:T(8,128)(2,1)} %get-tuple-element.51.k_ref, bf16[1024,512]{1,0:T(8,128)(2,1)} %get-tuple-element.52.v_ref, ...), custom_call_target="tpu_custom_call" | custom-call | flops 4294967296 | bytes 7340032 | tf_op jit(solution)/shard_map/attention_backward/pallas_call | solution.py:524
  606.1 4.9 convolution_convert_fusion.4
  640.4 71.8 %scatter_last.1 = (f32[256,2048]{1,0:T(8,128)}, f32[8,2048]{1,0:T(8,128)}) custom-call(bf16[1024,512]{1,0:T(8,128)(2,1)} %get-tuple-element.54.refs_0_, bf16[1024,512]{1,0:T(8,128)(2,1)} %get-tuple-element.55.refs_1_, bf16[1024,512]{1,0:T(8,128)(2,1)} %get-tuple-element.56.refs_2_, bf16[2048,2048]{1,0:T(8,128)(2,1)} %all-gather.3.cloned.1.call-done.refs_1_.refs_3_, ...), custom_call_target="tpu_custom_call" | custom-call | flops 6442450944 | bytes 300000000 | tf_op jit(solution)/shard_map/scatter_last/pallas_call | solution.py:471
  714.0 15.4 %sum_small.1 = f32[8,128]{1,0:T(8,128)} custom-call(f32[4,8,8,128]{3,2,1,0:T(8,128)} %pad.11.in_ref), custom_call_target="tpu_custom_call" | custom-call | tf_op jit(solution)/shard_map/sum_small/pallas_call | solution.py:616
  736.8 6.6 mul.246
  743.3 5.2 fusion.23
  760.7 11.0 %fusion.24 = (bf16[256,2,2048]{2,1,0:T(2,128)(2,1)}, f32[256,2,2048]{2,1,0:T(2,128)S(1)}, f32[256,2,2048]{2,1,0:T(2,128)}) fusion(f32[256,2,2048]{2,1,0:T(2,128)} %param.23, f32[256,2,2048]{2,1,0:T(2,128)} %mul.246, f32[256,2,2048]{2,1,0:T(2,128)} %param.28), kind=kLoop, calls=%fused_computation.71 | loop fusion | flops 7340032 | bytes 23068672 | tf_op jit(solution)/shard_map/convert_element_type | solution.py:831
  773.7 6.3 multiply_add_fusion
  (155 shorter events, 108.9 us)
Async XLA Ops:
  7.2 117.0 %all-gather.3.cloned.1.call-start = ((), (), s32[]{:S(2)}) async-start(), calls=%async_computation.2 | async-start | bytes 9437184 | tf_op jit(solution)/shard_map/all_gather | solution.py:700
  12.7 290.0 %all-gather.5.cloned.1.call-start = ((), (), s32[]{:S(2)}) async-start(), calls=%async_computation.3 | async-start | bytes 28311552 | tf_op jit(solution)/shard_map/all_gather | solution.py:702
  14.7 5.9 copy-start.1
  20.7 18.3 %copy-start.5 = (bf16[256,2048]{1,0:T(8,128)(2,1)S(1)}, bf16[256,2048]{1,0:T(8,128)(2,1)}, u32[]{:S(2)}) copy-start(bf16[256,2048]{1,0:T(8,128)(2,1)} %param.18) | copy-start | bytes 3145732
  22.6 604.4 %reduce-scatter.3.cloned.1.call-start = ((), (), s32[]{:S(2)}) async-start(), calls=%async_computation.4 | async-start | bytes 28311552 | tf_op jit(solution)/shard_map/reduce_scatter | solution.py:745
  39.0 78.0 %copy-start.22 = (f32[1,32,64]{2,1,0:T(8,128)}, f32[1,32,64]{2,1,0:T(8,128)S(1)}, u32[]{:S(2)}) copy-start(f32[1,32,64]{2,1,0:T(8,128)S(1)} %get-tuple-element.130) | copy-start | bytes 24580
  42.2 80.0 %copy-start.19 = (bf16[256,2048]{1,0:T(8,128)(2,1)S(1)}, bf16[256,2048]{1,0:T(8,128)(2,1)}, u32[]{:S(2)}) copy-start(bf16[256,2048]{1,0:T(8,128)(2,1)} %param.19) | copy-start | bytes 3145732
  302.7 14.7 %copy-start.12 = (bf16[1024,2048]{1,0:T(8,128)(2,1)S(1)}, bf16[1024,2048]{1,0:T(8,128)(2,1)}, u32[]{:S(2)}) copy-start(bf16[1024,2048]{1,0:T(8,128)(2,1)} %gather_rows.3) | copy-start | bytes 12582916
  351.9 39.9 %copy-start.10 = (bf16[1024,2048]{1,0:T(8,128)(2,1)}, bf16[1024,2048]{1,0:T(8,128)(2,1)S(1)}, u32[]{:S(2)}) copy-start(bf16[1024,2048]{1,0:T(8,128)(2,1)S(1)} %get-tuple-element.125.refs_0_) | copy-start | bytes 12582916
  365.4 12.7 %copy-start.13 = (bf16[1024,2048]{1,0:T(8,128)(2,1)S(1)}, bf16[1024,2048]{1,0:T(8,128)(2,1)}, u32[]{:S(2)}) copy-start(bf16[1024,2048]{1,0:T(8,128)(2,1)} %gather_rows.3) | copy-start | bytes 12582916
  378.1 13.7 %copy-start.30 = (bf16[1024,2048]{1,0:T(8,128)(2,1)S(1)}, bf16[1024,2048]{1,0:T(8,128)(2,1)}, u32[]{:S(2)}) copy-start(bf16[1024,2048]{1,0:T(8,128)(2,1)} %get-tuple-element.46) | copy-start | bytes 12582916
  403.4 376.6 %reduce-scatter.5.cloned.1.call-start = ((), (), s32[]{:S(2)}) async-start(), calls=%async_computation.5 | async-start | bytes 9437184 | tf_op jit(solution)/shard_map/reduce_scatter | solution.py:779
  627.7 4.7 copy-start.16
  631.4 6.1 copy-start.21
  640.3 71.8 %copy-start.24 = (f32[8,2048]{1,0:T(8,128)S(1)}, f32[8,2048]{1,0:T(8,128)}, u32[]{:S(2)}) copy-start(f32[8,2048]{1,0:T(8,128)} %get-tuple-element.66) | copy-start | bytes 196612
  640.3 89.8 %copy-start.26 = (f32[2,64]{1,0:T(2,128)S(1)}, f32[2,64]{1,0:T(2,128)}, u32[]{:S(2)}) copy-start(f32[2,64]{1,0:T(2,128)} %param.25) | copy-start | bytes 1540
  640.3 89.8 %copy-start.27 = (f32[2,64]{1,0:T(2,128)S(1)}, f32[2,64]{1,0:T(2,128)}, u32[]{:S(2)}) copy-start(f32[2,64]{1,0:T(2,128)} %param.35) | copy-start | bytes 1540
  640.3 89.8 %copy-start.28 = (f32[2,64]{1,0:T(2,128)S(1)}, f32[2,64]{1,0:T(2,128)}, u32[]{:S(2)}) copy-start(f32[2,64]{1,0:T(2,128)} %param.30) | copy-start | bytes 1540
  640.3 90.4 %copy-start.15 = (bf16[256,6144]{1,0:T(8,128)(2,1)S(1)}, bf16[256,6144]{1,0:T(8,128)(2,1)}, u32[]{:S(2)}) copy-start(bf16[256,6144]{1,0:T(8,128)(2,1)} %reduce-scatter.3.cloned.1.call-done) | copy-start | bytes 9437188
  760.7 13.0 %copy-start.9 = (f32[256,2,2048]{2,1,0:T(2,128)S(1)}, f32[256,2,2048]{2,1,0:T(2,128)}, u32[]{:S(2)}) copy-start(f32[256,2,2048]{2,1,0:T(2,128)} %param.33) | copy-start | bytes 12582916
  780.0 4.7 copy-start.4
  790.0 9.8 %copy-start.7 = (f32[256,3,512]{0,2,1:T(8,128)S(1)}, f32[256,3,512]{0,2,1:T(8,128)}, u32[]{:S(2)}) copy-start(f32[256,3,512]{0,2,1:T(8,128)} %copy.72) | copy-start | bytes 4718596
  801.2 5.6 copy-start.14
  804.3 7.7 copy-start.18
  (14 other events, 40.2 us)
Sparse Core Ops, SparseCore 0:
  12.8 58.4 all-gather.2
  73.8 125.3 all-gather.4
  403.6 155.7 reduce-scatter.2
  627.2 71.9 reduce-scatter.4

commit v3 on v2

--- a/solution.py
+++ b/solution.py
@@ -6,6 +6,7 @@
 from jax import lax
 from jax.experimental import pallas as pl
 from jax.experimental.pallas import tpu as pltpu
+import numpy as np
 from jax.sharding import PartitionSpec as P
 
 HDIM = 128
@@ -101,14 +102,17 @@
 
     def forward(self, step):
         for chunk in range(self.chunks):
-            for (got, arrival), (has, copy) in zip(
-                self.arrivals(step - 1, chunk), self.copies(step, chunk, False)
-            ):
-                pl.when(got)(arrival.wait_recv)
-                pl.when(has)(copy.start)
-
-    def finish(self):
-        for chunk in range(self.chunks):
+            self.forward_chunk(step, chunk, True)
+
+    def forward_chunk(self, step, chunk, more):
+        for (got, arrival), (has, copy) in zip(
+            self.arrivals(step - 1, chunk), self.copies(step, chunk, False)
+        ):
+            pl.when(got)(arrival.wait_recv)
+            pl.when(has & more)(copy.start)
+
+    def finish(self, arrivals=True):
+        for chunk in range(self.chunks if arrivals else 0):
             for got, arrival in self.arrivals(self.n - 2, chunk):
                 pl.when(got)(arrival.wait_recv)
         for chunk in range(self.chunks):
@@ -135,32 +139,207 @@
     return [pltpu.SemaphoreType.DMA(((n - 1) * chunks,))] * 4
 
 
-def gather_rows(n, own, collective_id):
-    rows, width = own.shape
-
-    def kernel(own_ref, whole_ref, local_sem, *sems):
-        me = lax.axis_index("mp")
-        stream = LineGather(n, rows, 1, own_ref, whole_ref, sems)
-        local = pltpu.make_async_copy(own_ref, stream.at(me, 0), local_sem)
-        local.start()
-        neighbour_barrier(n)
-        stream.send_own(0)
-        stream.forward_all()
-        stream.finish()
-        local.wait()
+class Exchange:
+    def __init__(self, n_dp, n_mp, sems):
+        self.n_dp, self.n_mp = n_dp, n_mp
+        self.s_mp, self.r_mp, self.s_dp, self.r_dp = sems
+        self.dp, self.mp = lax.axis_index("dp"), lax.axis_index("mp")
+
+    def barrier(self):
+        barrier = pltpu.get_barrier_semaphore()
+        for axis, here, count in (("mp", self.mp, self.n_mp), ("dp", self.dp, self.n_dp)):
+            for k in range(1, count):
+                pl.semaphore_signal(
+                    barrier,
+                    inc=1,
+                    device_id={axis: lax.rem(here + k, count)},
+                    device_id_type=MESH,
+                )
+        pl.semaphore_wait(barrier, self.n_mp + self.n_dp - 2)
+
+    def swap(self, axis, source_of, target):
+        if axis == "mp":
+            here, count, send, recv = self.mp, self.n_mp, self.s_mp, self.r_mp
+        else:
+            here, count, send, recv = self.dp, self.n_dp, self.s_dp, self.r_dp
+        copies = []
+        for k in range(1, count):
+            peer = lax.rem(here + k, count)
+            copies.append(
+                pltpu.make_async_remote_copy(
+                    src_ref=source_of(peer),
+                    dst_ref=target.at[here],
+                    send_sem=send.at[k - 1],
+                    recv_sem=recv.at[k - 1],
+                    device_id={axis: peer},
+                    device_id_type=MESH,
+                )
+            )
+        for copy in copies:
+            copy.start()
+        return copies
+
+
+def exchange_sems(n_dp, n_mp):
+    return [pltpu.SemaphoreType.DMA((n_mp - 1,))] * 2 + [pltpu.SemaphoreType.DMA((n_dp - 1,))] * 2
+
+
+def tile_of(dp, mp, n_mp, local):
+    return (dp * n_mp + mp) * local // 128
+
+
+def flat_pairs(x):
+    high, parts, wide = x.shape
+    return x.reshape(high, parts, wide // 128, 128).transpose(0, 2, 1, 3).reshape(-1, 128)
+
+
+def round_shares(w_gu, w_down):
+    high, parts, hidden = w_gu.shape
+    tiles = hidden // 128
+    step = 128
+    turn = min(256, hidden)
+
+    def kernel(gu_ref, down_ref, out_ref):
+        for part in range(parts):
+            for tile in range(tiles):
+                cols = pl.ds(part * hidden + tile * 128, 128)
+                out_ref[:, cols] = gu_ref[
+                    pl.ds(tile * parts + part, step, stride=tiles * parts), :
+                ].astype(jnp.bfloat16)
+        for i in range(hidden // turn):
+            piece = down_ref[pl.ds(i * turn, turn), :]
+            out_ref[:, pl.ds(parts * hidden + i * turn, turn)] = piece.T.astype(jnp.bfloat16)
 
     return pl.pallas_call(
         kernel,
-        out_shape=jax.ShapeDtypeStruct((n * rows, width), own.dtype),
-        in_specs=[ANY],
-        out_specs=ANY,
-        scratch_shapes=[pltpu.SemaphoreType.DMA] + gather_sems(n, 1),
-        compiler_params=pltpu.CompilerParams(collective_id=collective_id, has_side_effects=True),
+        grid=(high // step,),
+        out_shape=jax.ShapeDtypeStruct((high, (parts + 1) * hidden), jnp.bfloat16),
+        in_specs=[
+            pl.BlockSpec((step * tiles * parts, 128), lambda i: (i, 0)),
+            pl.BlockSpec((hidden, step), lambda i: (0, i)),
+        ],
+        out_specs=pl.BlockSpec((step, (parts + 1) * hidden), lambda i: (i, 0)),
+        compiler_params=pltpu.CompilerParams(vmem_limit_bytes=VMEM_LIMIT),
+        cost_estimate=pl.CostEstimate(
+            flops=0, bytes_accessed=6 * (w_gu.size + w_down.size), transcendentals=0
+        ),
+        name="round_shares",
+    )(flat_pairs(w_gu), w_down)
+
+
+def gather_first(n_dp, n_mp, own, gains, cotangent, live, collective_id, chunks=2):
+    rows, width = own.shape
+    local = gains.shape[1]
+    lanes = jnp.arange(128, dtype=jnp.int32) // local
+    place = lax.rem(lax.axis_index("mp"), 128 // local)
+    if n_mp * local < 128:
+        place = lax.rem(lax.axis_index("dp") * n_mp + lax.axis_index("mp"), 128 // local)
+    tile = jnp.where(
+        (lanes == place)[None, :], jnp.tile(gains, (1, 128 // local)), 0.0
+    )
+    tile = jnp.concatenate([tile, jnp.zeros((6, 128), jnp.float32)], axis=0)
+
+    block = 64 if rows % 64 == 0 else rows
+
+    def kernel(
+        own_ref,
+        tile_ref,
+        cotangent_ref,
+        live_ref,
+        normed_ref,
+        gain_ref,
+        base_ref,
+        branch_ref,
+        all_ref,
+        first,
+        second,
+        *sems,
+    ):
+        me = lax.axis_index("mp")
+        exchange = Exchange(n_dp, n_mp, sems[:4])
+        stream = LineGather(n_mp, rows, chunks, own_ref, all_ref, sems[4:])
+        exchange.barrier()
+        first[me] = tile_ref[...]
+        copies = exchange.swap("mp", lambda peer: tile_ref, first)
+        for chunk in range(chunks):
+            stream.send_own(chunk)
+        all_ref[rows_at(me * rows, rows), :] = own_ref[...]
+        for copy in copies:
+            copy.wait()
+        dp = lax.axis_index("dp")
+        second[dp] = first[...]
+        copies = exchange.swap("dp", lambda peer: first, second)
+
+        def enter(i, carry):
+            span = rows_at(i * block, block)
+            value = cotangent_ref[span, :].astype(jnp.float32) * live_ref[span, :]
+            base_ref[span, :] = value
+            branch_ref[span, :] = value.astype(jnp.bfloat16)
+            return carry
+
+        lax.fori_loop(0, rows // block, enter, 0)
+        for copy in copies:
+            copy.wait()
+        gain_ref[...] = jnp.zeros_like(gain_ref)
+        for d in range(n_dp):
+            for m in range(n_mp):
+                cols = pl.ds(tile_of(d, m, n_mp, local) * 128, 128)
+                gain_ref[:, cols] += second[d, m]
+        def norm(block_id):
+            def body(i, carry):
+                span = rows_at(block_id * rows + i * block, block)
+                value = all_ref[span, :].astype(jnp.float32)
+                inverse = lax.rsqrt(jnp.mean(value * value, axis=1, keepdims=True) + norm_eps)
+                normed_ref[span, :] = (value * inverse * gain_ref[0:1, :]).astype(jnp.bfloat16)
+                return carry
+
+            lax.fori_loop(0, rows // block, body, 0)
+
+        def step_of(step, carry):
+            @pl.when(step > 0)
+            def _():
+                for chunk in range(chunks):
+                    stream.forward_chunk(step, chunk, step < n_mp - 1)
+
+            @pl.when(me + step < n_mp)
+            def _():
+                norm(me + step)
+
+            @pl.when((me - step >= 0) & (step > 0))
+            def _():
+                norm(me - step)
+
+            return carry
+
+        lax.fori_loop(0, n_mp, step_of, 0)
+        stream.finish(False)
+
+    half = jnp.bfloat16
+    return pl.pallas_call(
+        kernel,
+        out_shape=[
+            jax.ShapeDtypeStruct((n_mp * rows, width), half),
+            jax.ShapeDtypeStruct((8, width), jnp.float32),
+            jax.ShapeDtypeStruct((rows, width), jnp.float32),
+            jax.ShapeDtypeStruct((rows, width), half),
+        ],
+        in_specs=[VMEM] * 4,
+        out_specs=[VMEM] * 4,
+        scratch_shapes=[
+            pltpu.VMEM((n_mp * rows, width), half),
+            pltpu.VMEM((n_mp, 8, 128), jnp.float32),
+            pltpu.VMEM((n_dp, n_mp, 8, 128), jnp.float32),
+        ]
+        + exchange_sems(n_dp, n_mp)
+        + gather_sems(n_mp, chunks),
+        compiler_params=pltpu.CompilerParams(
+            collective_id=collective_id, has_side_effects=True, vmem_limit_bytes=VMEM_LIMIT
+        ),
         cost_estimate=pl.CostEstimate(
             flops=0, bytes_accessed=200 * own.size * own.dtype.itemsize, transcendentals=0
         ),
-        name="gather_rows",
-    )(own)
+        name="gather_first",
+    )(own, tile, cotangent, live)
 
 
 def dot_t(left, right):
@@ -189,7 +368,21 @@
 
 
 def scatter_rows(
-    n, lhs, rhs, rhs_start, own_rows, epilogue, gains_row, collective_id, heads=None, extra=None, chunks=2
+    n,
+    lhs,
+    rhs,
+    rhs_start,
+    own_rows,
+    epilogue,
+    gains_row,
+    collective_id,
+    heads=None,
+    extra=None,
+    other_gain=None,
+    grad_lefts=None,
+    grad_right=None,
+    n_dp=1,
+    chunks=2,
 ):
     total_rows = lhs[0].shape[0]
     rows = total_rows // n
@@ -200,7 +393,7 @@
     count = len(lhs)
     block = 32
     if heads is not None:
-        inner_width = lhs[0].shape[1] // 3
+        inner_width = rhs_start // 3
         head_count = inner_width // HDIM
         pieces = [inner_width]
     else:
@@ -219,41 +412,135 @@
         own = take(len(own_rows))
         if heads is not None:
             cosine_ref, sine_ref, mask_ref = take(3)
+        if other_gain is not None:
+            (other_ref,) = take(1)
+            grad_left_refs, grad_right_ref = take(2), take(1)[0]
         extra_ref = take(1)[0] if extra is not None else None
         outs = take(1 + has_gain)
+        owned_ref = take(1)[0] if other_gain is not None else None
         normed = take(1)[0] if has_norm else None
         if heads is not None:
             query_ref, key_ref, value_ref, mixed_ref = take(4)
         extra_whole = take(1)[0] if extra is not None else None
         right, held, sent, part = take(4)
+        joined_ref = take(1)[0] if heads is not None else None
         right_sem, send_sems, recv_sems = take(3)
         me = lax.axis_index("mp")
         fetch = pltpu.make_async_copy(
             right_hbm.at[:, pl.ds(rhs_start, depth)], right, right_sem
         )
         fetch.start()
+        if heads is not None:
+            (joined_sem,) = take(1)
+            fetch_joined = pltpu.make_async_copy(
+                right_hbm.at[:, pl.ds(0, rhs_start)], joined_ref, joined_sem
+            )
+            fetch_joined.start()
         if extra is not None:
             (extra_sem,) = take(1)
             extra_gather = LineGather(n, rows, 1, extra_ref, extra_whole, take(4))
             extra_local = pltpu.make_async_copy(extra_ref, extra_gather.at(me, 0), extra_sem)
             extra_local.start()
-        neighbour_barrier(n)
+        if other_gain is not None:
+            gain_sum, table, first, middle, second = take(5)
+            exchange = Exchange(n_dp, n, take(4))
+            grads, paired, landed = take(3)
+            pair_send, pair_recv, land_send, land_recv = take(4)
+            dp = lax.axis_index("dp")
+            core, chip = lax.rem(dp, 2), dp // 2
+            chips, share = n_dp // 2, landed.shape[1]
+            exchange.barrier()
+            pair_copies = [
+                pltpu.make_async_remote_copy(
+                    src_ref=grads.at[rows_at((2 * q + 1 - core) * share, share)],
+                    dst_ref=paired.at[q],
+                    send_sem=pair_send.at[q],
+                    recv_sem=pair_recv.at[q],
+                    device_id={"dp": dp + 1 - 2 * core},
+                    device_id_type=MESH,
+                )
+                for q in range(chips)
+            ]
+            land_copies = [
+                pltpu.make_async_remote_copy(
+                    src_ref=paired.at[lax.rem(chip + k, chips)],
+                    dst_ref=landed.at[k - 1],
+                    send_sem=land_send.at[k - 1],
+                    recv_sem=land_recv.at[k - 1],
+                    device_id={"dp": 2 * lax.rem(chip + k, chips) + core},
+                    device_id_type=MESH,
+                )
+                for k in range(1, chips)
+            ]
+
+            def make_grads():
+                start, narrow = 0, 256
+                for k, right_ref in enumerate([*left_refs, grad_right_ref]):
+                    left_ref = grad_left_refs[0 if k < count else 1]
+
+                    def column(i, carry, start=start, left_ref=left_ref, right_ref=right_ref):
+                        grads[:, rows_at(start + i * narrow, narrow)] = t_dot(
+                            left_ref[...], right_ref[:, rows_at(i * narrow, narrow)]
+                        ).astype(jnp.bfloat16)
+                        return carry
+
+                    lax.fori_loop(0, right_ref.shape[1] // narrow, column, 0)
+                    start += right_ref.shape[1]
+                for copy in pair_copies:
+                    copy.start()
+
+            def pair_up():
+                for copy in pair_copies:
+                    copy.wait()
+
+                def add(i, carry):
+                    span = rows_at(i * block, block)
+                    for q in range(chips):
+                        own_span = rows_at((2 * q + core) * share + i * block, block)
+                        paired[q, span, :] = (
+                            paired[q, span, :].astype(jnp.float32)
+                            + grads[own_span, :].astype(jnp.float32)
+                        ).astype(jnp.bfloat16)
+                    return carry
+
+                lax.fori_loop(0, share // block, add, 0)
+                for copy in land_copies:
+                    copy.start()
+
+            def land():
+                for copy in land_copies:
+                    copy.wait()
+
+                def add(i, carry):
+                    span = rows_at(i * block, block)
+                    total = paired[chip, span, :].astype(jnp.float32)
+                    for k in range(chips - 1):
+                        total = total + landed[k, span, :].astype(jnp.float32)
+                    owned_ref[span, :] = total
+                    return carry
+
+                lax.fori_loop(0, share // block, add, 0)
+
+        else:
+            gain_sum = outs[1] if has_gain else None
+            neighbour_barrier(n)
         if extra is not None:
             extra_gather.send_own(0)
         if heads is not None:
-            turn = 128
+            turn = 256
+            fetch_joined.wait()
 
             def enter(i, carry):
                 span = rows_at(i * turn, turn)
                 cosine, sine = cosine_ref[span, :], sine_ref[span, :]
-                for h in range(head_count):
-                    cols = pl.ds(h * HDIM, HDIM)
-                    for k, target in ((0, query_ref), (1, key_ref)):
-                        piece = left_refs[0][span, pl.ds(k * inner_width + h * HDIM, HDIM)]
-                        target[span, cols] = rotated(piece, cosine, sine).astype(jnp.bfloat16)
-                value_ref[span, :] = left_refs[0][
-                    span, pl.ds(2 * inner_width, inner_width)
-                ].astype(jnp.bfloat16)
+                row_vals = left_refs[0][span, :]
+                for k, target in ((0, query_ref), (1, key_ref), (2, value_ref)):
+                    piece = dot(row_vals, joined_ref[:, pl.ds(k * inner_width, inner_width)])
+                    for h in range(head_count):
+                        value = piece[:, h * HDIM : (h + 1) * HDIM]
+                        if k < 2:
+                            value = rotated(value, cosine, sine)
+                        target[span, pl.ds(h * HDIM, HDIM)] = value.astype(jnp.bfloat16)
                 return carry
 
             lax.fori_loop(0, total_rows // turn, enter, 0)
@@ -365,12 +652,16 @@
                 def _():
                     extra_gather.forward(step)
 
+            if other_gain is not None:
+                pl.when(step == 1)(make_grads)
+                pl.when(step == 2)(pair_up)
+
             return carry
 
         lax.fori_loop(1, n, step_of, 0)
         product(me)
         if has_gain:
-            outs[1][...] = jnp.zeros_like(outs[1])
+            gain_sum[...] = jnp.zeros_like(gain_sum)
         for chunk in range(chunks):
 
             @pl.when(me > 0)
@@ -409,7 +700,7 @@
                     inner = jnp.mean(scaled * unit, axis=1, keepdims=True)
                     result = own[1][span, :] + inverse * (scaled - unit * inner)
                     outs[0][span, :] = result
-                    outs[1][...] += jnp.sum(
+                    gain_sum[...] += jnp.sum(
                         (total * unit).reshape(block // 8, 8, width), axis=0
                     )
                     if has_norm:
@@ -420,6 +711,30 @@
         if extra is not None:
             extra_gather.finish()
             extra_local.wait()
+        if other_gain is not None:
+            local = width // (n * n_dp)
+            for source, rows_of in ((gain_sum, pl.ds(0, 8)), (other_ref, pl.ds(8, 8))):
+                for d in range(n_dp):
+                    for m in range(n):
+                        cols = pl.ds(tile_of(d, m, n, local) * 128, 128)
+                        table[m, d, rows_of, :] = source[:, cols]
+            copies = exchange.swap("mp", lambda peer: table.at[peer], first)
+            first[me] = table[me]
+            for copy in copies:
+                copy.wait()
+            total = first[0]
+            for m in range(1, n):
+                total = total + first[m]
+            middle[...] = total
+            copies = exchange.swap("dp", lambda peer: middle.at[peer], second)
+            second[dp] = middle[dp]
+            land()
+            for copy in copies:
+                copy.wait()
+            total = second[0]
+            for d in range(1, n_dp):
+                total = total + second[d]
+            outs[1][...] = total
 
         def sends(step, carry):
             for chunk in range(chunks):
@@ -440,7 +755,14 @@
     out_shape = [jax.ShapeDtypeStruct((rows, width), out_type)]
     out_specs = [VMEM]
     if has_gain:
-        out_shape.append(jax.ShapeDtypeStruct((8, width), jnp.float32))
+        out_shape.append(
+            jax.ShapeDtypeStruct((8, width) if other_gain is None else (16, 128), jnp.float32)
+        )
+        out_specs.append(VMEM)
+    if other_gain is not None:
+        share = width // n_dp
+        grad_width = sum(pieces) + grad_right.shape[1]
+        out_shape.append(jax.ShapeDtypeStruct((share, grad_width), jnp.float32))
         out_specs.append(VMEM)
     scratch = [
         pltpu.VMEM((width, depth), jnp.bfloat16),
@@ -448,6 +770,8 @@
         pltpu.VMEM((n, rows, width), jnp.bfloat16),
         pltpu.VMEM((rows, width), jnp.float32),
     ]
+    if heads is not None:
+        scratch.append(pltpu.VMEM((width, rhs_start), jnp.bfloat16))
     if has_norm:
         out_shape.append(jax.ShapeDtypeStruct((rows, width), jnp.bfloat16))
         out_specs.append(VMEM)
@@ -458,6 +782,7 @@
     ]
     head_args = []
     if heads is not None:
+        scratch.append(pltpu.SemaphoreType.DMA)
         head_args = list(heads)
         out_shape += [jax.ShapeDtypeStruct((total_rows, inner_width), jnp.bfloat16)] * 4
         out_specs += [VMEM] * 4
@@ -467,6 +792,21 @@
         out_specs.append(ANY)
         scratch += [pltpu.SemaphoreType.DMA] + gather_sems(n, 1)
         extra_args = [extra]
+    if other_gain is not None:
+        head_args += [other_gain, *grad_lefts, grad_right]
+        scratch += [
+            pltpu.VMEM((8, width), jnp.float32),
+            pltpu.VMEM((n, n_dp, 16, 128), jnp.float32),
+            pltpu.VMEM((n, n_dp, 16, 128), jnp.float32),
+            pltpu.VMEM((n_dp, 16, 128), jnp.float32),
+            pltpu.VMEM((n_dp, 16, 128), jnp.float32),
+        ] + exchange_sems(n_dp, n)
+        chips = n_dp // 2
+        scratch.append(pltpu.VMEM((width, grad_width), jnp.bfloat16))
+        scratch.append(pltpu.VMEM((chips, share, grad_width), jnp.bfloat16))
+        scratch.append(pltpu.VMEM((chips - 1, share, grad_width), jnp.bfloat16))
+        scratch += [pltpu.SemaphoreType.DMA((chips,))] * 2
+        scratch += [pltpu.SemaphoreType.DMA((chips - 1,))] * 2
     flops = 2 * total_rows * depth * width
     return pl.pallas_call(
         kernel,
@@ -485,6 +825,287 @@
         ),
         name="scatter_" + epilogue,
     )(*lhs, rhs, gains_row, *own_rows, *head_args, *extra_args)
+
+
+def feed_forward(n, normed, branch_grad, weights, own_rows, gains_row, collective_id, chunks=1, hops=4):
+    rows, width = normed.shape
+    total_rows = n * rows
+    hidden = weights.shape[1] // 3
+    size = rows // chunks
+    part_size = size // hops
+    count = chunks * hops
+    tile = min(1024, hidden)
+    block = min(32, part_size)
+
+    def kernel(
+        normed_ref,
+        branch_hbm,
+        weights_hbm,
+        second_ref,
+        base_ref,
+        gain_ref,
+        result_ref,
+        rounded_ref,
+        gain_sum,
+        whole_hbm,
+        act_hbm,
+        gate_hbm,
+        up_hbm,
+        weight_ref,
+        branch_ref,
+        all_ref,
+        held,
+        sent,
+        own_part,
+        act_ref,
+        gate_ref,
+        up_ref,
+        load_sems,
+        stage_sems,
+        send_sems,
+        recv_sems,
+        *gather_refs,
+    ):
+        me = lax.axis_index("mp")
+        middle = (me > 0) & (me < n - 1)
+        loads = [
+            pltpu.make_async_copy(weights_hbm, weight_ref, load_sems.at[0]),
+            pltpu.make_async_copy(branch_hbm, branch_ref, load_sems.at[1]),
+        ]
+        for load in loads:
+            load.start()
+        gather = LineGather(n, rows, chunks, normed_ref, all_ref, gather_refs)
+        neighbour_barrier(n)
+        for chunk in range(chunks):
+            gather.send_own(chunk)
+        all_ref[rows_at(me * rows, rows), :] = normed_ref[...]
+        for load in loads:
+            load.wait()
+
+        def hop(block_id, chunk, rightward):
+            peer = me + 1 if rightward else me - 1
+            slot = block_id if rightward else jnp.where(block_id == peer, n, block_id)
+            return remote(
+                sent.at[block_id, pl.ds(chunk * part_size, part_size)],
+                held.at[slot, pl.ds(chunk * part_size, part_size)],
+                send_sems.at[block_id * count + chunk],
+                recv_sems.at[slot * count + chunk],
+                peer,
+            )
+
+        def arrival(slot, chunk):
+            ref = held.at[slot, pl.ds(chunk * part_size, part_size)]
+            return remote(
+                ref, ref, send_sems.at[chunk], recv_sems.at[slot * count + chunk], me
+            )
+
+        def stages(block_id, chunk):
+            span = rows_at(block_id * rows + chunk * size, size)
+            return [
+                pltpu.make_async_copy(ref.at[chunk], hbm.at[span], stage_sems.at[chunk * 3 + k])
+                for k, (ref, hbm) in enumerate(
+                    ((act_ref, act_hbm), (gate_ref, gate_hbm), (up_ref, up_hbm))
+                )
+            ]
+
+        def compute(block_id, chunk, first):
+            span = rows_at(block_id * rows + chunk * size, size)
+
+            @pl.when(jnp.logical_not(first))
+            def _():
+                for stage in stages(block_id, chunk):
+                    stage.wait()
+
+            def units(ct, carry):
+                cols = rows_at(ct * tile, tile)
+                row_vals, branch = all_ref[span, :], branch_ref[span, :]
+                gate = dot(row_vals, weight_ref[:, cols])
+                up = dot(row_vals, weight_ref[:, rows_at(hidden + ct * tile, tile)])
+                act_grad = dot(branch, weight_ref[:, rows_at(2 * hidden + ct * tile, tile)])
+                sigma = 1.0 / (1.0 + jnp.exp(-gate))
+                silu = gate * sigma
+                act_ref[chunk, :, cols] = (silu * up).astype(jnp.bfloat16)
+                gate_ref[chunk, :, cols] = (
+                    act_grad * up * sigma * (1.0 + gate * (1.0 - sigma))
+                ).astype(jnp.bfloat16)
+                up_ref[chunk, :, cols] = (act_grad * silu).astype(jnp.bfloat16)
+                return carry
+
+            lax.fori_loop(0, hidden // tile, units, 0)
+            for stage in stages(block_id, chunk):
+                stage.start()
+
+            def columns(ct, carry):
+                cols = rows_at(ct * tile, tile)
+                total = dot_t(gate_ref[chunk], weight_ref[cols, pl.ds(0, hidden)])
+                total += dot_t(up_ref[chunk], weight_ref[cols, pl.ds(hidden, hidden)])
+
+                @pl.when(block_id == me)
+                def _():
+                    own_part[pl.ds(chunk * size, size), cols] = total
+
+                @pl.when(block_id != me)
+                def _():
+                    sent[block_id, pl.ds(chunk * size, size), cols] = total.astype(jnp.bfloat16)
+
+                return carry
+
+            lax.fori_loop(0, width // tile, columns, 0)
+
+            @pl.when((me == 0) & (block_id > me))
+            def _():
+                for k in range(hops):
+                    hop(block_id, chunk * hops + k, True).start()
+
+            @pl.when((me == n - 1) & (block_id < me))
+            def _():
+                for k in range(hops):
+                    hop(block_id, chunk * hops + k, False).start()
+
+        def step_of(step, carry):
+            def side_of(side, carry):
+                block_id = me + (1 - 2 * side) * step
+                valid = (block_id >= 0) & (block_id < n) & ((step > 0) | (side == 0))
+                for chunk in range(chunks):
+
+                    @pl.when(middle & (step > 0) & (step < n - 1) & (side == 1))
+                    def _():
+                        gather.forward_chunk(step + 1, chunk, step < n - 2)
+
+                    @pl.when(jnp.logical_not(middle) & valid & (step > 0))
+                    def _():
+                        gather.forward_chunk(step, chunk, step < n - 1)
+
+                    @pl.when(valid)
+                    def _():
+                        compute(block_id, chunk, step == 0)
+
+                    @pl.when(middle & (step == 0) & (side == 0))
+                    def _():
+                        gather.forward_chunk(1, chunk, 1 < n - 1)
+
+                return carry
+
+            return lax.fori_loop(0, 2, side_of, carry)
+
+        lax.fori_loop(0, n, step_of, 0)
+        whole_copy = pltpu.make_async_copy(all_ref, whole_hbm, load_sems.at[0])
+        whole_copy.start()
+
+        def add_rows(block_id, chunk):
+            def body(i, carry):
+                span = rows_at(chunk * part_size + i * block, block)
+                value = sent[block_id, span, :].astype(jnp.float32)
+                value = value + held[block_id, span, :].astype(jnp.float32)
+                sent[block_id, span, :] = value.astype(jnp.bfloat16)
+                return carry
+
+            lax.fori_loop(0, part_size // block, body, 0)
+
+        def relay_of(step, carry):
+            for chunk in range(count):
+                for rightward, block_id, has in (
+                    (True, step, (me > 0) & (step > me)),
+                    (False, n - 1 - step, (me < n - 1) & (n - 1 - step < me)),
+                ):
+
+                    @pl.when(has)
+                    def _():
+                        arrival(block_id, chunk).wait_recv()
+                        add_rows(block_id, chunk)
+                        hop(block_id, chunk, rightward).start()
+
+            return carry
+
+        lax.fori_loop(1, n, relay_of, 0)
+        gain_sum[...] = jnp.zeros_like(gain_sum)
+        for chunk in range(count):
+
+            @pl.when(me > 0)
+            def _():
+                arrival(me, chunk).wait_recv()
+
+            @pl.when(me < n - 1)
+            def _():
+                arrival(n, chunk).wait_recv()
+
+            def body(i, carry):
+                span = rows_at(chunk * part_size + i * block, block)
+                total = own_part[span, :]
+                zero = jnp.zeros_like(total)
+                total = total + jnp.where(me > 0, held[me, span, :].astype(jnp.float32), zero)
+                total = total + jnp.where(
+                    me < n - 1, held[n, span, :].astype(jnp.float32), zero
+                )
+                value = second_ref[span, :]
+                inverse = lax.rsqrt(jnp.mean(value * value, axis=1, keepdims=True) + norm_eps)
+                unit = value * inverse
+                scaled = total * gain_ref[...]
+                inner = jnp.mean(scaled * unit, axis=1, keepdims=True)
+                result = base_ref[span, :] + inverse * (scaled - unit * inner)
+                result_ref[span, :] = result
+                rounded_ref[span, :] = result.astype(jnp.bfloat16)
+                gain_sum[...] += jnp.sum((total * unit).reshape(block // 8, 8, width), axis=0)
+                return carry
+
+            lax.fori_loop(0, part_size // block, body, 0)
+        gather.finish(False)
+        for chunk in range(chunks):
+            for stage in stages(me, chunk):
+                stage.wait()
+
+        def sends(block_id, carry):
+            for chunk in range(count):
+
+                @pl.when((block_id > me) & (me < n - 1))
+                def _():
+                    hop(block_id, chunk, True).wait_send()
+
+                @pl.when((block_id < me) & (me > 0))
+                def _():
+                    hop(block_id, chunk, False).wait_send()
+
+            return carry
+
+        lax.fori_loop(0, n, sends, 0)
+        whole_copy.wait()
+
+    half = jnp.bfloat16
+    return pl.pallas_call(
+        kernel,
+        out_shape=[
+            jax.ShapeDtypeStruct((rows, width), jnp.float32),
+            jax.ShapeDtypeStruct((rows, width), half),
+            jax.ShapeDtypeStruct((8, width), jnp.float32),
+            jax.ShapeDtypeStruct((total_rows, width), half),
+        ]
+        + [jax.ShapeDtypeStruct((total_rows, hidden), half)] * 3,
+        in_specs=[VMEM, ANY, ANY, VMEM, VMEM, VMEM],
+        out_specs=[VMEM] * 3 + [ANY] * 4,
+        scratch_shapes=[
+            pltpu.VMEM((width, 3 * hidden), half),
+            pltpu.VMEM((total_rows, width), half),
+            pltpu.VMEM((total_rows, width), half),
+            pltpu.VMEM((n + 1, rows, width), half),
+            pltpu.VMEM((n, rows, width), half),
+            pltpu.VMEM((rows, width), jnp.float32),
+        ]
+        + [pltpu.VMEM((chunks, size, hidden), half)] * 3
+        + [
+            pltpu.SemaphoreType.DMA((2,)),
+            pltpu.SemaphoreType.DMA((chunks * 3,)),
+            pltpu.SemaphoreType.DMA((n * count,)),
+            pltpu.SemaphoreType.DMA(((n + 1) * count,)),
+        ]
+        + gather_sems(n, chunks),
+        compiler_params=pltpu.CompilerParams(
+            collective_id=collective_id, has_side_effects=True, vmem_limit_bytes=VMEM_LIMIT
+        ),
+        cost_estimate=pl.CostEstimate(
+            flops=10 * total_rows * width * hidden, bytes_accessed=300_000_000, transcendentals=0
+        ),
+        name="feed_forward",
+    )(normed, branch_grad, weights, *own_rows, gains_row)
 
 
 def attention_backward(queries, keys, values, mixed_grad, cosine, sine, key_mask):
@@ -538,132 +1159,163 @@
     )(queries, keys, values, mixed_grad, cosine, sine, key_mask)
 
 
-def small_exchange(n_dp, n_mp, table, reduces, collective_id):
-    peers_mp, peers_dp = n_mp - 1, n_dp - 1
-
-    def kernel(in_ref, out_ref, first, second, mid, s_mp, r_mp, s_dp, r_dp):
-        dp, mp = lax.axis_index("dp"), lax.axis_index("mp")
-        barrier = pltpu.get_barrier_semaphore()
-        for k in range(1, n_mp):
-            pl.semaphore_signal(
-                barrier, inc=1, device_id={"mp": lax.rem(mp + k, n_mp)}, device_id_type=MESH
-            )
-        for k in range(1, n_dp):
-            pl.semaphore_signal(
-                barrier, inc=1, device_id={"dp": lax.rem(dp + k, n_dp)}, device_id_type=MESH
-            )
-        pl.semaphore_wait(barrier, peers_mp + peers_dp)
-        if reduces:
-            first[mp] = in_ref[mp]
-        else:
-            first[mp] = in_ref[...]
-        copies = []
-        for k in range(1, n_mp):
-            peer = lax.rem(mp + k, n_mp)
-            copies.append(
-                pltpu.make_async_remote_copy(
-                    src_ref=in_ref.at[peer] if reduces else in_ref,
-                    dst_ref=first.at[mp],
-                    send_sem=s_mp.at[k - 1],
-                    recv_sem=r_mp.at[k - 1],
-                    device_id={"mp": peer},
-                    device_id_type=MESH,
+def updated(weight, moment, average, gradient, rate):
+    moment_new = momentum_decay * moment + (1.0 - momentum_decay) * gradient
+    weight_new = weight - rate * (
+        (1.0 - momentum_decay) * gradient + momentum_decay * moment_new
+    )
+    average_new = average_decay * average + (1.0 - average_decay) * weight_new
+    return weight_new, moment_new, average_new
+
+
+def store_update(ins, gradient, outs, rate):
+    weight, moment, average = updated(*[ref[...] for ref in ins], gradient, rate)
+    outs[0][...] = weight
+    outs[1][...] = moment
+    outs[2][...] = average
+    outs[3][...] = weight.astype(jnp.bfloat16)
+
+
+def update_call(body, grid, arrays, spec, total, total_spec, scratch, name):
+    kinds = [jnp.float32] * 3 + [jnp.bfloat16]
+    shape = arrays[0].shape
+    return pl.pallas_call(
+        body,
+        grid=grid,
+        out_shape=[jax.ShapeDtypeStruct(shape, kind) for kind in kinds],
+        in_specs=[spec] * 3 + [total_spec],
+        out_specs=[spec] * 4,
+        scratch_shapes=scratch,
+        compiler_params=pltpu.CompilerParams(vmem_limit_bytes=VMEM_LIMIT),
+        cost_estimate=pl.CostEstimate(
+            flops=10 * arrays[0].size, bytes_accessed=28 * arrays[0].size, transcendentals=0
+        ),
+        name=name,
+    )(*arrays, total)
+
+
+def update_flipped(arrays, total, start, rate, name):
+    high, wide = arrays[0].shape
+    step = min(256, high)
+
+    def body(w, m, a, g, *outs):
+        store_update((w, m, a), g[...].astype(jnp.float32).T, outs, rate)
+
+    return update_call(
+        body,
+        (high // step,),
+        arrays,
+        pl.BlockSpec((step, wide), lambda i: (i, 0)),
+        total,
+        pl.BlockSpec((wide, step), lambda i: (0, start // step + i)),
+        [],
+        name,
+    )
+
+
+def update_parts(arrays, total, rate, name):
+    high, parts, wide = arrays[0].shape
+
+    def body(w, m, a, g, *outs):
+        store_update((w, m, a), g[...].astype(jnp.float32), outs, rate)
+
+    turns = 2
+    outs = update_call(
+        body,
+        (parts, turns),
+        [x.transpose(1, 0, 2) for x in arrays],
+        pl.BlockSpec((None, high // turns, wide), lambda i, j: (i, j, 0)),
+        total,
+        pl.BlockSpec((high // turns, wide), lambda i, j: (j, i)),
+        [],
+        name,
+    )
+    return [x.transpose(1, 0, 2) for x in outs]
+
+
+def update_pairs(arrays, total, rate, name):
+    high, parts, wide = arrays[0].shape
+    tiles = wide // 128
+    step = min(16, high)
+    stride = tiles * parts
+
+    def body(w, m, a, g, *rest):
+        outs, spread = rest[:4], rest[4]
+        for part in range(parts):
+            for tile in range(tiles):
+                cols = pl.ds(part * wide + tile * 128, 128)
+                spread[pl.ds(tile * parts + part, step, stride=stride), :] = g[:, cols].astype(
+                    jnp.float32
                 )
-            )
-        for copy in copies:
-            copy.start()
-        for copy in copies:
-            copy.wait()
-        if reduces:
-            total = first[0]
-            for k in range(1, n_mp):
-                total = total + first[k]
-            mid[...] = total
-        else:
-            mid[...] = first[...]
-        second[dp] = mid[dp] if reduces else mid[...]
-        copies = []
-        for k in range(1, n_dp):
-            peer = lax.rem(dp + k, n_dp)
-            copies.append(
-                pltpu.make_async_remote_copy(
-                    src_ref=mid.at[peer] if reduces else mid,
-                    dst_ref=second.at[dp],
-                    send_sem=s_dp.at[k - 1],
-                    recv_sem=r_dp.at[k - 1],
-                    device_id={"dp": peer},
-                    device_id_type=MESH,
+        store_update((w, m, a), spread[...], outs, rate)
+
+    outs = update_call(
+        body,
+        (high // step,),
+        [flat_pairs(x) for x in arrays],
+        pl.BlockSpec((step * stride, 128), lambda i: (i, 0)),
+        total,
+        pl.BlockSpec((step, parts * wide), lambda i: (i, 0)),
+        [pltpu.VMEM((step * stride, 128), jnp.float32)],
+        name,
+    )
+    return [
+        x.reshape(high, tiles, parts, 128).transpose(0, 2, 1, 3).reshape(high, parts, wide)
+        for x in outs
+    ]
+
+
+def weight_gradients(lefts, rights, tile=512):
+    count = len(lefts)
+    rows, depth = lefts[0].shape
+    wide = rights[0].shape[1]
+    steps = wide // tile
+    distinct = []
+    for left in lefts:
+        if all(left is not other for other in distinct):
+            distinct.append(left)
+    which = [next(k for k, d in enumerate(distinct) if d is left) for left in lefts]
+
+    def kernel(*refs):
+        left_refs, right_refs = refs[: len(distinct)], refs[len(distinct) : -1]
+        out_ref = refs[-1]
+        pair = pl.program_id(0)
+        for k in range(count):
+
+            @pl.when(pair == k)
+            def _():
+                out_ref[...] = t_dot(left_refs[which[k]][...], right_refs[k][...]).astype(
+                    jnp.bfloat16
                 )
-            )
-        for copy in copies:
-            copy.start()
-        for copy in copies:
-            copy.wait()
-        if reduces:
-            total = second[0]
-            for k in range(1, n_dp):
-                total = total + second[k]
-            out_ref[...] = total
-        else:
-            out_ref[...] = second[...]
-
-    if reduces:
-        out = (8, 128)
-        first, mid, second = (n_mp, n_dp, 8, 128), (n_dp, 8, 128), (n_dp, 8, 128)
-    else:
-        out = (n_dp, n_mp, 8, 128)
-        first, mid, second = (n_mp, 8, 128), (n_mp, 8, 128), (n_dp, n_mp, 8, 128)
+
+    def right_map(k):
+        return lambda pair, i: (0, jnp.where(pair == k, i, jnp.where(pair < k, 0, steps - 1)))
+
     return pl.pallas_call(
         kernel,
-        out_shape=jax.ShapeDtypeStruct(out, jnp.float32),
-        in_specs=[VMEM],
-        out_specs=VMEM,
-        scratch_shapes=[
-            pltpu.VMEM(first, jnp.float32),
-            pltpu.VMEM(second, jnp.float32),
-            pltpu.VMEM(mid, jnp.float32),
-            pltpu.SemaphoreType.DMA((peers_mp,)),
-            pltpu.SemaphoreType.DMA((peers_mp,)),
-            pltpu.SemaphoreType.DMA((peers_dp,)),
-            pltpu.SemaphoreType.DMA((peers_dp,)),
-        ],
-        compiler_params=pltpu.CompilerParams(collective_id=collective_id, has_side_effects=True),
-        name="sum_small" if reduces else "gather_small",
-    )(table)
-
-
-def gather_gains(n_dp, n_mp, gains, collective_id):
-    local = gains.shape[1]
-    flat = jnp.pad(gains.reshape(1, 2 * local), ((0, 7), (0, 128 - 2 * local)))
-    whole = small_exchange(n_dp, n_mp, flat, False, collective_id)
-    rows = whole[:, :, 0, : 2 * local].reshape(n_dp * n_mp, 2, local)
-    return rows.transpose(1, 0, 2).reshape(2, n_dp * n_mp * local)
-
-
-def scatter_gains(n_dp, n_mp, partial, collective_id):
-    local = partial.shape[1] // (n_dp * n_mp)
-    table = partial.reshape(2, n_dp, n_mp, local).transpose(2, 1, 0, 3)
-    table = table.reshape(n_mp, n_dp, 1, 2 * local)
-    table = jnp.pad(table, ((0, 0), (0, 0), (0, 7), (0, 128 - 2 * local)))
-    out = small_exchange(n_dp, n_mp, table, True, collective_id)
-    return out[0, : 2 * local].reshape(2, local)
+        grid=(count, steps),
+        out_shape=jax.ShapeDtypeStruct((depth, count * wide), jnp.bfloat16),
+        in_specs=[VMEM] * len(distinct)
+        + [pl.BlockSpec((rows, tile), right_map(k)) for k in range(count)],
+        out_specs=pl.BlockSpec((depth, tile), lambda pair, i: (0, pair * steps + i)),
+        compiler_params=pltpu.CompilerParams(vmem_limit_bytes=VMEM_LIMIT),
+        cost_estimate=pl.CostEstimate(
+            flops=2 * rows * depth * count * wide,
+            bytes_accessed=2 * (len(distinct) * rows * depth + count * wide * (rows + depth)),
+            transcendentals=0,
+        ),
+        name="weight_gradients",
+    )(*distinct, *rights)
 
 
 def rope_tables(length, half_dim):
-    positions = jnp.arange(length, dtype=jnp.float32)[:, None]
-    inverse_freq = rope_base ** (-jnp.arange(half_dim, dtype=jnp.float32) / half_dim)
+    positions = np.arange(length, dtype=np.float32)[:, None]
+    inverse_freq = np.power(
+        np.float32(rope_base), -np.arange(half_dim, dtype=np.float32) / np.float32(half_dim)
+    )
     angles = positions * inverse_freq[None, :]
-    cosine, sine = jnp.cos(angles), jnp.sin(angles)
-    return jnp.concatenate([cosine, cosine], axis=1), jnp.concatenate([-sine, sine], axis=1)
-
-
-def update(weight, moment, average, gradient, step_size):
-    moment_new = momentum_decay * moment + (1.0 - momentum_decay) * gradient
-    weight_new = weight - step_size * (
-        (1.0 - momentum_decay) * gradient + momentum_decay * moment_new
-    )
-    average_new = average_decay * average + (1.0 - average_decay) * weight_new
-    return (weight_new, moment_new, average_new)
+    cosine, sine = np.cos(angles), np.sin(angles)
+    return np.concatenate([cosine, cosine], axis=1), np.concatenate([-sine, sine], axis=1)
 
 
 def per_device(
@@ -698,26 +1350,21 @@
         [w_qkv.reshape(owned, 3 * local_width), w_out.T], axis=1
     ).astype(half)
     attn_w = lax.all_gather(attn_part, "dp", axis=0, tiled=True)
-    ffn_part = jnp.concatenate([w_gu.reshape(owned, 2 * hidden), w_down.T], axis=1).astype(half)
-    ffn_w = lax.all_gather(ffn_part, "dp", axis=0, tiled=True)
-    qkv_w, out_wt = attn_w[:, : 3 * local_width], attn_w[:, 3 * local_width :]
-    down_wt = ffn_w[:, 2 * hidden :]
-
-    gain_all = gather_gains(n_dp, n_mp, gains, 0)
     row_ids = lax.axis_index("mp") * row_count + jnp.arange(row_count, dtype=jnp.int32)
     live_rows = (row_ids < valid_len).astype(jnp.float32)[:, None]
+    key_mask = (jnp.arange(SEQ, dtype=jnp.int32) < valid_len).astype(jnp.float32)
+    ffn_part, tokens_in = lax.optimization_barrier((round_shares(w_gu, w_down), tokens))
+    h_first, gain_all, out_grad, own_branch = gather_first(
+        n_dp, n_mp, tokens_in, gains, cotangent, live_rows, 1
+    )
+    ffn_w = lax.all_gather(ffn_part, "dp", axis=0, tiled=True)
+    out_wt = attn_w[:, 3 * local_width :]
     xin = tokens.astype(jnp.float32)
-    inverse = lax.rsqrt(jnp.mean(xin * xin, axis=1, keepdims=True) + norm_eps)
-    normed_first = (xin * inverse * gain_all[0][None, :]).astype(half)
-    h_first = gather_rows(n_mp, normed_first, 1)
-    out_grad = cotangent.astype(jnp.float32) * live_rows
-    cosine, sine = rope_tables(SEQ, HDIM // 2)
-    key_mask = (jnp.arange(SEQ, dtype=jnp.int32) < valid_len).astype(jnp.float32)
-
-    joined = dot(h_first, qkv_w)
+    cosine, sine = (jnp.asarray(x, jnp.float32) for x in rope_tables(SEQ, HDIM // 2))
+
     second, normed_second, queries, keys, values, mixed, branch_grad = scatter_rows(
         n_mp,
-        [joined],
+        [h_first],
         attn_w,
         3 * local_width,
         [xin],
@@ -725,27 +1372,17 @@
         gain_all[1:2],
         2,
         heads=(cosine, sine, key_mask[None, :]),
-        extra=out_grad.astype(half),
-    )
-
-    h_second = gather_rows(n_mp, normed_second, 6)
-    gate_val = dot(h_second, ffn_w[:, :hidden])
-    up_val = dot(h_second, ffn_w[:, hidden : 2 * hidden])
-    act = (jax.nn.silu(gate_val) * up_val).astype(half)
-    act_grad = dot(branch_grad, down_wt)
-    sigma = jax.nn.sigmoid(gate_val)
-    gate_grad = (act_grad * up_val * sigma * (1.0 + gate_val * (1.0 - sigma))).astype(half)
-    up_grad = (act_grad * gate_val * sigma).astype(half)
-    grad_ffn = jnp.zeros((width, 3 * hidden), half)
-    for k, (a, b) in enumerate(
-        ((h_second, gate_grad), (h_second, up_grad), (branch_grad, act))
-    ):
-        grad_ffn = lax.dynamic_update_slice(grad_ffn, t_dot(a, b).astype(half), (0, k * hidden))
-    grad_ffn, gate_grad = lax.optimization_barrier((grad_ffn, gate_grad))
+        extra=own_branch,
+    )
+
+    second_grad, own_grad, gain_two, h_second, act, gate_grad, up_grad = feed_forward(
+        n_mp, normed_second, branch_grad, ffn_w, [second, out_grad], gain_all[1:2], 3
+    )
+    grad_ffn = weight_gradients(
+        [h_second, h_second, branch_grad], [gate_grad, up_grad, act]
+    )
+    grad_ffn, own_grad = lax.optimization_barrier((grad_ffn, own_grad))
     sum_ffn = lax.psum_scatter(grad_ffn, "dp", scatter_dimension=0, tiled=True)
-    second_grad, gain_two, own_grad = scatter_rows(
-        n_mp, [gate_grad, up_grad], ffn_w, 0, [second, out_grad], "backward", gain_all[1:2], 3
-    )
     block_out, attn_grad = scatter_rows(
         n_mp,
         [act],
@@ -762,50 +1399,40 @@
     joined_grad = attention_backward(
         queries, keys, values, mixed_grad, cosine, sine, key_mask[:, None]
     )
-    grad_attn = jnp.zeros((width, 4 * local_width), half)
-    for k, (a, b) in enumerate(
-        (
-            (h_first, joined_grad[0]),
-            (h_first, joined_grad[1]),
-            (h_first, joined_grad[2]),
-            (attn_grad, mixed),
-        )
-    ):
-        grad_attn = lax.dynamic_update_slice(
-            grad_attn, t_dot(a, b).astype(half), (0, k * local_width)
-        )
-    grad_attn, second_grad = lax.optimization_barrier((grad_attn, second_grad))
-    grad_attn, sum_ffn = lax.optimization_barrier((grad_attn, sum_ffn))
-    sum_attn = lax.psum_scatter(grad_attn, "dp", scatter_dimension=0, tiled=True)
-    input_grad, gain_one = scatter_rows(
+    input_grad, gain_tile, sum_attn = scatter_rows(
         n_mp,
-        [joined_grad[0], joined_grad[1], joined_grad[2]],
+        list(joined_grad),
         attn_w,
         0,
         [xin, second_grad],
         "last",
         gain_all[0:1],
         4,
-    )
-    gain_partial = jnp.stack([gain_one.sum(axis=0), gain_two.sum(axis=0)], axis=0)
-    sum_gains = scatter_gains(n_dp, n_mp, gain_partial, 5)
+        other_gain=gain_two,
+        grad_lefts=[h_first, attn_grad],
+        grad_right=mixed,
+        n_dp=n_dp,
+    )
 
     total_rows = SEQ * n_dp
     matrix_rate = step_rate / math.sqrt(total_rows)
     scale_rate = gain_rate / math.sqrt(total_rows)
-    sum_attn = sum_attn.astype(jnp.float32)
-    sum_ffn = sum_ffn.astype(jnp.float32)
-    sum_qkv = sum_attn[:, : 3 * local_width].reshape(owned, 3, local_width)
-    sum_out = sum_attn[:, 3 * local_width :].T
-    sum_gu = sum_ffn[:, : 2 * hidden].reshape(owned, 2, hidden)
-    sum_down = sum_ffn[:, 2 * hidden :].T
-    new_qkv, next_mom_qkv, next_avg_qkv = update(w_qkv, mom_qkv, avg_qkv, sum_qkv, matrix_rate)
-    new_out, next_mom_out, next_avg_out = update(w_out, mom_out, avg_out, sum_out, matrix_rate)
-    new_gu, next_mom_gu, next_avg_gu = update(w_gu, mom_gu, avg_gu, sum_gu, matrix_rate)
-    new_down, next_mom_down, next_avg_down = update(
-        w_down, mom_down, avg_down, sum_down, matrix_rate
-    )
-    new_gains, next_mom_gains, next_avg_gains = update(
+    local = gains.shape[1]
+    place = lax.rem((lax.axis_index("dp") * n_mp + lax.axis_index("mp")) * local, 128)
+    sum_gains = lax.dynamic_slice(gain_tile.reshape(2, 8, 128).sum(axis=1), (0, place), (2, local))
+    new_gu, next_mom_gu, next_avg_gu, copy_gu = update_pairs(
+        [w_gu, mom_gu, avg_gu], sum_ffn, matrix_rate, "update_gu"
+    )
+    new_down, next_mom_down, next_avg_down, copy_down = update_flipped(
+        [w_down, mom_down, avg_down], sum_ffn, 2 * hidden, matrix_rate, "update_down"
+    )
+    new_qkv, next_mom_qkv, next_avg_qkv, copy_qkv = update_parts(
+        [w_qkv, mom_qkv, avg_qkv], sum_attn, matrix_rate, "update_qkv"
+    )
+    new_out, next_mom_out, next_avg_out, copy_out = update_flipped(
+        [w_out, mom_out, avg_out], sum_attn, 3 * local_width, matrix_rate, "update_out"
+    )
+    new_gains, next_mom_gains, next_avg_gains = updated(
         gains, mom_gains, avg_gains, sum_gains, scale_rate
     )
     return (
@@ -826,10 +1453,10 @@
         next_avg_gu,
         next_avg_down,
         next_avg_gains,
-        new_qkv.astype(half),
-        new_out.astype(half),
-        new_gu.astype(half),
-        new_down.astype(half),
+        copy_qkv,
+        copy_out,
+        copy_gu,
+        copy_down,
     )
 
 

time: 830 us -> 649 us (0.78)
  matrix products: 123 us -> 6.54 us
  local copies, waits for them, and re-layouts: 83.4 us -> 8.79 us
  Pallas kernels: 538 us -> 605 us
  other arithmetic: 60.2 us -> 5.47 us
    pallas_call x4 -> x8, Pallas kernels: 171 us -> 300 us  [the longest x1 143 us: feed_forward(): pl.pallas_call(kernel, out_shape=[jax.ShapeDtypeStruct((rows, width), jnp...]
    pallas_call x4 -> x3, Pallas kernels: 354 us -> 293 us  [scatter_rows(): pl.pallas_call(kernel, out_shape=out_shape, in_specs=[VMEM] * count + [AN...]
    dot_general x5 -> x1, matrix products: 67.7 us -> 6.54 us  [dot(): return jnp.dot(left, right, preferred_element_type=jnp.float32)]
    dot_general x7 -> x0, matrix products: 55.3 us -> none  [t_dot(): lax.dot_general(left, right, (((0,), (0,)), ((), ())), preferred_element_...]
    unnamed x92 -> x20, local copies, waits for them, and re-layouts: 53.7 us -> 6.3 us
    convert_element_type x7 -> x0, other arithmetic: 26.2 us -> none  [the longest x1 11 us: per_device(): new_gu.astype(half)]
    dynamic_update_slice x2 -> x0, local copies, waits for them, and re-layouts: 17.1 us -> none  [the longest x1 12.7 us: per_device(): lax.dynamic_update_slice(grad_ffn, t_dot(a, b).astype(half), (0, k * hidd...]
    add x5 -> x1, other arithmetic: 13 us -> 0.65 us  [updated(): average_new = average_decay * average + (1.0 - average_decay) * weight_new]
  transfers between devices with their start and end apart: 4 -> 3, of which waited for: 0 -> 0; matrix products, arithmetic and copies ran while one was open for 15% -> 2% of each run, Pallas kernels for 66% -> 63%
where the time goes in v3:
time: 649 us; the launch traced here: 641 us
  Pallas kernels  605 us (93%)
  between operations  14.9 us (2%)
  local copies, waits for them, and re-layouts  8.79 us (1%)
  matrix products  6.54 us (1%)
    pallas_call x3, Pallas kernels, scatter_rows(): pl.pallas_call(kernel, out_shape=out_shape, in_specs=[VMEM] * count + [AN...  293 us
    pallas_call x1, Pallas kernels, feed_forward(): pl.pallas_call(kernel, out_shape=[jax.ShapeDtypeStruct((rows, width), jnp...  143 us
    pallas_call x1, Pallas kernels, gather_first(): pl.pallas_call(kernel, out_shape=[jax.ShapeDtypeStruct((n_mp * rows, widt...  79.9 us
    pallas_call x1, Pallas kernels, weight_gradients(): pl.pallas_call(kernel, grid=(count, steps), out_shape=jax.ShapeDtypeStruc...  35.6 us
    pallas_call x4, Pallas kernels, update_call(): pl.pallas_call(body, grid=grid, out_shape=[jax.ShapeDtypeStruct(shape, ki...  35.4 us
  transfers between devices with their start and end apart: 3, of which 0 were waited for; matrix products, arithmetic and copies ran while one was open for 2% of the time, Pallas kernels for 63%

profile of v3, /device:TPU:0, one launch (start us, length us, event | category | flops | bytes accessed | tf_op | source)
XLA Modules:
  0.0 641.2 jit_solution(3690744319277478923)
XLA Ops:
  7.2 1.7 copy.62
  9.4 1.1 pad_maximum_fusion
  10.6 6.6 %round_shares.1 = bf16[256,6144]{1,0:T(8,128)(2,1)} custom-call(f32[8192,128]{1,0:T(8,128)} %bitcast.53, f32[2048,256]{1,0:T(8,128)} %w.3), custom_call_target="tpu_custom_call" | custom-call | bytes 9437184 | tf_op jit(solution)/shard_map/round_shares/pallas_call | solution.py:213
  17.3 1.1 copy-done
  18.5 1.6 convert_element_type.37.refs_3_.refs_5_
  21.4 0.7 fusion.6.live_ref
  22.1 79.9 %gather_first.1 = (bf16[1024,2048]{1,0:T(8,128)(2,1)}, f32[8,2048]{1,0:T(8,128)}, f32[256,2048]{1,0:T(8,128)}, bf16[256,2048]{1,0:T(8,128)(2,1)}) custom-call(bf16[256,2048]{1,0:T(8,128)(2,1)} %own_ref, f32[8,128]{1,0:T(8,128)} %concatenate.7.tile_ref, bf16[256,2048]{1,0:T(8,128)(2,1)} %cotangent_ref.1, f32[256,1]{1,0:T(8,128)} %fusion.6.live_ref), custom_call_target="tpu_custom_call" | custom-call | bytes 209715200 | tf_op jit(solution)/shard_map/gather_first/pallas_call | solution.py:318
  102.5 1.5 fusion.8
  104.1 102.0 %scatter_forward.1 = (f32[256,2048]{1,0:T(8,128)}, bf16[256,2048]{1,0:T(8,128)(2,1)}, bf16[1024,512]{1,0:T(8,128)(2,1)}, bf16[1024,512]{1,0:T(8,128)(2,1)}, bf16...) custom-call(bf16[1024,2048]{1,0:T(8,128)(2,1)} %get-tuple-element.68.refs_0_.refs_8_, ...), custom_call_target="tpu_custom_call" | custom-call | flops 2147483648 | bytes 300000000 | tf_op jit(solution)/shard_map/scatter_forward/pallas_call | solution.py:811
  206.1 142.6 %feed_forward.1 = (f32[256,2048]{1,0:T(8,128)}, bf16[256,2048]{1,0:T(8,128)(2,1)}, f32[8,2048]{1,0:T(8,128)}, bf16[1024,2048]{1,0:T(8,128)(2,1)}, bf16[1024,2048...) custom-call(bf16[256,2048]{1,0:T(8,128)(2,1)} %get-tuple-element.71.normed_ref, ...), custom_call_target="tpu_custom_call" | custom-call | flops 42949672960 | bytes 300000000 | tf_op jit(solution)/shard_map/feed_forward/pallas_call | solution.py:1074
  348.7 35.6 %weight_gradients.1 = bf16[2048,6144]{1,0:T(8,128)(2,1)} custom-call(bf16[1024,2048]{1,0:T(8,128)(2,1)} %get-tuple-element.77.refs_0_, bf16[1024,2048]{1,0:T(8,128)(2,1)} %get-tuple-element.72.branch_hbm.refs_1_, bf16[1024,2048]{1,0:T(8,128)(2,1)} %get-tuple-element.78.refs_2_, bf16[1024,2048]{1,0:T(8,128)(2,1)} %get-tuple-element.79.refs_3_, ...), custom_call_target="tpu_custom_call" | custom-call | flops 25769803776 | bytes 46137344 | tf_op jit(solution)/shard_map/weight_gradients/pallas_call | solution.py:1294
  384.4 0.8 fusion.5.mask_ref
  385.2 92.8 %scatter_residual.1 = (bf16[256,2048]{1,0:T(8,128)(2,1)}, bf16[1024,2048]{1,0:T(8,128)(2,1)}) custom-call(bf16[1024,2048]{1,0:T(8,128)(2,1)} %get-tuple-element.76.refs_4_.refs_0_, bf16[2048,6144]{1,0:T(8,128)(2,1)} %all-gather.5.cloned.1.call-done.weights_hbm.refs_1_, f32[1,2048]{1,0:T(1,128)} %get-tuple-element.117.refs_2_.gain_ref, ...), custom_call_target="tpu_custom_call" | custom-call | flops 8589934592 | bytes 300000000 | tf_op jit(solution)/shard_map/scatter_residual/pallas_call | solution.py:811
  478.0 6.5 %fusion.2.do_ref = bf16[1024,512]{1,0:T(8,128)(2,1)} fusion(bf16[1024,2048]{1,0:T(8,128)(2,1)} %get-tuple-element.86.refs_9_, bf16[2048,2048]{1,0:T(8,128)(2,1)} %all-gather.3.cloned.1.call-done.refs_1_.refs_3_), kind=kOutput, calls=%fused_computation.2 | convolution fusion | flops 2148007936 | bytes 7340032 | tf_op jit(solution)/shard_map/dot_general | solution.py:358
  484.6 12.5 %attention_backward.1 = (bf16[1024,512]{1,0:T(8,128)(2,1)}, bf16[1024,512]{1,0:T(8,128)(2,1)}, bf16[1024,512]{1,0:T(8,128)(2,1)}) custom-call(bf16[1024,512]{1,0:T(8,128)(2,1)} %get-tuple-element.83.q_ref, bf16[1024,512]{1,0:T(8,128)(2,1)} %get-tuple-element.84.k_ref, bf16[1024,512]{1,0:T(8,128)(2,1)} %get-tuple-element.85.v_ref, ...), custom_call_target="tpu_custom_call" | custom-call | flops 4294967296 | bytes 7340032 | tf_op jit(solution)/shard_map/attention_backward/pallas_call | solution.py:1145
  497.1 98.0 %scatter_last.1 = (f32[256,2048]{1,0:T(8,128)}, f32[16,128]{1,0:T(8,128)}, f32[256,2048]{1,0:T(8,128)}) custom-call(bf16[1024,512]{1,0:T(8,128)(2,1)} %get-tuple-element.87.refs_0_, bf16[1024,512]{1,0:T(8,128)(2,1)} %get-tuple-element.88.refs_1_, bf16[1024,512]{1,0:T(8,128)(2,1)} %get-tuple-element.89.refs_2_, ...), custom_call_target="tpu_custom_call" | custom-call | flops 6442450944 | bytes 300000000 | tf_op jit(solution)/shard_map/scatter_last/pallas_call | solution.py:811
  595.1 2.6 update_out.1
  597.7 6.6 %update_qkv.1 = (f32[3,256,512]{2,1,0:T(8,128)}, f32[3,256,512]{2,1,0:T(8,128)}, f32[3,256,512]{2,1,0:T(8,128)}, bf16[3,256,512]{2,1,0:T(8,128)(2,1)}) custom-call(f32[3,256,512]{2,1,0:T(8,128)} %bitcast.55, f32[3,256,512]{2,1,0:T(8,128)} %bitcast.59, f32[3,256,512]{2,1,0:T(8,128)} %bitcast.60, f32[256,2048]{1,0:T(8,128)} %get-tuple-element.94.g), custom_call_target="tpu_custom_call" | custom-call | flops 3932160 | bytes 11010048 | tf_op jit(solution)/shard_map/update_qkv/pallas_call | solution.py:1182
  604.4 0.7 multiply_add_fusion
  605.0 17.4 %update_gu.1 = (f32[8192,128]{1,0:T(8,128)}, f32[8192,128]{1,0:T(8,128)}, f32[8192,128]{1,0:T(8,128)}, bf16[8192,128]{1,0:T(8,128)(2,1)}) custom-call(f32[8192,128]{1,0:T(8,128)} %bitcast.54, f32[8192,128]{1,0:T(8,128)} %bitcast.56, f32[8192,128]{1,0:T(8,128)} %bitcast.57, bf16[256,6144]{1,0:T(8,128)(2,1)} %reduce-scatter.2.cloned.1.call-done.g), custom_call_target="tpu_custom_call" | custom-call | flops 10485760 | bytes 29360128 | tf_op jit(solution)/shard_map/update_gu/pallas_call | solution.py:1182
  622.5 8.7 %update_down.1 = (f32[2048,256]{1,0:T(8,128)}, f32[2048,256]{1,0:T(8,128)}, f32[2048,256]{1,0:T(8,128)}, bf16[2048,256]{1,0:T(8,128)(2,1)}) custom-call(f32[2048,256]{1,0:T(8,128)} %w.3, f32[2048,256]{1,0:T(8,128)} %m.3, f32[2048,256]{1,0:T(8,128)} %a.3, bf16[256,6144]{1,0:T(8,128)(2,1)} %reduce-scatter.2.cloned.1.call-done.g), custom_call_target="tpu_custom_call" | custom-call | flops 5242880 | bytes 14680064 | tf_op jit(solution)/shard_map/update_down/pallas_call | solution.py:1182
  631.2 1.0 copy.74
  632.1 1.0 copy-done.2
  633.1 1.3 copy.75
  (32 shorter events, 2.0 us)
Async XLA Ops:
  7.2 2.1 copy-start.1
  7.2 96.9 %all-gather.3.cloned.1.call-start = ((), (), s32[]{:S(2)}) async-start(), calls=%async_computation.1 | async-start | bytes 9437184 | tf_op jit(solution)/shard_map/all_gather | solution.py:1352
  10.5 195.6 %all-gather.5.cloned.1.call-start = ((), (), s32[]{:S(2)}) async-start(), calls=%async_computation.2 | async-start | bytes 28311552 | tf_op jit(solution)/shard_map/all_gather | solution.py:1360
  17.2 1.2 copy-start
  17.3 2.8 copy-start.5
  17.3 587.8 %reduce-scatter.2.cloned.1.call-start = ((), (), s32[]{:S(2)}) async-start(), calls=%async_computation.3 | async-start | bytes 28311552 | tf_op jit(solution)/shard_map/reduce_scatter | solution.py:1385
  597.7 6.7 %copy-start.4 = (f32[16,128]{1,0:T(8,128)S(1)}, f32[16,128]{1,0:T(8,128)}, u32[]{:S(2)}) copy-start(f32[16,128]{1,0:T(8,128)} %get-tuple-element.100) | copy-start | bytes 24580
  597.7 6.7 %copy-start.6 = (f32[2,64]{1,0:T(2,128)S(1)}, f32[2,64]{1,0:T(2,128)}, u32[]{:S(2)}) copy-start(f32[2,64]{1,0:T(2,128)} %param.37) | copy-start | bytes 1540
  597.7 6.7 %copy-start.7 = (f32[2,64]{1,0:T(2,128)S(1)}, f32[2,64]{1,0:T(2,128)}, u32[]{:S(2)}) copy-start(f32[2,64]{1,0:T(2,128)} %param.32) | copy-start | bytes 1540
  622.5 8.7 %copy-start.3 = (bf16[256,2048]{1,0:T(8,128)(2,1)S(1)}, bf16[256,2048]{1,0:T(8,128)(2,1)}, u32[]{:S(2)}) copy-start(bf16[256,2048]{1,0:T(8,128)(2,1)} %get-tuple-element.139) | copy-start | bytes 3145732
  631.1 2.0 copy-start.2
Sparse Core Ops, SparseCore 0:
  10.7 58.4 all-gather.2
  71.6 125.3 all-gather.4
  384.5 182.9 reduce-scatter.1

commit v4 on v3

--- a/solution.py
+++ b/solution.py
@@ -378,6 +378,7 @@
     collective_id,
     heads=None,
     extra=None,
+    extra_right=None,
     other_gain=None,
     grad_lefts=None,
     grad_right=None,
@@ -399,6 +400,8 @@
     else:
         pieces = [a.shape[1] for a in lhs]
     depth = sum(pieces)
+    if extra_right is not None:
+        extra_width = extra_right[0].shape[1] - extra_right[1]
 
     def kernel(*refs):
         refs = list(refs)
@@ -409,22 +412,30 @@
         left_refs = take(count)
         (right_hbm,) = take(1)
         (gain_ref,) = take(1)
-        own = take(len(own_rows))
+        own_hbm = take(len(own_rows))
         if heads is not None:
             cosine_ref, sine_ref, mask_ref = take(3)
         if other_gain is not None:
             (other_ref,) = take(1)
-            grad_left_refs, grad_right_ref = take(2), take(1)[0]
+            grad_hbm = take(3)
         extra_ref = take(1)[0] if extra is not None else None
+        extra_right_hbm = take(1)[0] if extra_right is not None else None
         outs = take(1 + has_gain)
         owned_ref = take(1)[0] if other_gain is not None else None
         normed = take(1)[0] if has_norm else None
         if heads is not None:
             query_ref, key_ref, value_ref, mixed_ref = take(4)
         extra_whole = take(1)[0] if extra is not None else None
+        if extra_right is not None:
+            (extra_out,) = take(1)
         right, held, sent, part = take(4)
         joined_ref = take(1)[0] if heads is not None else None
         right_sem, send_sems, recv_sems = take(3)
+        own, own_sems = take(len(own_rows)), take(1)[0]
+        own_loads = [
+            pltpu.make_async_copy(hbm, ref, own_sems.at[k])
+            for k, (hbm, ref) in enumerate(zip(own_hbm, own))
+        ]
         me = lax.axis_index("mp")
         fetch = pltpu.make_async_copy(
             right_hbm.at[:, pl.ds(rhs_start, depth)], right, right_sem
@@ -438,12 +449,38 @@
             fetch_joined.start()
         if extra is not None:
             (extra_sem,) = take(1)
-            extra_gather = LineGather(n, rows, 1, extra_ref, extra_whole, take(4))
-            extra_local = pltpu.make_async_copy(extra_ref, extra_gather.at(me, 0), extra_sem)
-            extra_local.start()
+            extra_sems = take(4)
+            if extra_right is None:
+                extra_gather = LineGather(n, rows, 1, extra_ref, extra_whole, extra_sems)
+                extra_local = pltpu.make_async_copy(extra_ref, extra_gather.at(me, 0), extra_sem)
+                extra_local.start()
+            else:
+                extra_all, extra_right_ref, extra_right_sem = take(3)
+                extra_gather = LineGather(n, rows, 1, extra_ref, extra_all, extra_sems)
+                extra_fetch = pltpu.make_async_copy(
+                    extra_right_hbm.at[:, pl.ds(extra_right[1], extra_width)],
+                    extra_right_ref,
+                    extra_right_sem,
+                )
+                extra_fetch.start()
+
+                def extra_product(block_id):
+                    @pl.when((block_id >= 0) & (block_id < n))
+                    def _():
+                        span = rows_at(block_id * rows, rows)
+                        extra_out[span, :] = dot(
+                            extra_all[span, :], extra_right_ref[...]
+                        ).astype(jnp.bfloat16)
         if other_gain is not None:
             gain_sum, table, first, middle, second = take(5)
             exchange = Exchange(n_dp, n, take(4))
+            *grad_left_refs, grad_right_ref, grad_load_sems = take(4)
+            grad_loads = [
+                pltpu.make_async_copy(hbm, ref, grad_load_sems.at[k])
+                for k, (hbm, ref) in enumerate(zip(grad_hbm, [*grad_left_refs, grad_right_ref]))
+            ]
+            for load in grad_loads:
+                load.start()
             grads, paired, landed = take(3)
             pair_send, pair_recv, land_send, land_recv = take(4)
             dp = lax.axis_index("dp")
@@ -474,6 +511,8 @@
             ]
 
             def make_grads():
+                for load in grad_loads:
+                    load.wait()
                 start, narrow = 0, 256
                 for k, right_ref in enumerate([*left_refs, grad_right_ref]):
                     left_ref = grad_left_refs[0 if k < count else 1]
@@ -488,8 +527,6 @@
                     start += right_ref.shape[1]
                 for copy in pair_copies:
                     copy.start()
-
-            def pair_up():
                 for copy in pair_copies:
                     copy.wait()
 
@@ -526,6 +563,9 @@
             neighbour_barrier(n)
         if extra is not None:
             extra_gather.send_own(0)
+        if extra_right is not None:
+            extra_all[rows_at(me * rows, rows), :] = extra_ref[...]
+            extra_fetch.wait()
         if heads is not None:
             turn = 256
             fetch_joined.wait()
@@ -544,6 +584,8 @@
                 return carry
 
             lax.fori_loop(0, total_rows // turn, enter, 0)
+        for load in own_loads:
+            load.start()
         fetch.wait()
 
         def attend(block_id):
@@ -651,15 +693,21 @@
                 @pl.when(step < n - 1)
                 def _():
                     extra_gather.forward(step)
+                    if extra_right is not None:
+                        extra_product(me - step)
+                        extra_product(me + step)
 
             if other_gain is not None:
                 pl.when(step == 1)(make_grads)
-                pl.when(step == 2)(pair_up)
 
             return carry
 
         lax.fori_loop(1, n, step_of, 0)
         product(me)
+        if extra_right is not None:
+            extra_product(me)
+        for load in own_loads:
+            load.wait()
         if has_gain:
             gain_sum[...] = jnp.zeros_like(gain_sum)
         for chunk in range(chunks):
@@ -684,14 +732,14 @@
                 if epilogue == "residual":
                     outs[0][span, :] = (own[0][span, :] + total).astype(jnp.bfloat16)
                 elif epilogue == "forward":
-                    value = own[0][span, :] + total
+                    value = own[0][span, :].astype(jnp.float32) + total
                     outs[0][span, :] = value
                     inverse = lax.rsqrt(
                         jnp.mean(value * value, axis=1, keepdims=True) + norm_eps
                     )
                     normed[span, :] = (value * inverse * gain).astype(jnp.bfloat16)
                 else:
-                    value = own[0][span, :]
+                    value = own[0][span, :].astype(jnp.float32)
                     inverse = lax.rsqrt(
                         jnp.mean(value * value, axis=1, keepdims=True) + norm_eps
                     )
@@ -710,6 +758,12 @@
             lax.fori_loop(0, size // block, body, 0)
         if extra is not None:
             extra_gather.finish()
+        if extra_right is not None:
+            extra_local = pltpu.make_async_copy(extra_all, extra_whole, extra_sem)
+            extra_local.start()
+            extra_product(me - (n - 1))
+            extra_product(me + (n - 1))
+        if extra is not None:
             extra_local.wait()
         if other_gain is not None:
             local = width // (n * n_dp)
@@ -780,6 +834,8 @@
         pltpu.SemaphoreType.DMA((n * chunks,)),
         pltpu.SemaphoreType.DMA(((n + 1) * chunks,)),
     ]
+    scratch += [pltpu.VMEM(x.shape, x.dtype) for x in own_rows]
+    scratch.append(pltpu.SemaphoreType.DMA((len(own_rows),)))
     head_args = []
     if heads is not None:
         scratch.append(pltpu.SemaphoreType.DMA)
@@ -792,8 +848,19 @@
         out_specs.append(ANY)
         scratch += [pltpu.SemaphoreType.DMA] + gather_sems(n, 1)
         extra_args = [extra]
+    if extra_right is not None:
+        out_shape.append(jax.ShapeDtypeStruct((total_rows, extra_width), jnp.bfloat16))
+        out_specs.append(VMEM)
+        scratch += [
+            pltpu.VMEM((total_rows, width), jnp.bfloat16),
+            pltpu.VMEM((width, extra_width), jnp.bfloat16),
+            pltpu.SemaphoreType.DMA,
+        ]
+        extra_args.append(extra_right[0])
+    late_args = []
     if other_gain is not None:
-        head_args += [other_gain, *grad_lefts, grad_right]
+        head_args.append(other_gain)
+        late_args = [*grad_lefts, grad_right]
         scratch += [
             pltpu.VMEM((8, width), jnp.float32),
             pltpu.VMEM((n, n_dp, 16, 128), jnp.float32),
@@ -801,6 +868,8 @@
             pltpu.VMEM((n_dp, 16, 128), jnp.float32),
             pltpu.VMEM((n_dp, 16, 128), jnp.float32),
         ] + exchange_sems(n_dp, n)
+        scratch += [pltpu.VMEM(x.shape, x.dtype) for x in late_args]
+        scratch.append(pltpu.SemaphoreType.DMA((len(late_args),)))
         chips = n_dp // 2
         scratch.append(pltpu.VMEM((width, grad_width), jnp.bfloat16))
         scratch.append(pltpu.VMEM((chips, share, grad_width), jnp.bfloat16))
@@ -813,8 +882,12 @@
         out_shape=out_shape,
         in_specs=[VMEM] * count
         + [ANY]
-        + [VMEM] * (1 + len(own_rows) + len(head_args))
-        + [ANY] * len(extra_args),
+        + [VMEM]
+        + [ANY] * len(own_rows)
+        + [VMEM] * len(head_args)
+        + [ANY] * len(late_args)
+        + [VMEM if extra_right is not None else ANY] * min(1, len(extra_args))
+        + [ANY] * max(0, len(extra_args) - 1),
         out_specs=out_specs,
         scratch_shapes=scratch,
         compiler_params=pltpu.CompilerParams(
@@ -824,30 +897,34 @@
             flops=flops, bytes_accessed=300_000_000, transcendentals=0
         ),
         name="scatter_" + epilogue,
-    )(*lhs, rhs, gains_row, *own_rows, *head_args, *extra_args)
-
-
-def feed_forward(n, normed, branch_grad, weights, own_rows, gains_row, collective_id, chunks=1, hops=4):
+    )(*lhs, rhs, gains_row, *own_rows, *head_args, *late_args, *extra_args)
+
+
+def feed_forward(n, normed, branch_grad, weights, second, gains_row, collective_id, halves=1, hops=4):
     rows, width = normed.shape
     total_rows = n * rows
     hidden = weights.shape[1] // 3
-    size = rows // chunks
-    part_size = size // hops
-    count = chunks * hops
+    count, parcels = hops, halves
+    part_size = rows // hops
     tile = min(1024, hidden)
     block = min(32, part_size)
+    narrow = min(256, hidden)
+    per = hidden // narrow
+    pieces = 3 * per
+    before = pieces // 6
+    between = (pieces - 2 * before) // (count + 1)
+    tall = min(1024, width)
 
     def kernel(
         normed_ref,
         branch_hbm,
         weights_hbm,
         second_ref,
-        base_ref,
         gain_ref,
         result_ref,
         rounded_ref,
         gain_sum,
-        whole_hbm,
+        grads_hbm,
         act_hbm,
         gate_hbm,
         up_hbm,
@@ -860,8 +937,11 @@
         act_ref,
         gate_ref,
         up_ref,
+        piece_ref,
         load_sems,
         stage_sems,
+        piece_sems,
+        grad_sems,
         send_sems,
         recv_sems,
         *gather_refs,
@@ -874,10 +954,10 @@
         ]
         for load in loads:
             load.start()
-        gather = LineGather(n, rows, chunks, normed_ref, all_ref, gather_refs)
+        gather = LineGather(n, rows, parcels, normed_ref, all_ref, gather_refs)
         neighbour_barrier(n)
-        for chunk in range(chunks):
-            gather.send_own(chunk)
+        for parcel in range(parcels):
+            gather.send_own(parcel)
         all_ref[rows_at(me * rows, rows), :] = normed_ref[...]
         for load in loads:
             load.wait()
@@ -899,21 +979,24 @@
                 ref, ref, send_sems.at[chunk], recv_sems.at[slot * count + chunk], me
             )
 
-        def stages(block_id, chunk):
+        def stages(block_id, chunk, size):
             span = rows_at(block_id * rows + chunk * size, size)
             return [
-                pltpu.make_async_copy(ref.at[chunk], hbm.at[span], stage_sems.at[chunk * 3 + k])
+                pltpu.make_async_copy(
+                    ref.at[pl.ds(chunk * size, size)], hbm.at[span], stage_sems.at[chunk * 3 + k]
+                )
                 for k, (ref, hbm) in enumerate(
                     ((act_ref, act_hbm), (gate_ref, gate_hbm), (up_ref, up_hbm))
                 )
             ]
 
-        def compute(block_id, chunk, first):
+        def compute(block_id, chunk, size, first):
+            here = pl.ds(chunk * size, size)
             span = rows_at(block_id * rows + chunk * size, size)
 
             @pl.when(jnp.logical_not(first))
             def _():
-                for stage in stages(block_id, chunk):
+                for stage in stages(block_id, chunk, size):
                     stage.wait()
 
             def units(ct, carry):
@@ -924,29 +1007,29 @@
                 act_grad = dot(branch, weight_ref[:, rows_at(2 * hidden + ct * tile, tile)])
                 sigma = 1.0 / (1.0 + jnp.exp(-gate))
                 silu = gate * sigma
-                act_ref[chunk, :, cols] = (silu * up).astype(jnp.bfloat16)
-                gate_ref[chunk, :, cols] = (
+                act_ref[here, cols] = (silu * up).astype(jnp.bfloat16)
+                gate_ref[here, cols] = (
                     act_grad * up * sigma * (1.0 + gate * (1.0 - sigma))
                 ).astype(jnp.bfloat16)
-                up_ref[chunk, :, cols] = (act_grad * silu).astype(jnp.bfloat16)
+                up_ref[here, cols] = (act_grad * silu).astype(jnp.bfloat16)
                 return carry
 
             lax.fori_loop(0, hidden // tile, units, 0)
-            for stage in stages(block_id, chunk):
+            for stage in stages(block_id, chunk, size):
                 stage.start()
 
             def columns(ct, carry):
                 cols = rows_at(ct * tile, tile)
-                total = dot_t(gate_ref[chunk], weight_ref[cols, pl.ds(0, hidden)])
-                total += dot_t(up_ref[chunk], weight_ref[cols, pl.ds(hidden, hidden)])
+                total = dot_t(gate_ref[here, :], weight_ref[cols, pl.ds(0, hidden)])
+                total += dot_t(up_ref[here, :], weight_ref[cols, pl.ds(hidden, hidden)])
 
                 @pl.when(block_id == me)
                 def _():
-                    own_part[pl.ds(chunk * size, size), cols] = total
+                    own_part[here, cols] = total
 
                 @pl.when(block_id != me)
                 def _():
-                    sent[block_id, pl.ds(chunk * size, size), cols] = total.astype(jnp.bfloat16)
+                    sent[block_id, here, cols] = total.astype(jnp.bfloat16)
 
                 return carry
 
@@ -954,43 +1037,110 @@
 
             @pl.when((me == 0) & (block_id > me))
             def _():
-                for k in range(hops):
-                    hop(block_id, chunk * hops + k, True).start()
+                for k in range(size // part_size):
+                    hop(block_id, chunk * (size // part_size) + k, True).start()
 
             @pl.when((me == n - 1) & (block_id < me))
             def _():
-                for k in range(hops):
-                    hop(block_id, chunk * hops + k, False).start()
+                for k in range(size // part_size):
+                    hop(block_id, chunk * (size // part_size) + k, False).start()
+
+        def forward(step, parcel):
+            gather.forward_chunk(step, parcel, step < n - 1)
+
+        def forward_whole(step):
+            for parcel in range(parcels):
+                forward(step, parcel)
 
         def step_of(step, carry):
             def side_of(side, carry):
                 block_id = me + (1 - 2 * side) * step
                 valid = (block_id >= 0) & (block_id < n) & ((step > 0) | (side == 0))
-                for chunk in range(chunks):
-
-                    @pl.when(middle & (step > 0) & (step < n - 1) & (side == 1))
+
+                @pl.when(middle & (step > 0) & (step < n - 1) & (side == 1))
+                def _():
+                    forward_whole(step + 1)
+
+                @pl.when(middle & valid)
+                def _():
+                    compute(block_id, 0, rows, step == 0)
+
+                @pl.when(middle & (step == 0) & (side == 0))
+                def _():
+                    forward_whole(1)
+
+                for half in range(halves):
+
+                    @pl.when(jnp.logical_not(middle) & valid)
                     def _():
-                        gather.forward_chunk(step + 1, chunk, step < n - 2)
-
-                    @pl.when(jnp.logical_not(middle) & valid & (step > 0))
-                    def _():
-                        gather.forward_chunk(step, chunk, step < n - 1)
-
-                    @pl.when(valid)
-                    def _():
-                        compute(block_id, chunk, step == 0)
-
-                    @pl.when(middle & (step == 0) & (side == 0))
-                    def _():
-                        gather.forward_chunk(1, chunk, 1 < n - 1)
+                        pl.when(step > 0)(lambda: forward(step, half))
+                        compute(block_id, half, rows // halves, step == 0)
 
                 return carry
 
             return lax.fori_loop(0, 2, side_of, carry)
 
         lax.fori_loop(0, n, step_of, 0)
-        whole_copy = pltpu.make_async_copy(all_ref, whole_hbm, load_sems.at[0])
-        whole_copy.start()
+        @pl.when(middle)
+        def _():
+            for stage in stages(me, 0, rows):
+                stage.wait()
+
+        @pl.when(jnp.logical_not(middle))
+        def _():
+            for half in range(halves):
+                for stage in stages(me, half, rows // halves):
+                    stage.wait()
+
+
+        def load_of(source, index, slot):
+            return pltpu.make_async_copy(
+                source.at[:, rows_at(lax.rem(index, per) * narrow, narrow)],
+                piece_ref.at[slot],
+                piece_sems.at[slot],
+            )
+
+        def load_piece(index):
+            for k, source in enumerate((gate_hbm, up_hbm, act_hbm)):
+
+                @pl.when(index // per == k)
+                def _():
+                    load_of(source, index, lax.rem(index, 2)).start()
+
+        def grad_copy(index):
+            cols = rows_at(index * narrow, narrow)
+            return pltpu.make_async_copy(
+                weight_ref.at[:, cols], grads_hbm.at[:, cols], grad_sems.at[index]
+            )
+
+        def grad_piece(index, carry):
+            slot = lax.rem(index, 2)
+            load_of(gate_hbm, index, slot).wait()
+
+            @pl.when(index + 1 < pieces)
+            def _():
+                load_piece(index + 1)
+
+            cols = rows_at(index * narrow, narrow)
+            for start in range(0, width, tall):
+                span = pl.ds(start, tall)
+
+                @pl.when(index < 2 * per)
+                def _():
+                    weight_ref[span, cols] = t_dot(all_ref[:, span], piece_ref[slot]).astype(
+                        jnp.bfloat16
+                    )
+
+                @pl.when(index >= 2 * per)
+                def _():
+                    weight_ref[span, cols] = t_dot(branch_ref[:, span], piece_ref[slot]).astype(
+                        jnp.bfloat16
+                    )
+
+            grad_copy(index).start()
+            return carry
+
+        load_piece(0)
 
         def add_rows(block_id, chunk):
             def body(i, carry):
@@ -1002,22 +1152,53 @@
 
             lax.fori_loop(0, part_size // block, body, 0)
 
+        def relay_side(step, chunk, rightward):
+            block_id = step if rightward else n - 1 - step
+            has = (me > 0) & (step > me) if rightward else (me < n - 1) & (n - 1 - step < me)
+
+            @pl.when(has)
+            def _():
+                arrival(block_id, chunk).wait_recv()
+                add_rows(block_id, chunk)
+                hop(block_id, chunk, rightward).start()
+
+        def relay_chunk(step, chunk, near):
+            rightward_first = 2 * me < n
+
+            @pl.when(rightward_first)
+            def _():
+                relay_side(step, chunk, near)
+
+            @pl.when(jnp.logical_not(rightward_first))
+            def _():
+                relay_side(step, chunk, not near)
+
         def relay_of(step, carry):
             for chunk in range(count):
-                for rightward, block_id, has in (
-                    (True, step, (me > 0) & (step > me)),
-                    (False, n - 1 - step, (me < n - 1) & (n - 1 - step < me)),
-                ):
-
-                    @pl.when(has)
-                    def _():
-                        arrival(block_id, chunk).wait_recv()
-                        add_rows(block_id, chunk)
-                        hop(block_id, chunk, rightward).start()
-
+                relay_chunk(step, chunk, True)
+            for chunk in range(count):
+                relay_chunk(step, chunk, False)
             return carry
 
-        lax.fori_loop(1, n, relay_of, 0)
+        lax.fori_loop(1, n - 1, relay_of, 0)
+        lax.fori_loop(0, before, grad_piece, 0)
+
+        def last_relay(chunk, carry):
+            @pl.when(chunk < count)
+            def _():
+                relay_chunk(n - 1, chunk, True)
+
+            start = before + chunk * between
+            lax.fori_loop(start, start + between, grad_piece, 0)
+
+            @pl.when(chunk > 0)
+            def _():
+                relay_chunk(n - 1, chunk - 1, False)
+
+            return carry
+
+        lax.fori_loop(0, count + 1, last_relay, 0)
+        lax.fori_loop(before + (count + 1) * between, pieces, grad_piece, 0)
         gain_sum[...] = jnp.zeros_like(gain_sum)
         for chunk in range(count):
 
@@ -1042,7 +1223,10 @@
                 unit = value * inverse
                 scaled = total * gain_ref[...]
                 inner = jnp.mean(scaled * unit, axis=1, keepdims=True)
-                result = base_ref[span, :] + inverse * (scaled - unit * inner)
+                base = branch_ref[
+                    rows_at(me * rows + chunk * part_size + i * block, block), :
+                ].astype(jnp.float32)
+                result = base + inverse * (scaled - unit * inner)
                 result_ref[span, :] = result
                 rounded_ref[span, :] = result.astype(jnp.bfloat16)
                 gain_sum[...] += jnp.sum((total * unit).reshape(block // 8, 8, width), axis=0)
@@ -1050,9 +1234,6 @@
 
             lax.fori_loop(0, part_size // block, body, 0)
         gather.finish(False)
-        for chunk in range(chunks):
-            for stage in stages(me, chunk):
-                stage.wait()
 
         def sends(block_id, carry):
             for chunk in range(count):
@@ -1068,7 +1249,12 @@
             return carry
 
         lax.fori_loop(0, n, sends, 0)
-        whole_copy.wait()
+
+        def grads_out(index, carry):
+            grad_copy(index).wait()
+            return carry
+
+        lax.fori_loop(0, pieces, grads_out, 0)
 
     half = jnp.bfloat16
     return pl.pallas_call(
@@ -1077,10 +1263,10 @@
             jax.ShapeDtypeStruct((rows, width), jnp.float32),
             jax.ShapeDtypeStruct((rows, width), half),
             jax.ShapeDtypeStruct((8, width), jnp.float32),
-            jax.ShapeDtypeStruct((total_rows, width), half),
+            jax.ShapeDtypeStruct((width, 3 * hidden), half),
         ]
         + [jax.ShapeDtypeStruct((total_rows, hidden), half)] * 3,
-        in_specs=[VMEM, ANY, ANY, VMEM, VMEM, VMEM],
+        in_specs=[VMEM, ANY, ANY, VMEM, VMEM],
         out_specs=[VMEM] * 3 + [ANY] * 4,
         scratch_shapes=[
             pltpu.VMEM((width, 3 * hidden), half),
@@ -1090,22 +1276,25 @@
             pltpu.VMEM((n, rows, width), half),
             pltpu.VMEM((rows, width), jnp.float32),
         ]
-        + [pltpu.VMEM((chunks, size, hidden), half)] * 3
+        + [pltpu.VMEM((rows, hidden), half)] * 3
         + [
+            pltpu.VMEM((2, total_rows, narrow), half),
             pltpu.SemaphoreType.DMA((2,)),
-            pltpu.SemaphoreType.DMA((chunks * 3,)),
+            pltpu.SemaphoreType.DMA((halves * 3,)),
+            pltpu.SemaphoreType.DMA((2,)),
+            pltpu.SemaphoreType.DMA((pieces,)),
             pltpu.SemaphoreType.DMA((n * count,)),
             pltpu.SemaphoreType.DMA(((n + 1) * count,)),
         ]
-        + gather_sems(n, chunks),
+        + gather_sems(n, parcels),
         compiler_params=pltpu.CompilerParams(
             collective_id=collective_id, has_side_effects=True, vmem_limit_bytes=VMEM_LIMIT
         ),
         cost_estimate=pl.CostEstimate(
-            flops=10 * total_rows * width * hidden, bytes_accessed=300_000_000, transcendentals=0
+            flops=16 * total_rows * width * hidden, bytes_accessed=300_000_000, transcendentals=0
         ),
         name="feed_forward",
-    )(normed, branch_grad, weights, *own_rows, gains_row)
+    )(normed, branch_grad, weights, second, gains_row)
 
 
 def attention_backward(queries, keys, values, mixed_grad, cosine, sine, key_mask):
@@ -1196,7 +1385,7 @@
 
 def update_flipped(arrays, total, start, rate, name):
     high, wide = arrays[0].shape
-    step = min(256, high)
+    step = min(512, high)
 
     def body(w, m, a, g, *outs):
         store_update((w, m, a), g[...].astype(jnp.float32).T, outs, rate)
@@ -1219,7 +1408,7 @@
     def body(w, m, a, g, *outs):
         store_update((w, m, a), g[...].astype(jnp.float32), outs, rate)
 
-    turns = 2
+    turns = 1
     outs = update_call(
         body,
         (parts, turns),
@@ -1236,7 +1425,7 @@
 def update_pairs(arrays, total, rate, name):
     high, parts, wide = arrays[0].shape
     tiles = wide // 128
-    step = min(16, high)
+    step = min(64, high)
     stride = tiles * parts
 
     def body(w, m, a, g, *rest):
@@ -1263,49 +1452,6 @@
         x.reshape(high, tiles, parts, 128).transpose(0, 2, 1, 3).reshape(high, parts, wide)
         for x in outs
     ]
-
-
-def weight_gradients(lefts, rights, tile=512):
-    count = len(lefts)
-    rows, depth = lefts[0].shape
-    wide = rights[0].shape[1]
-    steps = wide // tile
-    distinct = []
-    for left in lefts:
-        if all(left is not other for other in distinct):
-            distinct.append(left)
-    which = [next(k for k, d in enumerate(distinct) if d is left) for left in lefts]
-
-    def kernel(*refs):
-        left_refs, right_refs = refs[: len(distinct)], refs[len(distinct) : -1]
-        out_ref = refs[-1]
-        pair = pl.program_id(0)
-        for k in range(count):
-
-            @pl.when(pair == k)
-            def _():
-                out_ref[...] = t_dot(left_refs[which[k]][...], right_refs[k][...]).astype(
-                    jnp.bfloat16
-                )
-
-    def right_map(k):
-        return lambda pair, i: (0, jnp.where(pair == k, i, jnp.where(pair < k, 0, steps - 1)))
-
-    return pl.pallas_call(
-        kernel,
-        grid=(count, steps),
-        out_shape=jax.ShapeDtypeStruct((depth, count * wide), jnp.bfloat16),
-        in_specs=[VMEM] * len(distinct)
-        + [pl.BlockSpec((rows, tile), right_map(k)) for k in range(count)],
-        out_specs=pl.BlockSpec((depth, tile), lambda pair, i: (0, pair * steps + i)),
-        compiler_params=pltpu.CompilerParams(vmem_limit_bytes=VMEM_LIMIT),
-        cost_estimate=pl.CostEstimate(
-            flops=2 * rows * depth * count * wide,
-            bytes_accessed=2 * (len(distinct) * rows * depth + count * wide * (rows + depth)),
-            transcendentals=0,
-        ),
-        name="weight_gradients",
-    )(*distinct, *rights)
 
 
 def rope_tables(length, half_dim):
@@ -1358,8 +1504,6 @@
         n_dp, n_mp, tokens_in, gains, cotangent, live_rows, 1
     )
     ffn_w = lax.all_gather(ffn_part, "dp", axis=0, tiled=True)
-    out_wt = attn_w[:, 3 * local_width :]
-    xin = tokens.astype(jnp.float32)
     cosine, sine = (jnp.asarray(x, jnp.float32) for x in rope_tables(SEQ, HDIM // 2))
 
     second, normed_second, queries, keys, values, mixed, branch_grad = scatter_rows(
@@ -1367,7 +1511,7 @@
         [h_first],
         attn_w,
         3 * local_width,
-        [xin],
+        [tokens],
         "forward",
         gain_all[1:2],
         2,
@@ -1375,15 +1519,11 @@
         extra=own_branch,
     )
 
-    second_grad, own_grad, gain_two, h_second, act, gate_grad, up_grad = feed_forward(
-        n_mp, normed_second, branch_grad, ffn_w, [second, out_grad], gain_all[1:2], 3
-    )
-    grad_ffn = weight_gradients(
-        [h_second, h_second, branch_grad], [gate_grad, up_grad, act]
-    )
-    grad_ffn, own_grad = lax.optimization_barrier((grad_ffn, own_grad))
+    second_grad, own_grad, gain_two, grad_ffn, act, _, _ = feed_forward(
+        n_mp, normed_second, branch_grad, ffn_w, second, gain_all[1:2], 3
+    )
     sum_ffn = lax.psum_scatter(grad_ffn, "dp", scatter_dimension=0, tiled=True)
-    block_out, attn_grad = scatter_rows(
+    block_out, attn_grad, mixed_grad = scatter_rows(
         n_mp,
         [act],
         ffn_w,
@@ -1393,9 +1533,9 @@
         gain_all[1:2],
         7,
         extra=own_grad,
-    )
-
-    mixed_grad = dot(attn_grad, out_wt).astype(half)
+        extra_right=(attn_w, 3 * local_width),
+    )
+
     joined_grad = attention_backward(
         queries, keys, values, mixed_grad, cosine, sine, key_mask[:, None]
     )
@@ -1404,7 +1544,7 @@
         list(joined_grad),
         attn_w,
         0,
-        [xin, second_grad],
+        [tokens, second_grad],
         "last",
         gain_all[0:1],
         4,

time: 649 us -> 586 us (0.903)
  Pallas kernels: 605 us -> 551 us
  matrix products: 6.54 us -> 0 us
    pallas_call x1 -> x0, Pallas kernels: 35.6 us -> none  [weight_gradients(): pl.pallas_call(kernel, grid=(count, steps), out_shape=jax.ShapeDtypeStruc...]
    pallas_call x1, Pallas kernels: 143 us -> 126 us  [feed_forward(): pl.pallas_call(kernel, out_shape=[jax.ShapeDtypeStruct((rows, width), jnp...]
    dot_general x1 -> x0, matrix products: 6.54 us -> none  [dot(): return jnp.dot(left, right, preferred_element_type=jnp.float32)]
  transfers between devices with their start and end apart: 3 -> 3, of which waited for: 0 -> 0; matrix products, arithmetic and copies ran while one was open for 2% -> 1% of each run, Pallas kernels for 63% -> 70%
where the time goes in v4:
time: 586 us; the launch traced here: 578 us
  Pallas kernels  551 us (94%)
  between operations  14.8 us (3%)
  local copies, waits for them, and re-layouts  8.24 us (1%)
    pallas_call x3, Pallas kernels, scatter_rows(): pl.pallas_call(kernel, out_shape=out_shape, in_specs=[VMEM] * count + [AN...  297 us
    pallas_call x1, Pallas kernels, feed_forward(): pl.pallas_call(kernel, out_shape=[jax.ShapeDtypeStruct((rows, width), jnp...  126 us
    pallas_call x1, Pallas kernels, gather_first(): pl.pallas_call(kernel, out_shape=[jax.ShapeDtypeStruct((n_mp * rows, widt...  80 us
    pallas_call x4, Pallas kernels, update_call(): pl.pallas_call(body, grid=grid, out_shape=[jax.ShapeDtypeStruct(shape, ki...  29 us
    pallas_call x1, Pallas kernels, attention_backward(): pl.pallas_call(kernel, grid=(inner_width // HDIM,), out_shape=[jax.ShapeD...  12.5 us
  transfers between devices with their start and end apart: 3, of which 0 were waited for; matrix products, arithmetic and copies ran while one was open for 1% of the time, Pallas kernels for 70%

profile of v4, /device:TPU:0, one launch (start us, length us, event | category | flops | bytes accessed | tf_op | source)
XLA Modules:
  0.0 578.4 jit_solution(8756800864425351996)
XLA Ops:
  7.2 1.7 copy.62
  9.0 0.3 copy.64
  9.4 1.1 pad_maximum_fusion
  10.6 6.6 %round_shares.1 = bf16[256,6144]{1,0:T(8,128)(2,1)} custom-call(f32[8192,128]{1,0:T(8,128)} %bitcast.52, f32[2048,256]{1,0:T(8,128)} %w.3), custom_call_target="tpu_custom_call" | custom-call | bytes 9437184 | tf_op jit(solution)/shard_map/round_shares/pallas_call | solution.py:213
  17.3 0.6 copy-done.4
  18.7 0.6 concatenate.7.tile_ref
  19.3 0.7 fusion.1.live_ref
  19.9 80.0 %gather_first.1 = (bf16[1024,2048]{1,0:T(8,128)(2,1)}, f32[8,2048]{1,0:T(8,128)}, f32[256,2048]{1,0:T(8,128)}, bf16[256,2048]{1,0:T(8,128)(2,1)}) custom-call(bf16[256,2048]{1,0:T(8,128)(2,1)} %refs_5_.2, f32[8,128]{1,0:T(8,128)} %concatenate.7.tile_ref, bf16[256,2048]{1,0:T(8,128)(2,1)} %cotangent_ref.1, f32[256,1]{1,0:T(8,128)} %fusion.1.live_ref), custom_call_target="tpu_custom_call" | custom-call | bytes 209715200 | tf_op jit(solution)/shard_map/gather_first/pallas_call | solution.py:318
  100.0 0.6 compare_convert_fusion.refs_6_
  100.6 1.5 fusion.3
  102.1 101.5 %scatter_forward.1 = (f32[256,2048]{1,0:T(8,128)}, bf16[256,2048]{1,0:T(8,128)(2,1)}, bf16[1024,512]{1,0:T(8,128)(2,1)}, bf16[1024,512]{1,0:T(8,128)(2,1)}, bf16...) custom-call(bf16[1024,2048]{1,0:T(8,128)(2,1)} %get-tuple-element.64.refs_0_.refs_8_, ...), custom_call_target="tpu_custom_call" | custom-call | flops 2147483648 | bytes 300000000 | tf_op jit(solution)/shard_map/scatter_forward/pallas_call | solution.py:880
  203.6 125.9 %feed_forward.1 = (f32[256,2048]{1,0:T(8,128)}, bf16[256,2048]{1,0:T(8,128)(2,1)}, f32[8,2048]{1,0:T(8,128)}, bf16[2048,6144]{1,0:T(8,128)(2,1)}, bf16[1024,2048...) custom-call(bf16[256,2048]{1,0:T(8,128)(2,1)} %get-tuple-element.67.normed_ref, ...), custom_call_target="tpu_custom_call" | custom-call | flops 68719476736 | bytes 300000000 | tf_op jit(solution)/shard_map/feed_forward/pallas_call | solution.py:1260
  329.6 0.8 fusion.mask_ref
  330.4 99.1 %scatter_residual.1 = (bf16[256,2048]{1,0:T(8,128)(2,1)}, bf16[1024,2048]{1,0:T(8,128)(2,1)}, bf16[1024,512]{1,0:T(8,128)(2,1)}) custom-call(bf16[1024,2048]{1,0:T(8,128)(2,1)} %get-tuple-element.71.refs_0_, bf16[2048,6144]{1,0:T(8,128)(2,1)} %all-gather.5.cloned.1.call-done.weights_hbm.refs_1_, f32[1,2048]{1,0:T(1,128)} %get-tuple-element.109.refs_2_.gain_ref, ...), custom_call_target="tpu_custom_call" | custom-call | flops 8589934592 | bytes 300000000 | tf_op jit(solution)/shard_map/scatter_residual/pallas_call | solution.py:880
  429.6 12.5 %attention_backward.1 = (bf16[1024,512]{1,0:T(8,128)(2,1)}, bf16[1024,512]{1,0:T(8,128)(2,1)}, bf16[1024,512]{1,0:T(8,128)(2,1)}) custom-call(bf16[1024,512]{1,0:T(8,128)(2,1)} %get-tuple-element.74.q_ref, bf16[1024,512]{1,0:T(8,128)(2,1)} %get-tuple-element.75.k_ref, bf16[1024,512]{1,0:T(8,128)(2,1)} %get-tuple-element.76.v_ref, ...), custom_call_target="tpu_custom_call" | custom-call | flops 4294967296 | bytes 7340032 | tf_op jit(solution)/shard_map/attention_backward/pallas_call | solution.py:1334
  442.1 96.6 %scatter_last.1 = (f32[256,2048]{1,0:T(8,128)}, f32[16,128]{1,0:T(8,128)}, f32[256,2048]{1,0:T(8,128)}) custom-call(bf16[1024,512]{1,0:T(8,128)(2,1)} %get-tuple-element.78.refs_0_, bf16[1024,512]{1,0:T(8,128)(2,1)} %get-tuple-element.79.refs_1_, bf16[1024,512]{1,0:T(8,128)(2,1)} %get-tuple-element.80.refs_2_, ...), custom_call_target="tpu_custom_call" | custom-call | flops 6442450944 | bytes 300000000 | tf_op jit(solution)/shard_map/scatter_last/pallas_call | solution.py:880
  538.7 3.0 update_out.1
  541.7 6.3 %update_qkv.1 = (f32[3,256,512]{2,1,0:T(8,128)}, f32[3,256,512]{2,1,0:T(8,128)}, f32[3,256,512]{2,1,0:T(8,128)}, bf16[3,256,512]{2,1,0:T(8,128)(2,1)}) custom-call(f32[3,256,512]{2,1,0:T(8,128)} %bitcast.54, f32[3,256,512]{2,1,0:T(8,128)} %bitcast.58, f32[3,256,512]{2,1,0:T(8,128)} %bitcast.59, f32[256,2048]{1,0:T(8,128)} %get-tuple-element.86.g), custom_call_target="tpu_custom_call" | custom-call | flops 3932160 | bytes 11010048 | tf_op jit(solution)/shard_map/update_qkv/pallas_call | solution.py:1371
  548.1 0.7 multiply_add_fusion
  548.7 12.9 %update_gu.1 = (f32[8192,128]{1,0:T(8,128)}, f32[8192,128]{1,0:T(8,128)}, f32[8192,128]{1,0:T(8,128)}, bf16[8192,128]{1,0:T(8,128)(2,1)}) custom-call(f32[8192,128]{1,0:T(8,128)} %bitcast.53, f32[8192,128]{1,0:T(8,128)} %bitcast.55, f32[8192,128]{1,0:T(8,128)} %bitcast.56, bf16[256,6144]{1,0:T(8,128)(2,1)} %reduce-scatter.2.cloned.1.call-done.g), custom_call_target="tpu_custom_call" | custom-call | flops 10485760 | bytes 29360128 | tf_op jit(solution)/shard_map/update_gu/pallas_call | solution.py:1371
  561.6 6.7 %update_down.1 = (f32[2048,256]{1,0:T(8,128)}, f32[2048,256]{1,0:T(8,128)}, f32[2048,256]{1,0:T(8,128)}, bf16[2048,256]{1,0:T(8,128)(2,1)}) custom-call(f32[2048,256]{1,0:T(8,128)} %w.3, f32[2048,256]{1,0:T(8,128)} %m.3, f32[2048,256]{1,0:T(8,128)} %a.3, bf16[256,6144]{1,0:T(8,128)(2,1)} %reduce-scatter.2.cloned.1.call-done.g), custom_call_target="tpu_custom_call" | custom-call | flops 5242880 | bytes 14680064 | tf_op jit(solution)/shard_map/update_down/pallas_call | solution.py:1371
  568.4 1.0 copy.74
  569.4 1.0 copy-done.1
  570.4 1.3 copy.75
  (27 shorter events, 0.5 us)
Async XLA Ops:
  7.2 2.1 copy-start
  7.2 94.9 %all-gather.3.cloned.1.call-start = ((), (), s32[]{:S(2)}) async-start(), calls=%async_computation.1 | async-start | bytes 9437184 | tf_op jit(solution)/shard_map/all_gather | solution.py:1498
  10.5 193.0 %all-gather.5.cloned.1.call-start = ((), (), s32[]{:S(2)}) async-start(), calls=%async_computation.2 | async-start | bytes 28311552 | tf_op jit(solution)/shard_map/all_gather | solution.py:1506
  17.2 0.7 copy-start.4
  17.3 531.5 %reduce-scatter.2.cloned.1.call-start = ((), (), s32[]{:S(2)}) async-start(), calls=%async_computation.3 | async-start | bytes 28311552 | tf_op jit(solution)/shard_map/reduce_scatter | solution.py:1525
  541.7 6.3 %copy-start.3 = (f32[16,128]{1,0:T(8,128)S(1)}, f32[16,128]{1,0:T(8,128)}, u32[]{:S(2)}) copy-start(f32[16,128]{1,0:T(8,128)} %get-tuple-element.92) | copy-start | bytes 24580
  541.7 6.3 %copy-start.5 = (f32[2,64]{1,0:T(2,128)S(1)}, f32[2,64]{1,0:T(2,128)}, u32[]{:S(2)}) copy-start(f32[2,64]{1,0:T(2,128)} %param.37) | copy-start | bytes 1540
  541.7 6.3 %copy-start.6 = (f32[2,64]{1,0:T(2,128)S(1)}, f32[2,64]{1,0:T(2,128)}, u32[]{:S(2)}) copy-start(f32[2,64]{1,0:T(2,128)} %param.32) | copy-start | bytes 1540
  561.6 6.8 %copy-start.2 = (bf16[256,2048]{1,0:T(8,128)(2,1)S(1)}, bf16[256,2048]{1,0:T(8,128)(2,1)}, u32[]{:S(2)}) copy-start(bf16[256,2048]{1,0:T(8,128)(2,1)} %get-tuple-element.131) | copy-start | bytes 3145732
  568.4 2.0 copy-start.1
Sparse Core Ops, SparseCore 0:
  10.7 58.4 all-gather.2
  71.7 125.3 all-gather.4
  329.7 194.2 reduce-scatter.1

commit v5 on v4

--- a/solution.py
+++ b/solution.py
@@ -374,7 +374,8 @@
     rhs_start,
     own_rows,
     epilogue,
-    gains_row,
+    gains,
+    gain_row,
     collective_id,
     heads=None,
     extra=None,
@@ -387,7 +388,7 @@
 ):
     total_rows = lhs[0].shape[0]
     rows = total_rows // n
-    width = gains_row.shape[1]
+    width = gains.shape[1]
     size = rows // chunks
     tile = 512
     has_norm, has_gain = epilogue in ("forward", "backward"), epilogue in ("backward", "last")
@@ -728,7 +729,7 @@
                 total = total + jnp.where(
                     me < n - 1, held[n, span, :].astype(jnp.float32), zero
                 )
-                gain = gain_ref[...]
+                gain = gain_ref[gain_row : gain_row + 1, :]
                 if epilogue == "residual":
                     outs[0][span, :] = (own[0][span, :] + total).astype(jnp.bfloat16)
                 elif epilogue == "forward":
@@ -767,11 +768,12 @@
             extra_local.wait()
         if other_gain is not None:
             local = width // (n * n_dp)
-            for source, rows_of in ((gain_sum, pl.ds(0, 8)), (other_ref, pl.ds(8, 8))):
+            for row, source in ((0, gain_sum), (1, other_ref)):
+                total = jnp.sum(source[...], axis=0, keepdims=True)
                 for d in range(n_dp):
                     for m in range(n):
-                        cols = pl.ds(tile_of(d, m, n, local) * 128, 128)
-                        table[m, d, rows_of, :] = source[:, cols]
+                        start = tile_of(d, m, n, local) * 128
+                        table[m, d, row : row + 1, :] = total[:, start : start + 128]
             copies = exchange.swap("mp", lambda peer: table.at[peer], first)
             first[me] = table[me]
             for copy in copies:
@@ -810,7 +812,7 @@
     out_specs = [VMEM]
     if has_gain:
         out_shape.append(
-            jax.ShapeDtypeStruct((8, width) if other_gain is None else (16, 128), jnp.float32)
+            jax.ShapeDtypeStruct((8, width) if other_gain is None else (2, 128), jnp.float32)
         )
         out_specs.append(VMEM)
     if other_gain is not None:
@@ -863,10 +865,10 @@
         late_args = [*grad_lefts, grad_right]
         scratch += [
             pltpu.VMEM((8, width), jnp.float32),
-            pltpu.VMEM((n, n_dp, 16, 128), jnp.float32),
-            pltpu.VMEM((n, n_dp, 16, 128), jnp.float32),
-            pltpu.VMEM((n_dp, 16, 128), jnp.float32),
-            pltpu.VMEM((n_dp, 16, 128), jnp.float32),
+            pltpu.VMEM((n, n_dp, 2, 128), jnp.float32),
+            pltpu.VMEM((n, n_dp, 2, 128), jnp.float32),
+            pltpu.VMEM((n_dp, 2, 128), jnp.float32),
+            pltpu.VMEM((n_dp, 2, 128), jnp.float32),
         ] + exchange_sems(n_dp, n)
         scratch += [pltpu.VMEM(x.shape, x.dtype) for x in late_args]
         scratch.append(pltpu.SemaphoreType.DMA((len(late_args),)))
@@ -897,10 +899,10 @@
             flops=flops, bytes_accessed=300_000_000, transcendentals=0
         ),
         name="scatter_" + epilogue,
-    )(*lhs, rhs, gains_row, *own_rows, *head_args, *late_args, *extra_args)
-
-
-def feed_forward(n, normed, branch_grad, weights, second, gains_row, collective_id, halves=1, hops=4):
+    )(*lhs, rhs, gains, *own_rows, *head_args, *late_args, *extra_args)
+
+
+def feed_forward(n, normed, branch_grad, weights, second, gains, collective_id, halves=1, hops=4):
     rows, width = normed.shape
     total_rows = n * rows
     hidden = weights.shape[1] // 3
@@ -1221,7 +1223,7 @@
                 value = second_ref[span, :]
                 inverse = lax.rsqrt(jnp.mean(value * value, axis=1, keepdims=True) + norm_eps)
                 unit = value * inverse
-                scaled = total * gain_ref[...]
+                scaled = total * gain_ref[1:2, :]
                 inner = jnp.mean(scaled * unit, axis=1, keepdims=True)
                 base = branch_ref[
                     rows_at(me * rows + chunk * part_size + i * block, block), :
@@ -1294,14 +1296,14 @@
             flops=16 * total_rows * width * hidden, bytes_accessed=300_000_000, transcendentals=0
         ),
         name="feed_forward",
-    )(normed, branch_grad, weights, second, gains_row)
-
-
-def attention_backward(queries, keys, values, mixed_grad, cosine, sine, key_mask):
+    )(normed, branch_grad, weights, second, gains)
+
+
+def attention_backward(queries, keys, values, mixed_grad, cosine, sine, valid_counts):
     total_rows, inner_width = queries.shape
     block = min(256, total_rows)
 
-    def kernel(q_ref, k_ref, v_ref, do_ref, cos_ref, sin_ref, mask_ref, dq_out, dk_out, dv_out, dk_ref, dv_ref):
+    def kernel(q_ref, k_ref, v_ref, do_ref, cos_ref, sin_ref, valid_ref, dq_out, dk_out, dv_out, dk_ref, dv_ref):
         dk_ref[...] = jnp.zeros_like(dk_ref)
         dv_ref[...] = jnp.zeros_like(dv_ref)
         for i in range(total_rows // block):
@@ -1310,7 +1312,7 @@
             shape = (upto, block)
             key_pos = lax.broadcasted_iota(jnp.int32, shape, 0)
             query_pos = i * block + lax.broadcasted_iota(jnp.int32, shape, 1)
-            allowed = jnp.where(key_pos <= query_pos, mask_ref[:upto, :], 0.0)
+            allowed = jnp.where((key_pos <= query_pos) & (key_pos < valid_ref[0]), 1.0, 0.0)
             query, grad = q_ref[span, :], do_ref[span, :]
             key = k_ref[:upto, :]
             prob = probability(dot_t(key, query)) * allowed
@@ -1335,7 +1337,7 @@
         kernel,
         grid=(inner_width // HDIM,),
         out_shape=[jax.ShapeDtypeStruct((total_rows, inner_width), jnp.bfloat16)] * 3,
-        in_specs=[head] * 4 + [table] * 2 + [pl.BlockSpec((total_rows, 1), lambda h: (0, 0))],
+        in_specs=[head] * 4 + [table] * 2 + [pl.BlockSpec(memory_space=pltpu.SMEM)],
         out_specs=[head] * 3,
         scratch_shapes=[pltpu.VMEM((total_rows, HDIM), jnp.float32)] * 2,
         compiler_params=pltpu.CompilerParams(vmem_limit_bytes=VMEM_LIMIT),
@@ -1345,7 +1347,7 @@
             transcendentals=0,
         ),
         name="attention_backward",
-    )(queries, keys, values, mixed_grad, cosine, sine, key_mask)
+    )(queries, keys, values, mixed_grad, cosine, sine, valid_counts)
 
 
 def updated(weight, moment, average, gradient, rate):
@@ -1365,93 +1367,121 @@
     outs[3][...] = weight.astype(jnp.bfloat16)
 
 
-def update_call(body, grid, arrays, spec, total, total_spec, scratch, name):
+def update_all(pairs, parts, flips, sum_ffn, sum_attn, passed, rate):
+    jobs = []
+
+    high, two, wide = pairs[0].shape
+    tiles = wide // 128
+    step = min(64, high)
+    stride = tiles * two
+
+    def spread_gradient(g, spread):
+        for part in range(two):
+            for tile in range(tiles):
+                cols = pl.ds(part * wide + tile * 128, 128)
+                spread[pl.ds(tile * two + part, step, stride=stride), :] = g[:, cols].astype(
+                    jnp.float32
+                )
+        return spread[...]
+
+    jobs.append(
+        (
+            [flat_pairs(x) for x in pairs],
+            ((step * stride, 128), lambda i: (i, 0)),
+            (sum_ffn, (step, two * wide), lambda i: (i, 0)),
+            high // step,
+            spread_gradient,
+        )
+    )
+    for arrays, total, start in ((flips[0][0], sum_ffn, flips[0][1]), (flips[1][0], sum_attn, flips[1][1])):
+        tall, narrow = arrays[0].shape
+        rows = min(512, tall)
+        jobs.append(
+            (
+                arrays,
+                ((rows, narrow), lambda i: (i, 0)),
+                (total, (narrow, rows), lambda i, first=start // rows: (0, first + i)),
+                tall // rows,
+                lambda g, spread: g[...].astype(jnp.float32).T,
+            )
+        )
+    deep, count, across = parts[0].shape
+    jobs.append(
+        (
+            [x.transpose(1, 0, 2) for x in parts],
+            ((None, deep, across), lambda i: (i, 0, 0)),
+            (sum_attn, (deep, across), lambda i: (0, i)),
+            count,
+            lambda g, spread: g[...].astype(jnp.float32),
+        )
+    )
+    starts = [sum(job[3] for job in jobs[:k]) for k in range(len(jobs))]
+    steps = sum(job[3] for job in jobs)
+
+    def within(k, index_map):
+        return lambda i: index_map(jnp.clip(i - starts[k], 0, jobs[k][3] - 1))
+
+    in_specs, out_specs, args, out_shape = [], [], [], []
     kinds = [jnp.float32] * 3 + [jnp.bfloat16]
-    shape = arrays[0].shape
-    return pl.pallas_call(
+    for k, (arrays, (shape, index_map), (total, total_shape, total_map), _, _) in enumerate(jobs):
+        spec = pl.BlockSpec(shape, within(k, index_map))
+        in_specs += [spec] * 3 + [pl.BlockSpec(total_shape, within(k, total_map))]
+        args += [*arrays, total]
+        out_specs += [spec] * 4
+        out_shape += [jax.ShapeDtypeStruct(arrays[0].shape, kind) for kind in kinds]
+    in_specs += [ANY] * len(passed)
+    out_specs += [ANY] * len(passed)
+    out_shape += [jax.ShapeDtypeStruct(x.shape, x.dtype) for x in passed]
+
+    def body(*refs):
+        ins, refs = refs[: len(in_specs)], refs[len(in_specs) :]
+        outs, (spread, sems) = refs[: len(out_specs)], refs[len(out_specs) :]
+        i = pl.program_id(0)
+        copies = [
+            pltpu.make_async_copy(ins[4 * len(jobs) + k], outs[4 * len(jobs) + k], sems.at[k])
+            for k in range(len(passed))
+        ]
+
+        @pl.when(i == 0)
+        def _():
+            for copy in copies:
+                copy.start()
+
+        for k, job in enumerate(jobs):
+
+            @pl.when((i >= starts[k]) & (i < starts[k] + job[3]))
+            def _():
+                gradient = job[4](ins[4 * k + 3], spread)
+                store_update(ins[4 * k : 4 * k + 3], gradient, outs[4 * k : 4 * k + 4], rate)
+
+        @pl.when(i == steps - 1)
+        def _():
+            for copy in copies:
+                copy.wait()
+
+    size = sum(job[0][0].size for job in jobs)
+    outs = pl.pallas_call(
         body,
-        grid=grid,
-        out_shape=[jax.ShapeDtypeStruct(shape, kind) for kind in kinds],
-        in_specs=[spec] * 3 + [total_spec],
-        out_specs=[spec] * 4,
-        scratch_shapes=scratch,
+        grid=(steps,),
+        out_shape=out_shape,
+        in_specs=in_specs,
+        out_specs=out_specs,
+        scratch_shapes=[
+            pltpu.VMEM((step * stride, 128), jnp.float32),
+            pltpu.SemaphoreType.DMA((len(passed),)),
+        ],
         compiler_params=pltpu.CompilerParams(vmem_limit_bytes=VMEM_LIMIT),
         cost_estimate=pl.CostEstimate(
-            flops=10 * arrays[0].size, bytes_accessed=28 * arrays[0].size, transcendentals=0
+            flops=10 * size, bytes_accessed=28 * size, transcendentals=0
         ),
-        name=name,
-    )(*arrays, total)
-
-
-def update_flipped(arrays, total, start, rate, name):
-    high, wide = arrays[0].shape
-    step = min(512, high)
-
-    def body(w, m, a, g, *outs):
-        store_update((w, m, a), g[...].astype(jnp.float32).T, outs, rate)
-
-    return update_call(
-        body,
-        (high // step,),
-        arrays,
-        pl.BlockSpec((step, wide), lambda i: (i, 0)),
-        total,
-        pl.BlockSpec((wide, step), lambda i: (0, start // step + i)),
-        [],
-        name,
-    )
-
-
-def update_parts(arrays, total, rate, name):
-    high, parts, wide = arrays[0].shape
-
-    def body(w, m, a, g, *outs):
-        store_update((w, m, a), g[...].astype(jnp.float32), outs, rate)
-
-    turns = 1
-    outs = update_call(
-        body,
-        (parts, turns),
-        [x.transpose(1, 0, 2) for x in arrays],
-        pl.BlockSpec((None, high // turns, wide), lambda i, j: (i, j, 0)),
-        total,
-        pl.BlockSpec((high // turns, wide), lambda i, j: (j, i)),
-        [],
-        name,
-    )
-    return [x.transpose(1, 0, 2) for x in outs]
-
-
-def update_pairs(arrays, total, rate, name):
-    high, parts, wide = arrays[0].shape
-    tiles = wide // 128
-    step = min(64, high)
-    stride = tiles * parts
-
-    def body(w, m, a, g, *rest):
-        outs, spread = rest[:4], rest[4]
-        for part in range(parts):
-            for tile in range(tiles):
-                cols = pl.ds(part * wide + tile * 128, 128)
-                spread[pl.ds(tile * parts + part, step, stride=stride), :] = g[:, cols].astype(
-                    jnp.float32
-                )
-        store_update((w, m, a), spread[...], outs, rate)
-
-    outs = update_call(
-        body,
-        (high // step,),
-        [flat_pairs(x) for x in arrays],
-        pl.BlockSpec((step * stride, 128), lambda i: (i, 0)),
-        total,
-        pl.BlockSpec((step, parts * wide), lambda i: (i, 0)),
-        [pltpu.VMEM((step * stride, 128), jnp.float32)],
-        name,
-    )
-    return [
-        x.reshape(high, tiles, parts, 128).transpose(0, 2, 1, 3).reshape(high, parts, wide)
-        for x in outs
+        name="update_all",
+    )(*args, *passed)
+    gu = [
+        x.reshape(high, tiles, two, 128).transpose(0, 2, 1, 3).reshape(high, two, wide)
+        for x in outs[:4]
     ]
+    qkv = [x.transpose(1, 0, 2) for x in outs[12:16]]
+    return gu, outs[4:8], outs[8:12], qkv, outs[16:]
 
 
 def rope_tables(length, half_dim):
@@ -1513,14 +1543,15 @@
         3 * local_width,
         [tokens],
         "forward",
-        gain_all[1:2],
+        gain_all,
+        1,
         2,
         heads=(cosine, sine, key_mask[None, :]),
         extra=own_branch,
     )
 
     second_grad, own_grad, gain_two, grad_ffn, act, _, _ = feed_forward(
-        n_mp, normed_second, branch_grad, ffn_w, second, gain_all[1:2], 3
+        n_mp, normed_second, branch_grad, ffn_w, second, gain_all, 3
     )
     sum_ffn = lax.psum_scatter(grad_ffn, "dp", scatter_dimension=0, tiled=True)
     block_out, attn_grad, mixed_grad = scatter_rows(
@@ -1530,14 +1561,15 @@
         2 * hidden,
         [second],
         "residual",
-        gain_all[1:2],
+        gain_all,
+        1,
         7,
         extra=own_grad,
         extra_right=(attn_w, 3 * local_width),
     )
 
     joined_grad = attention_backward(
-        queries, keys, values, mixed_grad, cosine, sine, key_mask[:, None]
+        queries, keys, values, mixed_grad, cosine, sine, valid_counts
     )
     input_grad, gain_tile, sum_attn = scatter_rows(
         n_mp,
@@ -1546,7 +1578,8 @@
         0,
         [tokens, second_grad],
         "last",
-        gain_all[0:1],
+        gain_all,
+        0,
         4,
         other_gain=gain_two,
         grad_lefts=[h_first, attn_grad],
@@ -1559,19 +1592,23 @@
     scale_rate = gain_rate / math.sqrt(total_rows)
     local = gains.shape[1]
     place = lax.rem((lax.axis_index("dp") * n_mp + lax.axis_index("mp")) * local, 128)
-    sum_gains = lax.dynamic_slice(gain_tile.reshape(2, 8, 128).sum(axis=1), (0, place), (2, local))
-    new_gu, next_mom_gu, next_avg_gu, copy_gu = update_pairs(
-        [w_gu, mom_gu, avg_gu], sum_ffn, matrix_rate, "update_gu"
-    )
-    new_down, next_mom_down, next_avg_down, copy_down = update_flipped(
-        [w_down, mom_down, avg_down], sum_ffn, 2 * hidden, matrix_rate, "update_down"
-    )
-    new_qkv, next_mom_qkv, next_avg_qkv, copy_qkv = update_parts(
-        [w_qkv, mom_qkv, avg_qkv], sum_attn, matrix_rate, "update_qkv"
-    )
-    new_out, next_mom_out, next_avg_out, copy_out = update_flipped(
-        [w_out, mom_out, avg_out], sum_attn, 3 * local_width, matrix_rate, "update_out"
-    )
+    sum_gains = lax.dynamic_slice(gain_tile, (0, place), (2, local))
+    gu, down, out, qkv, (block_out, input_grad) = update_all(
+        [w_gu, mom_gu, avg_gu],
+        [w_qkv, mom_qkv, avg_qkv],
+        (
+            ([w_down, mom_down, avg_down], 2 * hidden),
+            ([w_out, mom_out, avg_out], 3 * local_width),
+        ),
+        sum_ffn,
+        sum_attn,
+        [block_out, input_grad],
+        matrix_rate,
+    )
+    new_gu, next_mom_gu, next_avg_gu, copy_gu = gu
+    new_down, next_mom_down, next_avg_down, copy_down = down
+    new_out, next_mom_out, next_avg_out, copy_out = out
+    new_qkv, next_mom_qkv, next_avg_qkv, copy_qkv = qkv
     new_gains, next_mom_gains, next_avg_gains = updated(
         gains, mom_gains, avg_gains, sum_gains, scale_rate
     )

time: 586 us -> 653 us (1.11)
  Pallas kernels: 551 us -> 624 us
    pallas_call x4 -> x1, Pallas kernels: 29 us -> 104 us  [update_all(): pl.pallas_call(body, grid=(steps,), out_shape=out_shape, in_specs=in_spec...]
  transfers between devices with their start and end apart: 3 -> 3, of which waited for: 0 -> 0; matrix products, arithmetic and copies ran while one was open for 1% -> 1% of each run, Pallas kernels for 70% -> 61%
where the time goes in v5:
time: 653 us; the launch traced here: 646 us
  Pallas kernels  624 us (96%)
  between operations  14.8 us (2%)
    pallas_call x3, Pallas kernels, scatter_rows(): pl.pallas_call(kernel, out_shape=out_shape, in_specs=[VMEM] * count + [AN...  294 us
    pallas_call x1, Pallas kernels, feed_forward(): pl.pallas_call(kernel, out_shape=[jax.ShapeDtypeStruct((rows, width), jnp...  126 us
    pallas_call x1, Pallas kernels, update_all(): pl.pallas_call(body, grid=(steps,), out_shape=out_shape, in_specs=in_spec...  104 us
    pallas_call x1, Pallas kernels, gather_first(): pl.pallas_call(kernel, out_shape=[jax.ShapeDtypeStruct((n_mp * rows, widt...  80.1 us
  transfers between devices with their start and end apart: 3, of which 0 were waited for; matrix products, arithmetic and copies ran while one was open for 1% of the time, Pallas kernels for 61%

profile of v5, /device:TPU:0, one launch (start us, length us, event | category | flops | bytes accessed | tf_op | source)
XLA Modules:
  0.0 646.5 jit_solution(9960673233050533541)
XLA Ops:
  7.2 0.0 all-gather.3.cloned.1.call-start
  7.2 1.2 copy.65
  8.4 1.7 copy.64
  10.1 0.3 copy.66
  10.4 1.1 pad_maximum_fusion
  11.5 0.0 all-gather.3.cloned.1.call-update
  11.5 0.0 all-gather.5.cloned.1.call-start
  11.6 6.6 %round_shares.1 = bf16[256,6144]{1,0:T(8,128)(2,1)} custom-call(f32[8192,128]{1,0:T(8,128)} %bitcast.49, f32[2048,256]{1,0:T(8,128)} %refs_4_.2), custom_call_target="tpu_custom_call" | custom-call | bytes 9437184 | tf_op jit(solution)/shard_map/round_shares/pallas_call | solution.py:213
  18.2 0.0 all-gather.5.cloned.1.call-update
  18.2 0.0 reduce-scatter.2.cloned.1.call-start
  18.9 0.1 tile.10
  19.0 0.6 concatenate.7.tile_ref
  19.6 0.7 fusion.live_ref
  20.3 80.1 %gather_first.1 = (bf16[1024,2048]{1,0:T(8,128)(2,1)}, f32[8,2048]{1,0:T(8,128)}, f32[256,2048]{1,0:T(8,128)}, bf16[256,2048]{1,0:T(8,128)(2,1)}) custom-call(bf16[256,2048]{1,0:T(8,128)(2,1)} %refs_5_.3, f32[8,128]{1,0:T(8,128)} %concatenate.7.tile_ref, bf16[256,2048]{1,0:T(8,128)(2,1)} %cotangent_ref.1, f32[256,1]{1,0:T(8,128)} %fusion.live_ref), custom_call_target="tpu_custom_call" | custom-call | bytes 209715200 | tf_op jit(solution)/shard_map/gather_first/pallas_call | solution.py:318
  100.4 0.6 compare_convert_fusion.refs_6_
  101.0 101.6 %scatter_forward.1 = (f32[256,2048]{1,0:T(8,128)}, bf16[256,2048]{1,0:T(8,128)(2,1)}, bf16[1024,512]{1,0:T(8,128)(2,1)}, bf16[1024,512]{1,0:T(8,128)(2,1)}, bf16...) custom-call(bf16[1024,2048]{1,0:T(8,128)(2,1)} %get-tuple-element.66.refs_0_.refs_8_, ...), custom_call_target="tpu_custom_call" | custom-call | flops 2147483648 | bytes 300000000 | tf_op jit(solution)/shard_map/scatter_forward/pallas_call | solution.py:882
  202.6 0.0 all-gather.5.cloned.1.call-done.weights_hbm.refs_1_
  202.6 126.2 %feed_forward.1 = (f32[256,2048]{1,0:T(8,128)}, bf16[256,2048]{1,0:T(8,128)(2,1)}, f32[8,2048]{1,0:T(8,128)}, bf16[2048,6144]{1,0:T(8,128)(2,1)}, bf16[1024,2048...) custom-call(bf16[256,2048]{1,0:T(8,128)(2,1)} %get-tuple-element.69.normed_ref, ...), custom_call_target="tpu_custom_call" | custom-call | flops 68719476736 | bytes 300000000 | tf_op jit(solution)/shard_map/feed_forward/pallas_call | solution.py:1262
  328.8 0.0 reduce-scatter.2.cloned.1.call-update
  328.9 98.7 %scatter_residual.1 = (bf16[256,2048]{1,0:T(8,128)(2,1)}, bf16[1024,2048]{1,0:T(8,128)(2,1)}, bf16[1024,512]{1,0:T(8,128)(2,1)}) custom-call(bf16[1024,2048]{1,0:T(8,128)(2,1)} %get-tuple-element.77.refs_0_, bf16[2048,6144]{1,0:T(8,128)(2,1)} %all-gather.5.cloned.1.call-done.weights_hbm.refs_1_, f32[8,2048]{1,0:T(8,128)} %get-tuple-element.67.refs_2_.gain_ref.refs_4_, ...), custom_call_target="tpu_custom_call" | custom-call | flops 8589934592 | bytes 300000000 | tf_op jit(solution)/shard_map/scatter_residual/pallas_call | solution.py:882
  427.6 12.7 %attention_backward.1 = (bf16[1024,512]{1,0:T(8,128)(2,1)}, bf16[1024,512]{1,0:T(8,128)(2,1)}, bf16[1024,512]{1,0:T(8,128)(2,1)}) custom-call(bf16[1024,512]{1,0:T(8,128)(2,1)} %get-tuple-element.74.q_ref, bf16[1024,512]{1,0:T(8,128)(2,1)} %get-tuple-element.75.k_ref, bf16[1024,512]{1,0:T(8,128)(2,1)} %get-tuple-element.76.v_ref, ...), custom_call_target="tpu_custom_call" | custom-call | flops 4294967296 | bytes 7340032 | tf_op jit(solution)/shard_map/attention_backward/pallas_call | solution.py:1336
  440.3 94.1 %scatter_last.1 = (f32[256,2048]{1,0:T(8,128)}, f32[2,128]{1,0:T(2,128)}, f32[256,2048]{1,0:T(8,128)}) custom-call(bf16[1024,512]{1,0:T(8,128)(2,1)} %get-tuple-element.80.refs_0_, bf16[1024,512]{1,0:T(8,128)(2,1)} %get-tuple-element.81.refs_1_, bf16[1024,512]{1,0:T(8,128)(2,1)} %get-tuple-element.82.refs_2_, ...), custom_call_target="tpu_custom_call" | custom-call | flops 6442450944 | bytes 300000000 | tf_op jit(solution)/shard_map/scatter_last/pallas_call | solution.py:882
  534.4 1.3 multiply_add_fusion
  535.7 103.9 %update_all.1 = (f32[8192,128]{1,0:T(8,128)}, f32[8192,128]{1,0:T(8,128)}, f32[8192,128]{1,0:T(8,128)}, bf16[8192,128]{1,0:T(8,128)(2,1)}, f32[2048,256]{1,0:T(8...) custom-call(f32[8192,128]{1,0:T(8,128)} %bitcast.50, ...), custom_call_target="tpu_custom_call" | custom-call | flops 20971520 | bytes 58720256 | tf_op jit(solution)/shard_map/update_all/pallas_call | solution.py:1463
  (11 shorter events, 0.0 us)
Async XLA Ops:
  7.2 93.8 %all-gather.3.cloned.1.call-start = ((), (), s32[]{:S(2)}) async-start(), calls=%async_computation.1 | async-start | bytes 9437184 | tf_op jit(solution)/shard_map/all_gather | solution.py:1528
  11.5 191.1 %all-gather.5.cloned.1.call-start = ((), (), s32[]{:S(2)}) async-start(), calls=%async_computation.2 | async-start | bytes 28311552 | tf_op jit(solution)/shard_map/all_gather | solution.py:1536
  18.2 0.7 copy-start
  18.2 517.5 %reduce-scatter.2.cloned.1.call-start = ((), (), s32[]{:S(2)}) async-start(), calls=%async_computation.3 | async-start | bytes 28311552 | tf_op jit(solution)/shard_map/reduce_scatter | solution.py:1556
  440.3 94.1 %copy-start.1 = (f32[2,64]{1,0:T(2,128)S(1)}, f32[2,64]{1,0:T(2,128)}, u32[]{:S(2)}) copy-start(f32[2,64]{1,0:T(2,128)} %param.37) | copy-start | bytes 1540
  440.3 94.1 %copy-start.2 = (f32[2,64]{1,0:T(2,128)S(1)}, f32[2,64]{1,0:T(2,128)}, u32[]{:S(2)}) copy-start(f32[2,64]{1,0:T(2,128)} %param.32) | copy-start | bytes 1540
Sparse Core Ops, SparseCore 0:
  11.6 58.4 all-gather.2
  72.6 125.3 all-gather.4
  329.0 196.6 reduce-scatter.1

commit v6 on v5

--- a/solution.py
+++ b/solution.py
@@ -1435,16 +1435,26 @@
 
     def body(*refs):
         ins, refs = refs[: len(in_specs)], refs[len(in_specs) :]
-        outs, (spread, sems) = refs[: len(out_specs)], refs[len(out_specs) :]
+        outs, (spread, sems, *kept) = refs[: len(out_specs)], refs[len(out_specs) :]
         i = pl.program_id(0)
-        copies = [
-            pltpu.make_async_copy(ins[4 * len(jobs) + k], outs[4 * len(jobs) + k], sems.at[k])
-            for k in range(len(passed))
+        entering = [
+            pltpu.make_async_copy(ins[4 * len(jobs) + k], ref, sems.at[0, k])
+            for k, ref in enumerate(kept)
+        ]
+        leaving = [
+            pltpu.make_async_copy(ref, outs[4 * len(jobs) + k], sems.at[1, k])
+            for k, ref in enumerate(kept)
         ]
 
         @pl.when(i == 0)
         def _():
-            for copy in copies:
+            for copy in entering:
+                copy.start()
+
+        @pl.when(i == 1)
+        def _():
+            for arrived, copy in zip(entering, leaving):
+                arrived.wait()
                 copy.start()
 
         for k, job in enumerate(jobs):
@@ -1456,7 +1466,7 @@
 
         @pl.when(i == steps - 1)
         def _():
-            for copy in copies:
+            for copy in leaving:
                 copy.wait()
 
     size = sum(job[0][0].size for job in jobs)
@@ -1468,8 +1478,9 @@
         out_specs=out_specs,
         scratch_shapes=[
             pltpu.VMEM((step * stride, 128), jnp.float32),
-            pltpu.SemaphoreType.DMA((len(passed),)),
-        ],
+            pltpu.SemaphoreType.DMA((2, len(passed))),
+        ]
+        + [pltpu.VMEM(x.shape, x.dtype) for x in passed],
         compiler_params=pltpu.CompilerParams(vmem_limit_bytes=VMEM_LIMIT),
         cost_estimate=pl.CostEstimate(
             flops=10 * size, bytes_accessed=28 * size, transcendentals=0

time: 653 us -> 577 us (0.88)
  Pallas kernels: 624 us -> 547 us
    pallas_call x1, Pallas kernels: 104 us -> 27.3 us  [update_all(): pl.pallas_call(body, grid=(steps,), out_shape=out_shape, in_specs=in_spec...]
  transfers between devices with their start and end apart: 3 -> 3, of which waited for: 0 -> 0; matrix products, arithmetic and copies ran while one was open for 1% -> 1% of each run, Pallas kernels for 61% -> 69%
where the time goes in v6:
time: 577 us; the launch traced here: 570 us
  Pallas kernels  547 us (95%)
  between operations  14.8 us (3%)
    pallas_call x3, Pallas kernels, scatter_rows(): pl.pallas_call(kernel, out_shape=out_shape, in_specs=[VMEM] * count + [AN...  294 us
    pallas_call x1, Pallas kernels, feed_forward(): pl.pallas_call(kernel, out_shape=[jax.ShapeDtypeStruct((rows, width), jnp...  126 us
    pallas_call x1, Pallas kernels, gather_first(): pl.pallas_call(kernel, out_shape=[jax.ShapeDtypeStruct((n_mp * rows, widt...  80.1 us
    pallas_call x1, Pallas kernels, update_all(): pl.pallas_call(body, grid=(steps,), out_shape=out_shape, in_specs=in_spec...  27.3 us
    pallas_call x1, Pallas kernels, attention_backward(): pl.pallas_call(kernel, grid=(inner_width // HDIM,), out_shape=[jax.ShapeD...  12.7 us
  transfers between devices with their start and end apart: 3, of which 0 were waited for; matrix products, arithmetic and copies ran while one was open for 1% of the time, Pallas kernels for 69%

profile of v6, /device:TPU:0, one launch (start us, length us, event | category | flops | bytes accessed | tf_op | source)
XLA Modules:
  0.0 569.8 jit_solution(16930385543888073924)
XLA Ops:
  7.2 0.0 all-gather.3.cloned.1.call-start
  7.2 1.2 copy.65
  8.4 1.7 copy.64
  10.1 0.3 copy.66
  10.4 1.1 pad_maximum_fusion
  11.5 0.0 all-gather.3.cloned.1.call-update
  11.5 0.0 all-gather.5.cloned.1.call-start
  11.6 6.6 %round_shares.1 = bf16[256,6144]{1,0:T(8,128)(2,1)} custom-call(f32[8192,128]{1,0:T(8,128)} %bitcast.49, f32[2048,256]{1,0:T(8,128)} %refs_4_.2), custom_call_target="tpu_custom_call" | custom-call | bytes 9437184 | tf_op jit(solution)/shard_map/round_shares/pallas_call | solution.py:213
  18.2 0.0 all-gather.5.cloned.1.call-update
  18.2 0.0 reduce-scatter.2.cloned.1.call-start
  18.9 0.1 tile.10
  19.0 0.6 concatenate.7.tile_ref
  19.6 0.7 fusion.live_ref
  20.3 80.1 %gather_first.1 = (bf16[1024,2048]{1,0:T(8,128)(2,1)}, f32[8,2048]{1,0:T(8,128)}, f32[256,2048]{1,0:T(8,128)}, bf16[256,2048]{1,0:T(8,128)(2,1)}) custom-call(bf16[256,2048]{1,0:T(8,128)(2,1)} %refs_5_.3, f32[8,128]{1,0:T(8,128)} %concatenate.7.tile_ref, bf16[256,2048]{1,0:T(8,128)(2,1)} %cotangent_ref.1, f32[256,1]{1,0:T(8,128)} %fusion.live_ref), custom_call_target="tpu_custom_call" | custom-call | bytes 209715200 | tf_op jit(solution)/shard_map/gather_first/pallas_call | solution.py:318
  100.4 0.6 compare_convert_fusion.refs_6_
  101.0 101.6 %scatter_forward.1 = (f32[256,2048]{1,0:T(8,128)}, bf16[256,2048]{1,0:T(8,128)(2,1)}, bf16[1024,512]{1,0:T(8,128)(2,1)}, bf16[1024,512]{1,0:T(8,128)(2,1)}, bf16...) custom-call(bf16[1024,2048]{1,0:T(8,128)(2,1)} %get-tuple-element.66.refs_0_.refs_8_, ...), custom_call_target="tpu_custom_call" | custom-call | flops 2147483648 | bytes 300000000 | tf_op jit(solution)/shard_map/scatter_forward/pallas_call | solution.py:882
  202.6 0.0 all-gather.5.cloned.1.call-done.weights_hbm.refs_1_
  202.6 126.2 %feed_forward.1 = (f32[256,2048]{1,0:T(8,128)}, bf16[256,2048]{1,0:T(8,128)(2,1)}, f32[8,2048]{1,0:T(8,128)}, bf16[2048,6144]{1,0:T(8,128)(2,1)}, bf16[1024,2048...) custom-call(bf16[256,2048]{1,0:T(8,128)(2,1)} %get-tuple-element.69.normed_ref, ...), custom_call_target="tpu_custom_call" | custom-call | flops 68719476736 | bytes 300000000 | tf_op jit(solution)/shard_map/feed_forward/pallas_call | solution.py:1262
  328.8 0.0 reduce-scatter.2.cloned.1.call-update
  328.9 98.7 %scatter_residual.1 = (bf16[256,2048]{1,0:T(8,128)(2,1)}, bf16[1024,2048]{1,0:T(8,128)(2,1)}, bf16[1024,512]{1,0:T(8,128)(2,1)}) custom-call(bf16[1024,2048]{1,0:T(8,128)(2,1)} %get-tuple-element.77.refs_0_, bf16[2048,6144]{1,0:T(8,128)(2,1)} %all-gather.5.cloned.1.call-done.weights_hbm.refs_1_, f32[8,2048]{1,0:T(8,128)} %get-tuple-element.67.refs_2_.gain_ref.refs_4_, ...), custom_call_target="tpu_custom_call" | custom-call | flops 8589934592 | bytes 300000000 | tf_op jit(solution)/shard_map/scatter_residual/pallas_call | solution.py:882
  427.6 12.7 %attention_backward.1 = (bf16[1024,512]{1,0:T(8,128)(2,1)}, bf16[1024,512]{1,0:T(8,128)(2,1)}, bf16[1024,512]{1,0:T(8,128)(2,1)}) custom-call(bf16[1024,512]{1,0:T(8,128)(2,1)} %get-tuple-element.74.q_ref, bf16[1024,512]{1,0:T(8,128)(2,1)} %get-tuple-element.75.k_ref, bf16[1024,512]{1,0:T(8,128)(2,1)} %get-tuple-element.76.v_ref, ...), custom_call_target="tpu_custom_call" | custom-call | flops 4294967296 | bytes 7340032 | tf_op jit(solution)/shard_map/attention_backward/pallas_call | solution.py:1336
  440.3 94.1 %scatter_last.1 = (f32[256,2048]{1,0:T(8,128)}, f32[2,128]{1,0:T(2,128)}, f32[256,2048]{1,0:T(8,128)}) custom-call(bf16[1024,512]{1,0:T(8,128)(2,1)} %get-tuple-element.80.refs_0_, bf16[1024,512]{1,0:T(8,128)(2,1)} %get-tuple-element.81.refs_1_, bf16[1024,512]{1,0:T(8,128)(2,1)} %get-tuple-element.82.refs_2_, ...), custom_call_target="tpu_custom_call" | custom-call | flops 6442450944 | bytes 300000000 | tf_op jit(solution)/shard_map/scatter_last/pallas_call | solution.py:882
  534.4 1.3 multiply_add_fusion
  535.7 27.3 %update_all.1 = (f32[8192,128]{1,0:T(8,128)}, f32[8192,128]{1,0:T(8,128)}, f32[8192,128]{1,0:T(8,128)}, bf16[8192,128]{1,0:T(8,128)(2,1)}, f32[2048,256]{1,0:T(8...) custom-call(f32[8192,128]{1,0:T(8,128)} %bitcast.50, ...), custom_call_target="tpu_custom_call" | custom-call | flops 20971520 | bytes 58720256 | tf_op jit(solution)/shard_map/update_all/pallas_call | solution.py:1473
  (11 shorter events, 0.0 us)
Async XLA Ops:
  7.2 93.8 %all-gather.3.cloned.1.call-start = ((), (), s32[]{:S(2)}) async-start(), calls=%async_computation.1 | async-start | bytes 9437184 | tf_op jit(solution)/shard_map/all_gather | solution.py:1539
  11.5 191.1 %all-gather.5.cloned.1.call-start = ((), (), s32[]{:S(2)}) async-start(), calls=%async_computation.2 | async-start | bytes 28311552 | tf_op jit(solution)/shard_map/all_gather | solution.py:1547
  18.2 0.7 copy-start
  18.2 517.5 %reduce-scatter.2.cloned.1.call-start = ((), (), s32[]{:S(2)}) async-start(), calls=%async_computation.3 | async-start | bytes 28311552 | tf_op jit(solution)/shard_map/reduce_scatter | solution.py:1567
  440.3 94.1 %copy-start.1 = (f32[2,64]{1,0:T(2,128)S(1)}, f32[2,64]{1,0:T(2,128)}, u32[]{:S(2)}) copy-start(f32[2,64]{1,0:T(2,128)} %param.37) | copy-start | bytes 1540
  440.3 94.1 %copy-start.2 = (f32[2,64]{1,0:T(2,128)S(1)}, f32[2,64]{1,0:T(2,128)}, u32[]{:S(2)}) copy-start(f32[2,64]{1,0:T(2,128)} %param.32) | copy-start | bytes 1540
Sparse Core Ops, SparseCore 0:
  11.6 58.4 all-gather.2
  72.6 125.3 all-gather.4
  329.0 196.6 reduce-scatter.1

commit v7 on v6

--- a/solution.py
+++ b/solution.py
@@ -246,13 +246,17 @@
         tile_ref,
         cotangent_ref,
         live_ref,
-        normed_ref,
+        normed_hbm,
         gain_ref,
-        base_ref,
-        branch_ref,
+        base_hbm,
+        branch_hbm,
         all_ref,
         first,
         second,
+        normed_ref,
+        base_ref,
+        branch_ref,
+        out_sems,
         *sems,
     ):
         me = lax.axis_index("mp")
@@ -278,6 +282,12 @@
             return carry
 
         lax.fori_loop(0, rows // block, enter, 0)
+        leaving = [
+            pltpu.make_async_copy(base_ref, base_hbm, out_sems.at[n_mp]),
+            pltpu.make_async_copy(branch_ref, branch_hbm, out_sems.at[n_mp + 1]),
+        ]
+        for copy in leaving:
+            copy.start()
         for copy in copies:
             copy.wait()
         gain_ref[...] = jnp.zeros_like(gain_ref)
@@ -285,6 +295,12 @@
             for m in range(n_mp):
                 cols = pl.ds(tile_of(d, m, n_mp, local) * 128, 128)
                 gain_ref[:, cols] += second[d, m]
+        def leave(block_id):
+            span = rows_at(block_id * rows, rows)
+            return pltpu.make_async_copy(
+                normed_ref.at[span], normed_hbm.at[span], out_sems.at[block_id]
+            )
+
         def norm(block_id):
             def body(i, carry):
                 span = rows_at(block_id * rows + i * block, block)
@@ -294,6 +310,7 @@
                 return carry
 
             lax.fori_loop(0, rows // block, body, 0)
+            leave(block_id).start()
 
         def step_of(step, carry):
             @pl.when(step > 0)
@@ -313,6 +330,10 @@
 
         lax.fori_loop(0, n_mp, step_of, 0)
         stream.finish(False)
+        for block_id in range(n_mp):
+            leave(block_id).wait()
+        for copy in leaving:
+            copy.wait()
 
     half = jnp.bfloat16
     return pl.pallas_call(
@@ -324,11 +345,15 @@
             jax.ShapeDtypeStruct((rows, width), half),
         ],
         in_specs=[VMEM] * 4,
-        out_specs=[VMEM] * 4,
+        out_specs=[ANY, VMEM, ANY, ANY],
         scratch_shapes=[
             pltpu.VMEM((n_mp * rows, width), half),
             pltpu.VMEM((n_mp, 8, 128), jnp.float32),
             pltpu.VMEM((n_dp, n_mp, 8, 128), jnp.float32),
+            pltpu.VMEM((n_mp * rows, width), half),
+            pltpu.VMEM((rows, width), jnp.float32),
+            pltpu.VMEM((rows, width), half),
+            pltpu.SemaphoreType.DMA((n_mp + 2,)),
         ]
         + exchange_sems(n_dp, n_mp)
         + gather_sems(n_mp, chunks),
@@ -410,12 +435,13 @@
         def take(k):
             return [refs.pop(0) for _ in range(k)]
 
-        left_refs = take(count)
+        left_hbm = take(count)
         (right_hbm,) = take(1)
         (gain_ref,) = take(1)
         own_hbm = take(len(own_rows))
         if heads is not None:
-            cosine_ref, sine_ref, mask_ref = take(3)
+            (mask_ref,) = take(1)
+            table_hbm = take(2)
         if other_gain is not None:
             (other_ref,) = take(1)
             grad_hbm = take(3)
@@ -425,7 +451,7 @@
         owned_ref = take(1)[0] if other_gain is not None else None
         normed = take(1)[0] if has_norm else None
         if heads is not None:
-            query_ref, key_ref, value_ref, mixed_ref = take(4)
+            head_hbm = take(4)
         extra_whole = take(1)[0] if extra is not None else None
         if extra_right is not None:
             (extra_out,) = take(1)
@@ -433,6 +459,29 @@
         joined_ref = take(1)[0] if heads is not None else None
         right_sem, send_sems, recv_sems = take(3)
         own, own_sems = take(len(own_rows)), take(1)[0]
+        left_refs, left_sems = take(count), take(1)[0]
+        left_loads = [
+            pltpu.make_async_copy(hbm, ref, left_sems.at[k])
+            for k, (hbm, ref) in enumerate(zip(left_hbm, left_refs))
+        ]
+        for load in left_loads:
+            load.start()
+        if heads is not None:
+            cosine_ref, sine_ref = take(2)
+            query_ref, key_ref, value_ref, mixed_ref = take(4)
+            table_sems, head_sems = take(2)
+            tables = [
+                pltpu.make_async_copy(hbm, ref, table_sems.at[k])
+                for k, (hbm, ref) in enumerate(zip(table_hbm, (cosine_ref, sine_ref)))
+            ]
+            for load in tables:
+                load.start()
+            heads_out = [
+                pltpu.make_async_copy(ref, hbm, head_sems.at[k])
+                for k, (ref, hbm) in enumerate(
+                    zip((query_ref, key_ref, value_ref, mixed_ref), head_hbm)
+                )
+            ]
         own_loads = [
             pltpu.make_async_copy(hbm, ref, own_sems.at[k])
             for k, (hbm, ref) in enumerate(zip(own_hbm, own))
@@ -570,6 +619,8 @@
         if heads is not None:
             turn = 256
             fetch_joined.wait()
+            for load in [*tables, *left_loads]:
+                load.wait()
 
             def enter(i, carry):
                 span = rows_at(i * turn, turn)
@@ -585,9 +636,14 @@
                 return carry
 
             lax.fori_loop(0, total_rows // turn, enter, 0)
+            for copy in heads_out[:3]:
+                copy.start()
         for load in own_loads:
             load.start()
         fetch.wait()
+        if heads is None:
+            for load in left_loads:
+                load.wait()
 
         def attend(block_id):
             span = rows_at(block_id * rows, rows)
@@ -705,6 +761,8 @@
 
         lax.fori_loop(1, n, step_of, 0)
         product(me)
+        if heads is not None:
+            heads_out[3].start()
         if extra_right is not None:
             extra_product(me)
         for load in own_loads:
@@ -806,6 +864,9 @@
             return carry
 
         lax.fori_loop(1, n, sends, 0)
+        if heads is not None:
+            for copy in heads_out:
+                copy.wait()
 
     out_type = jnp.bfloat16 if epilogue == "residual" else jnp.float32
     out_shape = [jax.ShapeDtypeStruct((rows, width), out_type)]
@@ -838,12 +899,18 @@
     ]
     scratch += [pltpu.VMEM(x.shape, x.dtype) for x in own_rows]
     scratch.append(pltpu.SemaphoreType.DMA((len(own_rows),)))
+    scratch += [pltpu.VMEM(x.shape, x.dtype) for x in lhs]
+    scratch.append(pltpu.SemaphoreType.DMA((count,)))
+    if heads is not None:
+        scratch += [pltpu.VMEM(x.shape, x.dtype) for x in heads[:2]]
+        scratch += [pltpu.VMEM((total_rows, inner_width), jnp.bfloat16)] * 4
+        scratch += [pltpu.SemaphoreType.DMA((2,)), pltpu.SemaphoreType.DMA((4,))]
     head_args = []
     if heads is not None:
         scratch.append(pltpu.SemaphoreType.DMA)
-        head_args = list(heads)
+        head_args = [heads[2]]
         out_shape += [jax.ShapeDtypeStruct((total_rows, inner_width), jnp.bfloat16)] * 4
-        out_specs += [VMEM] * 4
+        out_specs += [ANY] * 4
     extra_args = []
     if extra is not None:
         out_shape.append(jax.ShapeDtypeStruct((total_rows, width), jnp.bfloat16))
@@ -859,7 +926,7 @@
             pltpu.SemaphoreType.DMA,
         ]
         extra_args.append(extra_right[0])
-    late_args = []
+    late_args = list(heads[:2]) if heads is not None else []
     if other_gain is not None:
         head_args.append(other_gain)
         late_args = [*grad_lefts, grad_right]
@@ -882,8 +949,7 @@
     return pl.pallas_call(
         kernel,
         out_shape=out_shape,
-        in_specs=[VMEM] * count
-        + [ANY]
+        in_specs=[ANY] * (count + 1)
         + [VMEM]
         + [ANY] * len(own_rows)
         + [VMEM] * len(head_args)

time: 577 us -> 578 us (level)
  transfers between devices with their start and end apart: 3 -> 3, of which waited for: 0 -> 0; matrix products, arithmetic and copies ran while one was open for 1% -> 1% of each run, Pallas kernels for 69% -> 68%
where the time goes in v7:
time: 578 us; the launch traced here: 571 us
  Pallas kernels  549 us (95%)
  between operations  14.8 us (3%)
    pallas_call x3, Pallas kernels, scatter_rows(): pl.pallas_call(kernel, out_shape=out_shape, in_specs=[ANY] * (count + 1)...  292 us
    pallas_call x1, Pallas kernels, feed_forward(): pl.pallas_call(kernel, out_shape=[jax.ShapeDtypeStruct((rows, width), jnp...  132 us
    pallas_call x1, Pallas kernels, gather_first(): pl.pallas_call(kernel, out_shape=[jax.ShapeDtypeStruct((n_mp * rows, widt...  78.6 us
    pallas_call x1, Pallas kernels, update_all(): pl.pallas_call(body, grid=(steps,), out_shape=out_shape, in_specs=in_spec...  27.3 us
    pallas_call x1, Pallas kernels, attention_backward(): pl.pallas_call(kernel, grid=(inner_width // HDIM,), out_shape=[jax.ShapeD...  12.5 us
  transfers between devices with their start and end apart: 3, of which 0 were waited for; matrix products, arithmetic and copies ran while one was open for 1% of the time, Pallas kernels for 68%

profile of v7, /device:TPU:0, one launch (start us, length us, event | category | flops | bytes accessed | tf_op | source)
XLA Modules:
  0.0 571.4 jit_solution(6039576855956585694)
XLA Ops:
  7.2 0.0 all-gather.3.cloned.1.call-start
  7.2 1.2 copy.65
  8.4 1.7 copy.64
  10.1 0.3 copy.66
  10.4 1.1 pad_maximum_fusion
  11.5 0.0 all-gather.3.cloned.1.call-update
  11.5 0.0 all-gather.5.cloned.1.call-start
  11.6 6.6 %round_shares.1 = bf16[256,6144]{1,0:T(8,128)(2,1)} custom-call(f32[8192,128]{1,0:T(8,128)} %bitcast.49, f32[2048,256]{1,0:T(8,128)} %refs_4_.1), custom_call_target="tpu_custom_call" | custom-call | bytes 9437184 | tf_op jit(solution)/shard_map/round_shares/pallas_call | solution.py:213
  18.2 0.0 all-gather.5.cloned.1.call-update
  18.2 0.0 reduce-scatter.2.cloned.1.call-start
  18.9 0.1 tile.10
  19.0 0.6 concatenate.7.tile_ref
  19.6 0.7 fusion.live_ref
  20.3 78.6 %gather_first.1 = (bf16[1024,2048]{1,0:T(8,128)(2,1)}, f32[8,2048]{1,0:T(8,128)}, f32[256,2048]{1,0:T(8,128)}, bf16[256,2048]{1,0:T(8,128)(2,1)}) custom-call(bf16[256,2048]{1,0:T(8,128)(2,1)} %refs_5_.3, f32[8,128]{1,0:T(8,128)} %concatenate.7.tile_ref, bf16[256,2048]{1,0:T(8,128)(2,1)} %cotangent_ref.1, f32[256,1]{1,0:T(8,128)} %fusion.live_ref), custom_call_target="tpu_custom_call" | custom-call | bytes 209715200 | tf_op jit(solution)/shard_map/gather_first/pallas_call | solution.py:339
  98.9 0.6 compare_convert_fusion.refs_4_
  99.5 98.7 %scatter_forward.1 = (f32[256,2048]{1,0:T(8,128)}, bf16[256,2048]{1,0:T(8,128)(2,1)}, bf16[1024,512]{1,0:T(8,128)(2,1)}, bf16[1024,512]{1,0:T(8,128)(2,1)}, bf16...) custom-call(bf16[1024,2048]{1,0:T(8,128)(2,1)} %get-tuple-element.66.refs_0_.refs_8_, ...), custom_call_target="tpu_custom_call" | custom-call | flops 2147483648 | bytes 300000000 | tf_op jit(solution)/shard_map/scatter_forward/pallas_call | solution.py:949
  198.2 0.0 all-gather.5.cloned.1.call-done.weights_hbm.refs_1_
  198.2 131.9 %feed_forward.1 = (f32[256,2048]{1,0:T(8,128)}, bf16[256,2048]{1,0:T(8,128)(2,1)}, f32[8,2048]{1,0:T(8,128)}, bf16[2048,6144]{1,0:T(8,128)(2,1)}, bf16[1024,2048...) custom-call(bf16[256,2048]{1,0:T(8,128)(2,1)} %get-tuple-element.69.normed_ref, ...), custom_call_target="tpu_custom_call" | custom-call | flops 68719476736 | bytes 300000000 | tf_op jit(solution)/shard_map/feed_forward/pallas_call | solution.py:1328
  330.1 0.0 reduce-scatter.2.cloned.1.call-update
  330.2 99.4 %scatter_residual.1 = (bf16[256,2048]{1,0:T(8,128)(2,1)}, bf16[1024,2048]{1,0:T(8,128)(2,1)}, bf16[1024,512]{1,0:T(8,128)(2,1)}) custom-call(bf16[1024,2048]{1,0:T(8,128)(2,1)} %get-tuple-element.77.refs_0_, bf16[2048,6144]{1,0:T(8,128)(2,1)} %all-gather.5.cloned.1.call-done.weights_hbm.refs_1_, f32[8,2048]{1,0:T(8,128)} %get-tuple-element.67.refs_2_.gain_ref.refs_4_, ...), custom_call_target="tpu_custom_call" | custom-call | flops 8589934592 | bytes 300000000 | tf_op jit(solution)/shard_map/scatter_residual/pallas_call | solution.py:949
  429.6 12.5 %attention_backward.1 = (bf16[1024,512]{1,0:T(8,128)(2,1)}, bf16[1024,512]{1,0:T(8,128)(2,1)}, bf16[1024,512]{1,0:T(8,128)(2,1)}) custom-call(bf16[1024,512]{1,0:T(8,128)(2,1)} %get-tuple-element.74.q_ref, bf16[1024,512]{1,0:T(8,128)(2,1)} %get-tuple-element.75.k_ref, bf16[1024,512]{1,0:T(8,128)(2,1)} %get-tuple-element.76.v_ref, ...), custom_call_target="tpu_custom_call" | custom-call | flops 4294967296 | bytes 7340032 | tf_op jit(solution)/shard_map/attention_backward/pallas_call | solution.py:1402
  442.1 93.8 %scatter_last.1 = (f32[256,2048]{1,0:T(8,128)}, f32[2,128]{1,0:T(2,128)}, f32[256,2048]{1,0:T(8,128)}) custom-call(bf16[1024,512]{1,0:T(8,128)(2,1)} %get-tuple-element.80.refs_0_, bf16[1024,512]{1,0:T(8,128)(2,1)} %get-tuple-element.81.refs_1_, bf16[1024,512]{1,0:T(8,128)(2,1)} %get-tuple-element.82.refs_2_, ...), custom_call_target="tpu_custom_call" | custom-call | flops 6442450944 | bytes 300000000 | tf_op jit(solution)/shard_map/scatter_last/pallas_call | solution.py:949
  536.0 1.3 multiply_add_fusion
  537.3 27.3 %update_all.1 = (f32[8192,128]{1,0:T(8,128)}, f32[8192,128]{1,0:T(8,128)}, f32[8192,128]{1,0:T(8,128)}, bf16[8192,128]{1,0:T(8,128)(2,1)}, f32[2048,256]{1,0:T(8...) custom-call(f32[8192,128]{1,0:T(8,128)} %bitcast.50, ...), custom_call_target="tpu_custom_call" | custom-call | flops 20971520 | bytes 58720256 | tf_op jit(solution)/shard_map/update_all/pallas_call | solution.py:1539
  (11 shorter events, 0.0 us)
Async XLA Ops:
  7.2 92.3 %all-gather.3.cloned.1.call-start = ((), (), s32[]{:S(2)}) async-start(), calls=%async_computation.1 | async-start | bytes 9437184 | tf_op jit(solution)/shard_map/all_gather | solution.py:1605
  11.5 186.7 %all-gather.5.cloned.1.call-start = ((), (), s32[]{:S(2)}) async-start(), calls=%async_computation.2 | async-start | bytes 28311552 | tf_op jit(solution)/shard_map/all_gather | solution.py:1613
  18.2 0.7 copy-start
  18.2 519.1 %reduce-scatter.2.cloned.1.call-start = ((), (), s32[]{:S(2)}) async-start(), calls=%async_computation.3 | async-start | bytes 28311552 | tf_op jit(solution)/shard_map/reduce_scatter | solution.py:1633
  442.1 93.8 %copy-start.1 = (f32[2,64]{1,0:T(2,128)S(1)}, f32[2,64]{1,0:T(2,128)}, u32[]{:S(2)}) copy-start(f32[2,64]{1,0:T(2,128)} %param.37) | copy-start | bytes 1540
  442.1 93.8 %copy-start.2 = (f32[2,64]{1,0:T(2,128)S(1)}, f32[2,64]{1,0:T(2,128)}, u32[]{:S(2)}) copy-start(f32[2,64]{1,0:T(2,128)} %param.32) | copy-start | bytes 1540
Sparse Core Ops, SparseCore 0:
  11.6 58.4 all-gather.2
  72.6 125.3 all-gather.4
  330.3 195.8 reduce-scatter.1

commit v8 on v6

--- a/solution.py
+++ b/solution.py
@@ -246,13 +246,17 @@
         tile_ref,
         cotangent_ref,
         live_ref,
-        normed_ref,
+        normed_hbm,
         gain_ref,
-        base_ref,
-        branch_ref,
+        base_hbm,
+        branch_hbm,
         all_ref,
         first,
         second,
+        normed_ref,
+        base_ref,
+        branch_ref,
+        out_sems,
         *sems,
     ):
         me = lax.axis_index("mp")
@@ -278,6 +282,12 @@
             return carry
 
         lax.fori_loop(0, rows // block, enter, 0)
+        leaving = [
+            pltpu.make_async_copy(base_ref, base_hbm, out_sems.at[n_mp]),
+            pltpu.make_async_copy(branch_ref, branch_hbm, out_sems.at[n_mp + 1]),
+        ]
+        for copy in leaving:
+            copy.start()
         for copy in copies:
             copy.wait()
         gain_ref[...] = jnp.zeros_like(gain_ref)
@@ -285,6 +295,12 @@
             for m in range(n_mp):
                 cols = pl.ds(tile_of(d, m, n_mp, local) * 128, 128)
                 gain_ref[:, cols] += second[d, m]
+        def leave(block_id):
+            span = rows_at(block_id * rows, rows)
+            return pltpu.make_async_copy(
+                normed_ref.at[span], normed_hbm.at[span], out_sems.at[block_id]
+            )
+
         def norm(block_id):
             def body(i, carry):
                 span = rows_at(block_id * rows + i * block, block)
@@ -294,6 +310,7 @@
                 return carry
 
             lax.fori_loop(0, rows // block, body, 0)
+            leave(block_id).start()
 
         def step_of(step, carry):
             @pl.when(step > 0)
@@ -313,6 +330,10 @@
 
         lax.fori_loop(0, n_mp, step_of, 0)
         stream.finish(False)
+        for block_id in range(n_mp):
+            leave(block_id).wait()
+        for copy in leaving:
+            copy.wait()
 
     half = jnp.bfloat16
     return pl.pallas_call(
@@ -324,11 +345,15 @@
             jax.ShapeDtypeStruct((rows, width), half),
         ],
         in_specs=[VMEM] * 4,
-        out_specs=[VMEM] * 4,
+        out_specs=[ANY, VMEM, ANY, ANY],
         scratch_shapes=[
             pltpu.VMEM((n_mp * rows, width), half),
             pltpu.VMEM((n_mp, 8, 128), jnp.float32),
             pltpu.VMEM((n_dp, n_mp, 8, 128), jnp.float32),
+            pltpu.VMEM((n_mp * rows, width), half),
+            pltpu.VMEM((rows, width), jnp.float32),
+            pltpu.VMEM((rows, width), half),
+            pltpu.SemaphoreType.DMA((n_mp + 2,)),
         ]
         + exchange_sems(n_dp, n_mp)
         + gather_sems(n_mp, chunks),

time: 577 us -> 578 us (level)
  no operation moved by 1% of the time
where the time goes in v8:
time: 578 us; the launch traced here: 571 us
  Pallas kernels  549 us (95%)
  between operations  14.8 us (3%)
    pallas_call x3, Pallas kernels, scatter_rows(): pl.pallas_call(kernel, out_shape=out_shape, in_specs=[VMEM] * count + [AN...  296 us
    pallas_call x1, Pallas kernels, feed_forward(): pl.pallas_call(kernel, out_shape=[jax.ShapeDtypeStruct((rows, width), jnp...  128 us
    pallas_call x1, Pallas kernels, gather_first(): pl.pallas_call(kernel, out_shape=[jax.ShapeDtypeStruct((n_mp * rows, widt...  78.6 us
    pallas_call x1, Pallas kernels, update_all(): pl.pallas_call(body, grid=(steps,), out_shape=out_shape, in_specs=in_spec...  27.3 us
    pallas_call x1, Pallas kernels, attention_backward(): pl.pallas_call(kernel, grid=(inner_width // HDIM,), out_shape=[jax.ShapeD...  12.5 us
  transfers between devices with their start and end apart: 3, of which 0 were waited for; matrix products, arithmetic and copies ran while one was open for 1% of the time, Pallas kernels for 69%

profile of v8, /device:TPU:0, one launch (start us, length us, event | category | flops | bytes accessed | tf_op | source)
XLA Modules:
  0.0 571.4 jit_solution(16058916769103334028)
XLA Ops:
  7.2 0.0 all-gather.3.cloned.1.call-start
  7.2 1.2 copy.65
  8.4 1.7 copy.64
  10.1 0.3 copy.66
  10.4 1.1 pad_maximum_fusion
  11.5 0.0 all-gather.3.cloned.1.call-update
  11.5 0.0 all-gather.5.cloned.1.call-start
  11.6 6.6 %round_shares.1 = bf16[256,6144]{1,0:T(8,128)(2,1)} custom-call(f32[8192,128]{1,0:T(8,128)} %bitcast.49, f32[2048,256]{1,0:T(8,128)} %refs_4_.2), custom_call_target="tpu_custom_call" | custom-call | bytes 9437184 | tf_op jit(solution)/shard_map/round_shares/pallas_call | solution.py:213
  18.2 0.0 all-gather.5.cloned.1.call-update
  18.2 0.0 reduce-scatter.2.cloned.1.call-start
  18.9 0.1 tile.10
  19.0 0.6 concatenate.7.tile_ref
  19.6 0.7 fusion.live_ref
  20.3 78.6 %gather_first.1 = (bf16[1024,2048]{1,0:T(8,128)(2,1)}, f32[8,2048]{1,0:T(8,128)}, f32[256,2048]{1,0:T(8,128)}, bf16[256,2048]{1,0:T(8,128)(2,1)}) custom-call(bf16[256,2048]{1,0:T(8,128)(2,1)} %refs_5_.3, f32[8,128]{1,0:T(8,128)} %concatenate.7.tile_ref, bf16[256,2048]{1,0:T(8,128)(2,1)} %cotangent_ref.1, f32[256,1]{1,0:T(8,128)} %fusion.live_ref), custom_call_target="tpu_custom_call" | custom-call | bytes 209715200 | tf_op jit(solution)/shard_map/gather_first/pallas_call | solution.py:339
  98.9 0.6 compare_convert_fusion.refs_6_
  99.5 101.6 %scatter_forward.1 = (f32[256,2048]{1,0:T(8,128)}, bf16[256,2048]{1,0:T(8,128)(2,1)}, bf16[1024,512]{1,0:T(8,128)(2,1)}, bf16[1024,512]{1,0:T(8,128)(2,1)}, bf16...) custom-call(bf16[1024,2048]{1,0:T(8,128)(2,1)} %get-tuple-element.66.refs_0_.refs_8_, ...), custom_call_target="tpu_custom_call" | custom-call | flops 2147483648 | bytes 300000000 | tf_op jit(solution)/shard_map/scatter_forward/pallas_call | solution.py:907
  201.1 0.0 all-gather.5.cloned.1.call-done.weights_hbm.refs_1_
  201.1 127.7 %feed_forward.1 = (f32[256,2048]{1,0:T(8,128)}, bf16[256,2048]{1,0:T(8,128)(2,1)}, f32[8,2048]{1,0:T(8,128)}, bf16[2048,6144]{1,0:T(8,128)(2,1)}, bf16[1024,2048...) custom-call(bf16[256,2048]{1,0:T(8,128)(2,1)} %get-tuple-element.69.normed_ref, ...), custom_call_target="tpu_custom_call" | custom-call | flops 68719476736 | bytes 300000000 | tf_op jit(solution)/shard_map/feed_forward/pallas_call | solution.py:1287
  328.9 0.0 reduce-scatter.2.cloned.1.call-update
  328.9 98.4 %scatter_residual.1 = (bf16[256,2048]{1,0:T(8,128)(2,1)}, bf16[1024,2048]{1,0:T(8,128)(2,1)}, bf16[1024,512]{1,0:T(8,128)(2,1)}) custom-call(bf16[1024,2048]{1,0:T(8,128)(2,1)} %get-tuple-element.77.refs_0_, bf16[2048,6144]{1,0:T(8,128)(2,1)} %all-gather.5.cloned.1.call-done.weights_hbm.refs_1_, f32[8,2048]{1,0:T(8,128)} %get-tuple-element.67.refs_2_.gain_ref.refs_4_, ...), custom_call_target="tpu_custom_call" | custom-call | flops 8589934592 | bytes 300000000 | tf_op jit(solution)/shard_map/scatter_residual/pallas_call | solution.py:907
  427.3 12.5 %attention_backward.1 = (bf16[1024,512]{1,0:T(8,128)(2,1)}, bf16[1024,512]{1,0:T(8,128)(2,1)}, bf16[1024,512]{1,0:T(8,128)(2,1)}) custom-call(bf16[1024,512]{1,0:T(8,128)(2,1)} %get-tuple-element.74.q_ref, bf16[1024,512]{1,0:T(8,128)(2,1)} %get-tuple-element.75.k_ref, bf16[1024,512]{1,0:T(8,128)(2,1)} %get-tuple-element.76.v_ref, ...), custom_call_target="tpu_custom_call" | custom-call | flops 4294967296 | bytes 7340032 | tf_op jit(solution)/shard_map/attention_backward/pallas_call | solution.py:1361
  439.8 96.2 %scatter_last.1 = (f32[256,2048]{1,0:T(8,128)}, f32[2,128]{1,0:T(2,128)}, f32[256,2048]{1,0:T(8,128)}) custom-call(bf16[1024,512]{1,0:T(8,128)(2,1)} %get-tuple-element.80.refs_0_, bf16[1024,512]{1,0:T(8,128)(2,1)} %get-tuple-element.81.refs_1_, bf16[1024,512]{1,0:T(8,128)(2,1)} %get-tuple-element.82.refs_2_, ...), custom_call_target="tpu_custom_call" | custom-call | flops 6442450944 | bytes 300000000 | tf_op jit(solution)/shard_map/scatter_last/pallas_call | solution.py:907
  536.0 1.3 multiply_add_fusion
  537.3 27.3 %update_all.1 = (f32[8192,128]{1,0:T(8,128)}, f32[8192,128]{1,0:T(8,128)}, f32[8192,128]{1,0:T(8,128)}, bf16[8192,128]{1,0:T(8,128)(2,1)}, f32[2048,256]{1,0:T(8...) custom-call(f32[8192,128]{1,0:T(8,128)} %bitcast.50, ...), custom_call_target="tpu_custom_call" | custom-call | flops 20971520 | bytes 58720256 | tf_op jit(solution)/shard_map/update_all/pallas_call | solution.py:1498
  (11 shorter events, 0.0 us)
Async XLA Ops:
  7.2 92.3 %all-gather.3.cloned.1.call-start = ((), (), s32[]{:S(2)}) async-start(), calls=%async_computation.1 | async-start | bytes 9437184 | tf_op jit(solution)/shard_map/all_gather | solution.py:1564
  11.5 189.6 %all-gather.5.cloned.1.call-start = ((), (), s32[]{:S(2)}) async-start(), calls=%async_computation.2 | async-start | bytes 28311552 | tf_op jit(solution)/shard_map/all_gather | solution.py:1572
  18.2 0.7 copy-start
  18.2 519.1 %reduce-scatter.2.cloned.1.call-start = ((), (), s32[]{:S(2)}) async-start(), calls=%async_computation.3 | async-start | bytes 28311552 | tf_op jit(solution)/shard_map/reduce_scatter | solution.py:1592
  439.7 96.2 %copy-start.1 = (f32[2,64]{1,0:T(2,128)S(1)}, f32[2,64]{1,0:T(2,128)}, u32[]{:S(2)}) copy-start(f32[2,64]{1,0:T(2,128)} %param.37) | copy-start | bytes 1540
  439.7 96.2 %copy-start.2 = (f32[2,64]{1,0:T(2,128)S(1)}, f32[2,64]{1,0:T(2,128)}, u32[]{:S(2)}) copy-start(f32[2,64]{1,0:T(2,128)} %param.32) | copy-start | bytes 1540
Sparse Core Ops, SparseCore 0:
  11.6 58.4 all-gather.2
  72.6 125.3 all-gather.4
  329.0 198.9 reduce-scatter.1
